TPU v7x, 256 devices: a whole 4x4x8 slice. The times are simulated.
256 devices in a mesh: sec: 8 (over x, y_hi), strip: 32 (over z, y_lo, core).
Axes of the slice: x: 4, y: 4 (y_hi: 2, y_lo: 2; y = y_hi * 2 + y_lo), z: 8, core: 2. Of those that a mesh axis runs over, the one named last changes fastest.
Arguments:
- features: bfloat16 [8, 384, 128, 128], P('sec', 'strip'), may hold values from -6 to 6
- offsets: int32 [8], replicated, may hold values from -2 to 2
- state: float32 [2, 8, 384, 128], P(None, 'sec', 'strip'), may hold values from -6 to 6
- w_first: bfloat16 [3, 3, 162, 128], replicated, may hold values from -0.15625 to 0.15625
- b_first: float32 [128], replicated, may hold values from -3 to 3
- w_second: bfloat16 [3, 3, 128, 128], replicated, may hold values from -0.1875 to 0.1875
- b_second: float32 [128], replicated, may hold values from -3 to 3
- w_third: bfloat16 [3, 3, 128, 2], replicated, may hold values from -0.1875 to 0.1875
Outputs:
- updated: float32 [2, 8, 384, 128], P(None, 'sec', 'strip')
Inputs may be any that keep to these rules, and one draw needn't show every extreme that they name: offsets[s] is the integer row offset of section s+1 against section s; the last entry is not used.
All inputs are finite; a program needn't handle non-finite values.
Results may differ from a plain program's by a relative error of at most 0.0029.
Values may be sent and summed in bfloat16 or wider, within the bound.
No kernel may reach another device: no remote copies, remote signals or barrier semaphores. Data moves between devices by JAX's collectives and lax.ppermute only.
A program may use at most 64 MiB of HBM per device.

v0:
```python
import jax
import jax.numpy as jnp
from jax import lax
from jax.sharding import PartitionSpec as P

C = 128


def extended(cells, sides, width):
    for axis, dim in sides:
        count = lax.axis_size(axis)
        ends = count - 1
        head = lax.slice_in_dim(cells, 0, width, axis=dim)
        tail = lax.slice_in_dim(cells, cells.shape[dim] - width, cells.shape[dim], axis=dim)
        cells = jnp.concatenate(
            [
                lax.ppermute(tail, axis, [(i, (i + 1) % count) for i in range(ends)]),
                cells,
                lax.ppermute(head, axis, [((i + 1) % count, i) for i in range(ends)]),
            ],
            axis=dim,
        )
    return cells


def passed_along(x, axis, by):
    length = lax.axis_size(axis)
    pairs = [(i, i + by) for i in range(length) if 0 <= i + by < length]
    return lax.ppermute(x, axis, pairs)


def band_corr(mine, other, shift, extra):
    rows, cols, chans = mine.shape
    padded = jnp.pad(other, ((0, 0), (4, 4), (0, 0)))
    reach = jnp.arange(cols + 8)[:, None] - jnp.arange(cols)[None, :]
    select = (reach[None] == jnp.arange(9)[:, None, None]).astype(jnp.float32)
    planes = []
    for row_step in range(-4, 5):
        start = extra + row_step + shift
        taken = lax.dynamic_slice_in_dim(padded, start, rows, 0)
        products = jnp.einsum("rjc,ric->rji", taken, mine, preferred_element_type=jnp.float32)
        band = jnp.sum(products[None] * select[:, None], axis=2)
        planes.append(band)
    return jnp.concatenate(planes, 0)


def convolve(values, kernel, layout, rows_pad):
    return lax.conv_general_dilated(
        values[None],
        kernel,
        (1, 1),
        ((rows_pad, rows_pad), (1, 1)),
        dimension_numbers=(layout, "HWIO", "NHWC"),
        preferred_element_type=jnp.float32,
    )[0]


def hidden_edge(values):
    return extended(values, (("strip", 0),), 1)


def body(features, offsets, state, w_first, b_first, w_second, b_second, w_third):
    mine = features[0]
    sec_index = lax.axis_index("sec")
    above = passed_along(features, "sec", -1)[0]
    below = passed_along(features, "sec", 1)[0]
    shift_above = offsets[sec_index]
    shift_below = jnp.where(sec_index > 0, -offsets[jnp.maximum(sec_index - 1, 0)], 0)
    neighbours = jnp.stack([below, above])
    scale = C ** (-0.5)
    wide = extended(neighbours, (("strip", 1),), 6)
    corr = jnp.concatenate(
        [band_corr(mine, wide[0], shift_below, 6), band_corr(mine, wide[1], shift_above, 6)], 0
    )
    corr = (corr * scale).astype(jnp.bfloat16)
    corr_wide = extended(corr, (("strip", 1),), 1)
    hidden_one = jax.nn.relu(convolve(corr_wide, w_first, "NCHW", 0) + b_first).astype(jnp.bfloat16)
    hidden_two = jax.nn.relu(
        convolve(hidden_edge(hidden_one), w_second, "NHWC", 0) + b_second
    ).astype(jnp.bfloat16)
    delta = convolve(hidden_edge(hidden_two), w_third, "NHWC", 0)
    return state + jnp.moveaxis(delta, 2, 0)[:, None]


def solution(mesh):
    in_specs = (
        P("sec", "strip", None, None),
        P(),
        P(None, "sec", "strip", None),
        P(),
        P(),
        P(),
        P(),
        P(),
    )
    out_specs = P(None, "sec", "strip", None)
    return jax.shard_map(body, mesh=mesh, in_specs=in_specs, out_specs=out_specs, check_vma=False)
```

profile of v0, /device:TPU:111, one launch (start us, length us, event | category | flops | bytes accessed | tf_op | source)
XLA Modules:
  0.0 129.8 jit_solution(17063921399856422497)
XLA Ops:
  0.0 4.0 %collective-permute-start = (bf16[1,12,128,128]{3,2,1,0:T(8,128)(2,1)}, bf16[1,12,128,128]{3,2,1,0:T(8,128)(2,1)S(1)}, u32[]{:S(2)}, u32[]{:S(2)}) collective-permute-start(bf16[1,12,128,128]{3,2,1,0:T(8,128)(2,1)} %param.8), channel_id=1, source_target_pairs={{0,32},{32,64},{64,96},{96,128},{128,160},{160,192},{192,224},{1,3... | collective-permute-start | bytes 1179656 | tf_op jit(solution)/shard_map/ppermute | solution.py:29
  4.1 3.8 %collective-permute-start.1 = (bf16[1,12,128,128]{3,2,1,0:T(8,128)(2,1)}, bf16[1,12,128,128]{3,2,1,0:T(8,128)(2,1)S(1)}, u32[]{:S(2)}, u32[]{:S(2)}) collective-permute-start(bf16[1,12,128,128]{3,2,1,0:T(8,128)(2,1)} %param.8), channel_id=1, source_target_pairs={{32,0},{64,32},{96,64},{128,96},{160,128},{192,160},{224,192},{33,... | collective-permute-start | bytes 1179656 | tf_op jit(solution)/shard_map/ppermute | solution.py:29
  7.8 6.8 %collective-permute-done = bf16[1,12,128,128]{3,2,1,0:T(8,128)(2,1)S(1)} collective-permute-done((bf16[1,12,128,128]{3,2,1,0:T(8,128)(2,1)}, bf16[1,12,128,128]{3,2,1,0:T(8,128)(2,1)S(1)}, u32[]{:S(2)}, u32[]{:S(2)}) %collective-permute-start) | collective-permute-done | bytes 393248 | tf_op jit(solution)/shard_map/ppermute | solution.py:29
  14.7 9.4 %collective-permute-done.1 = bf16[1,12,128,128]{3,2,1,0:T(8,128)(2,1)S(1)} collective-permute-done((bf16[1,12,128,128]{3,2,1,0:T(8,128)(2,1)}, bf16[1,12,128,128]{3,2,1,0:T(8,128)(2,1)S(1)}, u32[]{:S(2)}, u32[]{:S(2)}) %collective-permute-start.1) | collective-permute-done | bytes 393248 | tf_op jit(solution)/shard_map/ppermute | solution.py:29
  24.2 5.0 %collective-permute-start.2 = (bf16[2,6,128,128]{3,2,1,0:T(8,128)(2,1)S(1)}, bf16[2,6,128,128]{3,2,1,0:T(8,128)(2,1)S(1)}, u32[]{:S(2)}, u32[]{:S(2)}) collective-permute-start(bf16[2,6,128,128]{3,2,1,0:T(8,128)(2,1)S(1)} %get-tuple-element.25), channel_id=1, source_target_pairs={{0,1},{1,2},{2,3},{3,4},{4,5},{5,6},{6,7},{7,8},{8,9},{9,10},{10,1... | collective-permute-start | bytes 1179656 | tf_op jit(solution)/shard_map/ppermute | solution.py:17
  29.3 1.9 %collective-permute-start.3 = (bf16[2,6,128,128]{3,2,1,0:T(8,128)(2,1)S(1)}, bf16[2,6,128,128]{3,2,1,0:T(8,128)(2,1)S(1)}, u32[]{:S(2)}, u32[]{:S(2)}) collective-permute-start(bf16[2,6,128,128]{3,2,1,0:T(8,128)(2,1)S(1)} %get-tuple-element.26), channel_id=1, source_target_pairs={{1,0},{2,1},{3,2},{4,3},{5,4},{6,5},{7,6},{8,7},{9,8},{10,9},{11,1... | collective-permute-start | bytes 1179656 | tf_op jit(solution)/shard_map/ppermute | solution.py:19
  31.2 0.7 fusion.153
  45.5 0.9 copy-done.1
  53.3 22.1 %multiply_reduce_fusion = (f32[9,12,128]{2,1,0:T(8,128)S(1)}, f32[9,12,128]{2,1,0:T(8,128)S(1)}, f32[9,12,128]{2,1,0:T(8,128)S(1)}, f32[9,12,128]{2,1,0:T(8,128)...) fusion(f32[12,136,128]{2,1,0:T(8,128)S(1)} %fusion.29, ...), kind=kLoop, calls=%fused_computation | loop fusion | flops 67433472 | bytes 16662528 | tf_op jit(solution)/shard_map/reduce_sum | solution.py:42
  76.0 2.3 %concatenate.16 = f32[162,12,128]{2,0,1:T(8,128)S(1)} concatenate(f32[9,12,128]{2,0,1:T(8,128)S(1)} %copy.36, f32[9,12,128]{2,0,1:T(8,128)S(1)} %copy.37, f32[9,12,128]{2,0,1:T(8,128)S(1)} %copy.38, f32[9,12,128]{2,0,1:T(8,128)S(1)} %copy.39, f32[9,12,128]{2,0,1:T(8,128)S(1)} %copy.40, f32[9,12,128]{2,0,1:T(8,128)S(1)} %copy.41, f32[9,12,128]{2,0,1:T(8,128)S(1)} %copy.42, ...), dimensions={0} | concatenate | bytes 1990656 | tf_op jit(solution)/shard_map/concatenate | solution.py:72
  78.5 5.8 %collective-permute-start.4 = (bf16[162,1,128]{2,0,1:T(8,128)(2,1)S(1)}, bf16[162,1,128]{2,0,1:T(8,128)(2,1)S(1)}, u32[]{:S(2)}, u32[]{:S(2)}) collective-permute-start(bf16[162,1,128]{2,0,1:T(8,128)(2,1)S(1)} %get-tuple-element.27), channel_id=1, source_target_pairs={{0,1},{1,2},{2,3},{3,4},{4,5},{5,6},{6,7},{7,8},{8,9},{9,10},{10,1... | collective-permute-start | bytes 124424 | tf_op jit(solution)/shard_map/ppermute | solution.py:17
  84.2 1.9 %collective-permute-start.5 = (bf16[162,1,128]{2,0,1:T(8,128)(2,1)S(1)}, bf16[162,1,128]{2,0,1:T(8,128)(2,1)S(1)}, u32[]{:S(2)}, u32[]{:S(2)}) collective-permute-start(bf16[162,1,128]{2,0,1:T(8,128)(2,1)S(1)} %get-tuple-element.28), channel_id=1, source_target_pairs={{1,0},{2,1},{3,2},{4,3},{5,4},{6,5},{7,6},{8,7},{9,8},{10,9},{11,1... | collective-permute-start | bytes 124424 | tf_op jit(solution)/shard_map/ppermute | solution.py:19
  86.1 5.5 %collective-permute-done.5 = bf16[162,1,128]{2,0,1:T(8,128)(2,1)S(1)} collective-permute-done((bf16[162,1,128]{2,0,1:T(8,128)(2,1)S(1)}, bf16[162,1,128]{2,0,1:T(8,128)(2,1)S(1)}, u32[]{:S(2)}, u32[]{:S(2)}) %collective-permute-start.5) | collective-permute-done | bytes 41504 | tf_op jit(solution)/shard_map/ppermute | solution.py:19
  91.7 1.5 %copy.68 = bf16[162,14,1,128]{0,1,3,2:T(8,128)(2,1)S(1)} copy(bf16[162,14,1,128]{3,0,1,2:T(8,128)(2,1)S(1)} %maximum_bitcast_fusion) | data formatting | bytes 1161216
  94.2 2.3 %convolution_select_fusion.1 = f32[12,8,17,128]{3,1,2,0:T(8,128)S(1)} fusion(bf16[3,3,162,128]{3,2,1,0:T(8,128)(2,1)S(1)} %copy-done, bf16[162,14,1,7,2]{0,3,4,1,2:T(8,128)(2,1)S(1)} %slice.52, bf16[162,14,1,8,17]{0,3,4,1,2:T(8,128)(2,1)S(1)} %copy.56, pred[8,17]{0,1:T(8,128)(4,1)S(1)} %copy-done.8), kind=kOutput, calls=%fused_computation.22 | convolution fusion | flops 611418048 | bytes 1889368 | tf_op jit(solution)/shard_map/conv_general_dilated | solution.py:48
  97.3 1.9 %collective-permute-start.6 = (bf16[1,128,128]{2,1,0:T(8,128)(2,1)S(1)}, bf16[1,128,128]{2,1,0:T(8,128)(2,1)S(1)}, u32[]{:S(2)}, u32[]{:S(2)}) collective-permute-start(bf16[1,128,128]{2,1,0:T(8,128)(2,1)S(1)} %get-tuple-element.31), channel_id=1, source_target_pairs={{0,1},{1,2},{2,3},{3,4},{4,5},{5,6},{6,7},{7,8},{8,9},{9,10},{10,1... | collective-permute-start | bytes 98312 | tf_op jit(solution)/shard_map/ppermute | solution.py:17
  99.2 2.6 %collective-permute-start.7 = (bf16[1,128,128]{2,1,0:T(8,128)(2,1)S(1)}, bf16[1,128,128]{2,1,0:T(8,128)(2,1)S(1)}, u32[]{:S(2)}, u32[]{:S(2)}) collective-permute-start(bf16[1,128,128]{2,1,0:T(8,128)(2,1)S(1)} %get-tuple-element.32), channel_id=1, source_target_pairs={{1,0},{2,1},{3,2},{4,3},{5,4},{6,5},{7,6},{8,7},{9,8},{10,9},{11,1... | collective-permute-start | bytes 98312 | tf_op jit(solution)/shard_map/ppermute | solution.py:19
  101.8 4.7 %collective-permute-done.7 = bf16[1,128,128]{2,1,0:T(8,128)(2,1)S(1)} collective-permute-done((bf16[1,128,128]{2,1,0:T(8,128)(2,1)S(1)}, bf16[1,128,128]{2,1,0:T(8,128)(2,1)S(1)}, u32[]{:S(2)}, u32[]{:S(2)}) %collective-permute-start.7) | collective-permute-done | bytes 32800 | tf_op jit(solution)/shard_map/ppermute | solution.py:19
  107.6 1.1 convolution_select_fusion
  109.5 1.9 %collective-permute-start.8 = (bf16[1,128,128]{2,1,0:T(8,128)(2,1)S(1)}, bf16[1,128,128]{2,1,0:T(8,128)(2,1)S(1)}, u32[]{:S(2)}, u32[]{:S(2)}) collective-permute-start(bf16[1,128,128]{2,1,0:T(8,128)(2,1)S(1)} %get-tuple-element.29), channel_id=1, source_target_pairs={{0,1},{1,2},{2,3},{3,4},{4,5},{5,6},{6,7},{7,8},{8,9},{9,10},{10,1... | collective-permute-start | bytes 98312 | tf_op jit(solution)/shard_map/ppermute | solution.py:17
  111.4 2.4 %collective-permute-start.9 = (bf16[1,128,128]{2,1,0:T(8,128)(2,1)S(1)}, bf16[1,128,128]{2,1,0:T(8,128)(2,1)S(1)}, u32[]{:S(2)}, u32[]{:S(2)}) collective-permute-start(bf16[1,128,128]{2,1,0:T(8,128)(2,1)S(1)} %get-tuple-element.30), channel_id=1, source_target_pairs={{1,0},{2,1},{3,2},{4,3},{5,4},{6,5},{7,6},{8,7},{9,8},{10,9},{11,1... | collective-permute-start | bytes 98312 | tf_op jit(solution)/shard_map/ppermute | solution.py:19
  113.8 4.9 %collective-permute-done.9 = bf16[1,128,128]{2,1,0:T(8,128)(2,1)S(1)} collective-permute-done((bf16[1,128,128]{2,1,0:T(8,128)(2,1)S(1)}, bf16[1,128,128]{2,1,0:T(8,128)(2,1)S(1)}, u32[]{:S(2)}, u32[]{:S(2)}) %collective-permute-start.9) | collective-permute-done | bytes 32800 | tf_op jit(solution)/shard_map/ppermute | solution.py:19
  119.5 9.2 %convolution_select_fusion.2 = f32[12,8,17,2]{1,3,2,0:T(2,128)S(1)} fusion(bf16[3,3,128,2]{2,3,1,0:T(2,128)(2,1)S(1)} %copy-done.7, bf16[14,1,7,2,128]{4,2,3,0,1:T(8,128)(2,1)S(1)} %slice.60, bf16[14,1,8,17,128]{4,2,3,0,1:T(8,128)(2,1)S(1)} %copy.64, pred[8,17]{0,1:T(8,128)(4,1)S(1)} %copy-done.8), kind=kOutput, calls=%fused_computation.23 | convolution fusion | flops 9157824 | bytes 555400 | tf_op jit(solution)/shard_map/conv_general_dilated | solution.py:48
  129.2 0.6 copy.67
  (92 shorter events, 12.4 us)
Async XLA Ops:
  0.0 93.8 %copy-start = (bf16[3,3,162,128]{3,2,1,0:T(8,128)(2,1)S(1)}, bf16[3,3,162,128]{3,2,1,0:T(8,128)(2,1)}, u32[]{:S(2)}) copy-start(bf16[3,3,162,128]{3,2,1,0:T(8,128)(2,1)} %param.11) | copy-start | bytes 1119748
  0.0 31.2 %copy-start.3 = (s32[8]{0:T(128)S(1)}, s32[8]{0:T(128)}, u32[]{:S(2)}) copy-start(s32[8]{0:T(128)} %param.9) | copy-start | bytes 100
  0.0 14.7 %collective-permute-start = (bf16[1,12,128,128]{3,2,1,0:T(8,128)(2,1)}, bf16[1,12,128,128]{3,2,1,0:T(8,128)(2,1)S(1)}, u32[]{:S(2)}, u32[]{:S(2)}) collective-permute-start(bf16[1,12,128,128]{3,2,1,0:T(8,128)(2,1)} %param.8), channel_id=1, source_target_pairs={{0,32},{32,64},{64,96},{96,128},{128,160},{160,192},{192,224},{1,3... | collective-permute-start | bytes 1179656 | tf_op jit(solution)/shard_map/ppermute | solution.py:29
  4.1 20.0 %collective-permute-start.1 = (bf16[1,12,128,128]{3,2,1,0:T(8,128)(2,1)}, bf16[1,12,128,128]{3,2,1,0:T(8,128)(2,1)S(1)}, u32[]{:S(2)}, u32[]{:S(2)}) collective-permute-start(bf16[1,12,128,128]{3,2,1,0:T(8,128)(2,1)} %param.8), channel_id=1, source_target_pairs={{32,0},{64,32},{96,64},{128,96},{160,128},{192,160},{224,192},{33,... | collective-permute-start | bytes 1179656 | tf_op jit(solution)/shard_map/ppermute | solution.py:29
  24.2 20.9 %collective-permute-start.2 = (bf16[2,6,128,128]{3,2,1,0:T(8,128)(2,1)S(1)}, bf16[2,6,128,128]{3,2,1,0:T(8,128)(2,1)S(1)}, u32[]{:S(2)}, u32[]{:S(2)}) collective-permute-start(bf16[2,6,128,128]{3,2,1,0:T(8,128)(2,1)S(1)} %get-tuple-element.25), channel_id=1, source_target_pairs={{0,1},{1,2},{2,3},{3,4},{4,5},{5,6},{6,7},{7,8},{8,9},{9,10},{10,1... | collective-permute-start | bytes 1179656 | tf_op jit(solution)/shard_map/ppermute | solution.py:17
  29.3 15.9 %collective-permute-start.3 = (bf16[2,6,128,128]{3,2,1,0:T(8,128)(2,1)S(1)}, bf16[2,6,128,128]{3,2,1,0:T(8,128)(2,1)S(1)}, u32[]{:S(2)}, u32[]{:S(2)}) collective-permute-start(bf16[2,6,128,128]{3,2,1,0:T(8,128)(2,1)S(1)} %get-tuple-element.26), channel_id=1, source_target_pairs={{1,0},{2,1},{3,2},{4,3},{5,4},{6,5},{7,6},{8,7},{9,8},{10,9},{11,1... | collective-permute-start | bytes 1179656 | tf_op jit(solution)/shard_map/ppermute | solution.py:19
  45.3 1.0 copy-start.1
  78.5 7.7 %collective-permute-start.4 = (bf16[162,1,128]{2,0,1:T(8,128)(2,1)S(1)}, bf16[162,1,128]{2,0,1:T(8,128)(2,1)S(1)}, u32[]{:S(2)}, u32[]{:S(2)}) collective-permute-start(bf16[162,1,128]{2,0,1:T(8,128)(2,1)S(1)} %get-tuple-element.27), channel_id=1, source_target_pairs={{0,1},{1,2},{2,3},{3,4},{4,5},{5,6},{6,7},{7,8},{8,9},{9,10},{10,1... | collective-permute-start | bytes 124424 | tf_op jit(solution)/shard_map/ppermute | solution.py:17
  84.2 7.5 %collective-permute-start.5 = (bf16[162,1,128]{2,0,1:T(8,128)(2,1)S(1)}, bf16[162,1,128]{2,0,1:T(8,128)(2,1)S(1)}, u32[]{:S(2)}, u32[]{:S(2)}) collective-permute-start(bf16[162,1,128]{2,0,1:T(8,128)(2,1)S(1)} %get-tuple-element.28), channel_id=1, source_target_pairs={{1,0},{2,1},{3,2},{4,3},{5,4},{6,5},{7,6},{8,7},{9,8},{10,9},{11,1... | collective-permute-start | bytes 124424 | tf_op jit(solution)/shard_map/ppermute | solution.py:19
  93.5 0.7 copy-start.8
  96.5 0.7 copy-start.4
  97.3 4.6 %collective-permute-start.6 = (bf16[1,128,128]{2,1,0:T(8,128)(2,1)S(1)}, bf16[1,128,128]{2,1,0:T(8,128)(2,1)S(1)}, u32[]{:S(2)}, u32[]{:S(2)}) collective-permute-start(bf16[1,128,128]{2,1,0:T(8,128)(2,1)S(1)} %get-tuple-element.31), channel_id=1, source_target_pairs={{0,1},{1,2},{2,3},{3,4},{4,5},{5,6},{6,7},{7,8},{8,9},{9,10},{10,1... | collective-permute-start | bytes 98312 | tf_op jit(solution)/shard_map/ppermute | solution.py:17
  99.2 7.3 %collective-permute-start.7 = (bf16[1,128,128]{2,1,0:T(8,128)(2,1)S(1)}, bf16[1,128,128]{2,1,0:T(8,128)(2,1)S(1)}, u32[]{:S(2)}, u32[]{:S(2)}) collective-permute-start(bf16[1,128,128]{2,1,0:T(8,128)(2,1)S(1)} %get-tuple-element.32), channel_id=1, source_target_pairs={{1,0},{2,1},{3,2},{4,3},{5,4},{6,5},{7,6},{8,7},{9,8},{10,9},{11,1... | collective-permute-start | bytes 98312 | tf_op jit(solution)/shard_map/ppermute | solution.py:19
  106.6 1.0 copy-start.6
  108.7 0.7 copy-start.5
  109.5 4.3 %collective-permute-start.8 = (bf16[1,128,128]{2,1,0:T(8,128)(2,1)S(1)}, bf16[1,128,128]{2,1,0:T(8,128)(2,1)S(1)}, u32[]{:S(2)}, u32[]{:S(2)}) collective-permute-start(bf16[1,128,128]{2,1,0:T(8,128)(2,1)S(1)} %get-tuple-element.29), channel_id=1, source_target_pairs={{0,1},{1,2},{2,3},{3,4},{4,5},{5,6},{6,7},{7,8},{8,9},{9,10},{10,1... | collective-permute-start | bytes 98312 | tf_op jit(solution)/shard_map/ppermute | solution.py:17
  111.4 7.3 %collective-permute-start.9 = (bf16[1,128,128]{2,1,0:T(8,128)(2,1)S(1)}, bf16[1,128,128]{2,1,0:T(8,128)(2,1)S(1)}, u32[]{:S(2)}, u32[]{:S(2)}) collective-permute-start(bf16[1,128,128]{2,1,0:T(8,128)(2,1)S(1)} %get-tuple-element.30), channel_id=1, source_target_pairs={{1,0},{2,1},{3,2},{4,3},{5,4},{6,5},{7,6},{8,7},{9,8},{10,9},{11,1... | collective-permute-start | bytes 98312 | tf_op jit(solution)/shard_map/ppermute | solution.py:19
  118.8 0.7 copy-start.7
  119.5 9.6 %copy-start.2 = (f32[2,1,12,128]{3,1,2,0:T(1,128)S(1)}, f32[2,1,12,128]{3,1,2,0:T(1,128)}, u32[]{:S(2)}) copy-start(f32[2,1,12,128]{3,1,2,0:T(1,128)} %param.10) | copy-start | bytes 36868
where the time goes:
time: 130 us
  waiting for transfers between devices  31.4 us (24%)
  starting transfers between devices  31.3 us (24%)
  other arithmetic  22.9 us (18%)
  matrix products  19.6 us (15%)
  between operations  13.8 us (11%)
  local copies, waits for them, and re-layouts  10.7 us (8%)
    reduce_sum x1, other arithmetic, band_corr(): band = jnp.sum(products[None] * select[:, None], axis=2)  22.1 us
    ppermute x2, waiting for transfers between devices, passed_along(): return lax.ppermute(x, axis, pairs)  16.2 us
    ppermute x4, waiting for transfers between devices, extended(): lax.ppermute(head, axis, [((i + 1) % count, i) for i in range(ends)])  15.1 us
    ppermute x4, starting transfers between devices, extended(): lax.ppermute(tail, axis, [(i, (i + 1) % count) for i in range(ends)])  14.6 us
    conv_general_dilated x3, matrix products, convolve(): lax.conv_general_dilated(values[None], kernel, (1, 1), ((rows_pad, rows_p...  12.7 us
    ppermute x4, starting transfers between devices, extended(): lax.ppermute(head, axis, [((i + 1) % count, i) for i in range(ends)])  8.87 us
    ppermute x2, starting transfers between devices, passed_along(): return lax.ppermute(x, axis, pairs)  7.81 us
    dot_general x18, matrix products, band_corr(): jnp.einsum('rjc,ric->rji', taken, mine, preferred_element_type=jnp.float32)  6.9 us
  transfers between devices with their start and end apart: 10, of which 5 were waited for; matrix products, arithmetic and copies ran while one was open for 1% of the time, Pallas kernels for 0%

commit v1 on v0

v1 whole, which is shorter than its diff:
```python
import jax
import jax.numpy as jnp
from jax import lax
from jax.experimental import pallas as pl
from jax.experimental.pallas import tpu as pltpu
from jax.sharding import PartitionSpec as P

C = 128
STRIP = 12
HALO = 9
LANES = 128


def corr_rows(src_ref, own_ref, corr_ref, nrot_ref, acc_ref, acc8_ref, base, shift, half):
    for k in range(26):
        turn = 16 * (k % 8)
        row = src_ref[base + (k - 7) + shift]
        if turn:
            nrot_ref[k, turn:] = row[: LANES - turn]
            nrot_ref[k, :turn] = row[LANES - turn :]
        else:
            nrot_ref[k] = row
    col = lax.broadcasted_iota(jnp.int32, (LANES, LANES), 0)
    lane = lax.broadcasted_iota(jnp.int32, (LANES, LANES), 1)
    place = (lane - col + 4) & 127
    for k in range(0, 26, 2):
        first, last = max(0, k - 8), min(17, k + 1)
        right = nrot_ref[k : k + 2].reshape(2 * LANES, C)
        for i in range(first, last + 1):
            both = lax.dot_general(
                own_ref[i], right, (((1,), (1,)), ((), ())), preferred_element_type=jnp.float32
            )
            for side in range(2):
                a = k + side - i
                part = both[:, side * LANES : (side + 1) * LANES]
                if a == 8:
                    acc8_ref[i] = part
                elif 0 <= a < 8:
                    mask = (place >> 4) == (k + side) % 8
                    pltpu.store(acc_ref.at[i], part, mask=mask)
    step_row = (lane * 57) >> 9
    step_col = lane - 9 * step_row
    reach = col + step_col - 4
    valid = (lane < 81) & (reach >= 0) & (reach < LANES)
    start = 16 * step_row + reach
    for i in range(18):
        index = (start + 16 * i) & 127
        merged = jnp.take_along_axis(acc_ref[i], index, axis=1)
        last_a = jnp.take_along_axis(acc8_ref[i], index, axis=1)
        band = jnp.where(lane < 72, merged, last_a) * (C ** (-0.5))
        corr_ref[i, :, half * LANES : (half + 1) * LANES] = jnp.where(valid, band, 0.0).astype(
            jnp.bfloat16
        )


def shifted_sum(wide, bias):
    col = lax.broadcasted_iota(jnp.int32, (LANES, C), 0)
    left = jnp.where(col == 0, 0.0, pltpu.roll(wide[:, :C], 1, 0))
    right = jnp.where(col == LANES - 1, 0.0, pltpu.roll(wide[:, 2 * C :], LANES - 1, 0))
    return left + wide[:, C : 2 * C] + right + bias


def make_kernel(total_rows):
    def kernel(
        scal_ref, own, own_x, own_c, pair, pair_x, pair_c, outer, outer_x, outer_c,
        w1_ref, w2_ref, w3_ref, b1_ref, b2_ref, state_ref, out_ref,
        own_buf, src_buf, nrot_ref, acc_ref, acc8_ref, corr_ref, h1_ref, h2_ref, sems,
    ):
        core = scal_ref[2]
        parity = scal_ref[3]
        top = scal_ref[4]
        copies = [
            (own.at[0], own_buf.at[pl.ds(3, 12)]),
            (own_x.at[0], own_buf.at[pl.ds(15 * core, 3)]),
            (own_c.at[0, pl.ds(9 * core, 3)], own_buf.at[pl.ds(15 * (1 - core), 3)]),
        ]
        for n, (mid, far, near) in enumerate(((pair, pair_x, pair_c), (outer, outer_x, outer_c))):
            copies += [
                (mid.at[0], src_buf.at[n, pl.ds(9 + 3 * core, 12)]),
                (far.at[0], src_buf.at[n, pl.ds(24 * core, 9)]),
                (near.at[0], src_buf.at[n, pl.ds(21 * (1 - core), 12)]),
            ]
        started = [
            pltpu.make_async_copy(src, dst, sems.at[n]) for n, (src, dst) in enumerate(copies)
        ]
        for copy in started:
            copy.start()
        for copy in started:
            copy.wait()
        base = 9 + 3 * core
        corr_rows(
            src_buf.at[1 - parity], own_buf, corr_ref, nrot_ref, acc_ref, acc8_ref, base, scal_ref[0], 0
        )
        corr_rows(
            src_buf.at[parity], own_buf, corr_ref, nrot_ref, acc_ref, acc8_ref, base, scal_ref[1], 1
        )
        for m in range(16):
            left = jnp.concatenate([corr_ref[m], corr_ref[m + 1], corr_ref[m + 2]], axis=1)
            wide = jnp.dot(left, w1_ref[...], preferred_element_type=jnp.float32)
            value = jnp.maximum(shifted_sum(wide, b1_ref[...]), 0.0)
            if m < 2 or m > 13:
                row = top + (m - 2)
                value = jnp.where((row >= 0) & (row < total_rows), value, 0.0)
            h1_ref[m] = value.astype(jnp.bfloat16)
        for n in range(14):
            left = jnp.concatenate([h1_ref[n], h1_ref[n + 1], h1_ref[n + 2]], axis=1)
            wide = jnp.dot(left, w2_ref[...], preferred_element_type=jnp.float32)
            value = jnp.maximum(shifted_sum(wide, b2_ref[...]), 0.0)
            if n < 1 or n > 12:
                row = top + (n - 1)
                value = jnp.where((row >= 0) & (row < total_rows), value, 0.0)
            h2_ref[n] = value.astype(jnp.bfloat16)
        lane = lax.broadcasted_iota(jnp.int32, (8, LANES), 1)
        sums = []
        for n in range(14):
            taps = lax.dot_general(
                w3_ref[...], h2_ref[n], (((1,), (1,)), ((), ())), preferred_element_type=jnp.float32
            )
            left = jnp.where(lane == 0, 0.0, pltpu.roll(taps[:8], 1, 1))
            right = jnp.where(lane == LANES - 1, 0.0, pltpu.roll(taps[16:], LANES - 1, 1))
            sums.append(left + taps[8:16] + right)
        for r in range(12):
            delta = sums[r][0:2] + sums[r + 1][2:4] + sums[r + 2][4:6]
            out_ref[:, 0, r, :] = state_ref[:, 0, r, :] + delta

    return kernel


def align(scal, blocks, weights, biases, state, total_rows):
    hbm = pl.BlockSpec(memory_space=pl.ANY)
    vmem = pl.BlockSpec(memory_space=pltpu.VMEM)
    return pl.pallas_call(
        make_kernel(total_rows),
        out_shape=jax.ShapeDtypeStruct((2, 1, STRIP, LANES), jnp.float32),
        in_specs=[pl.BlockSpec(memory_space=pltpu.SMEM)] + [hbm] * 9 + [vmem] * 6,
        out_specs=vmem,
        scratch_shapes=[
            pltpu.VMEM((18, LANES, C), jnp.bfloat16),
            pltpu.VMEM((2, 33, LANES, C), jnp.bfloat16),
            pltpu.VMEM((26, LANES, C), jnp.bfloat16),
            pltpu.VMEM((18, LANES, LANES), jnp.float32),
            pltpu.VMEM((18, LANES, LANES), jnp.float32),
            pltpu.VMEM((18, LANES, 2 * LANES), jnp.bfloat16),
            pltpu.VMEM((16, LANES, C), jnp.bfloat16),
            pltpu.VMEM((14, LANES, C), jnp.bfloat16),
            pltpu.SemaphoreType.DMA((9,)),
        ],
        compiler_params=pltpu.CompilerParams(vmem_limit_bytes=40 * 1024 * 1024),
    )(scal, *blocks, *weights, *biases, state)


def arranged(w_first, w_second, w_third):
    first = jnp.pad(w_first.reshape(3, 3, 2, 81, 128), ((0, 0), (0, 0), (0, 0), (0, 47), (0, 0)))
    first = first.transpose(0, 2, 3, 1, 4).reshape(768, 384)
    second = w_second.transpose(0, 2, 1, 3).reshape(384, 384)
    third = jnp.pad(w_third.transpose(1, 0, 3, 2).reshape(3, 6, 128), ((0, 0), (0, 2), (0, 0)))
    return first, second, third.reshape(24, 128)


def make_body(sections, strips):
    both = ("sec", "strip")
    core_swap = [(t, t ^ 1) for t in range(strips)]
    chip_swap = [(t, ((t + 1) ^ 1) - 1) for t in range(1, strips - 1)]
    pair_swap = [(s, s ^ 1) for s in range(sections)]
    onward = [(s, s + 2 if s % 2 == 0 else s - 2) for s in range(sections)]
    onward = [(s, d) for s, d in onward if 0 <= d < sections]
    onward_chip = [(s * strips + t, d * strips + u) for s, d in onward for t, u in chip_swap]

    def body(features, offsets, state, w_first, b_first, w_second, b_second, w_third):
        sec = lax.axis_index("sec")
        strip = lax.axis_index("strip")
        core = strip % 2
        shift_above = offsets[sec]
        shift_below = jnp.where(sec > 0, -offsets[jnp.maximum(sec - 1, 0)], 0)
        scal = jnp.stack([shift_below, shift_above, core, sec % 2, strip * STRIP]).astype(jnp.int32)
        pair = lax.ppermute(features, "sec", pair_swap)
        own_x = lax.ppermute(
            lax.dynamic_slice_in_dim(features, 9 * core, 3, 1), "strip", chip_swap
        )
        own_c = lax.ppermute(features, "strip", core_swap)
        outer = lax.ppermute(pair, "sec", onward)
        edge = lax.dynamic_slice_in_dim(pair, 3 * core, HALO, 1)
        outer_x = lax.ppermute(edge, both, onward_chip)
        pair_x = lax.ppermute(edge, "strip", chip_swap)
        pair_c = lax.ppermute(pair, "strip", core_swap)
        outer_c = lax.ppermute(outer, "strip", core_swap)
        return align(
            scal,
            (features, own_x, own_c, pair, pair_x, pair_c, outer, outer_x, outer_c),
            arranged(w_first, w_second, w_third),
            (b_first[None], b_second[None]),
            state,
            strips * STRIP,
        )

    return body


def solution(mesh):
    sections, strips = mesh.shape["sec"], mesh.shape["strip"]
    in_specs = (
        P("sec", "strip", None, None),
        P(),
        P(None, "sec", "strip", None),
        P(),
        P(),
        P(),
        P(),
        P(),
    )
    out_specs = P(None, "sec", "strip", None)
    return jax.shard_map(
        make_body(sections, strips), mesh=mesh, in_specs=in_specs, out_specs=out_specs, check_vma=False
    )
```

time: 130 us -> 55.2 us (0.42)
  the two profiles are of different devices: /device:TPU:111 before, /device:TPU:113 now
where the time goes in v1:
time: 55.2 us; the launch traced here: 54.7 us
  waiting for transfers between devices  21.6 us (39%)
  starting transfers between devices  12.4 us (22%)
  local copies, waits for them, and re-layouts  10.9 us (20%)
  Pallas kernels  8.95 us (16%)
  between operations  0.87 us (2%)
    ppermute x1, waiting for transfers between devices, body(): pair = lax.ppermute(features, 'sec', pair_swap)  11.6 us
    pallas_call x1, Pallas kernels, align(): pl.pallas_call(make_kernel(total_rows), out_shape=jax.ShapeDtypeStruct((2...  8.95 us
    ppermute x1, waiting for transfers between devices, body(): pair_x = lax.ppermute(edge, 'strip', chip_swap)  5.81 us
    unnamed x23, local copies, waits for them, and re-layouts  4.59 us
    ppermute x1, waiting for transfers between devices, body(): outer = lax.ppermute(pair, 'sec', onward)  4.13 us
    ppermute x1, starting transfers between devices, body(): lax.ppermute(lax.dynamic_slice_in_dim(features, 9 * core, 3, 1), 'strip',...  2.83 us
    ppermute x1, starting transfers between devices, body(): pair_x = lax.ppermute(edge, 'strip', chip_swap)  2.79 us
    ppermute x1, starting transfers between devices, body(): outer_c = lax.ppermute(outer, 'strip', core_swap)  2.47 us
  transfers between devices with their start and end apart: 8, of which 3 were waited for; matrix products, arithmetic and copies ran while one was open for 12% of the time, Pallas kernels for 0%

profile of v1, /device:TPU:113, one launch (start us, length us, event | category | flops | bytes accessed | tf_op | source)
XLA Modules:
  0.0 54.7 jit_solution(5479638467593502518)
XLA Ops:
  0.1 11.6 %collective-permute-done.2.pair = bf16[1,12,128,128]{3,2,1,0:T(8,128)(2,1)S(1)} collective-permute-done((bf16[1,12,128,128]{3,2,1,0:T(8,128)(2,1)}, bf16[1,12,128,128]{3,2,1,0:T(8,128)(2,1)S(1)}, u32[]{:S(2)}, u32[]{:S(2)}) %collective-permute-start.2) | collective-permute-done | bytes 393248 | tf_op jit(solution)/shard_map/ppermute | solution.py:176
  11.7 1.3 %collective-permute-start.5 = (bf16[1,12,128,128]{3,2,1,0:T(8,128)(2,1)S(1)}, bf16[1,12,128,128]{3,2,1,0:T(8,128)(2,1)S(1)}, u32[]{:S(2)}, u32[]{:S(2)}) collective-permute-start(bf16[1,12,128,128]{3,2,1,0:T(8,128)(2,1)S(1)} %collective-permute-done.2.pair), channel_id=1, source_target_pairs={{0,64},{64,128},{96,32},{128,192},{160,96},{224,160},{1,65},{65,12... | collective-permute-start | bytes 1179656 | tf_op jit(solution)/shard_map/ppermute | solution.py:181
  13.0 1.6 %collective-permute-start.1 = (bf16[1,12,128,128]{3,2,1,0:T(8,128)(2,1)}, bf16[1,12,128,128]{3,2,1,0:T(8,128)(2,1)S(1)}, u32[]{:S(2)}, u32[]{:S(2)}) collective-permute-start(bf16[1,12,128,128]{3,2,1,0:T(8,128)(2,1)} %own.1), channel_id=1, source_target_pairs={{0,1},{1,0},{2,3},{3,2},{4,5},{5,4},{6,7},{7,6},{8,9},{9,8},{10,11... | collective-permute-start | bytes 1179656 | tf_op jit(solution)/shard_map/ppermute | solution.py:180
  14.6 0.9 %constant_dynamic-slice_fusion.1 = bf16[1,3,128,128]{3,2,1,0:T(8,128)(2,1)S(1)} fusion(bf16[1,12,128,128]{3,2,1,0:T(8,128)(2,1)} %own.1, s32[]{:T(128)S(6)} %select_n.29), kind=kLoop, calls=%fused_computation.5 | loop fusion | bytes 196612 | tf_op jit(solution)/shard_map/dynamic_slice | solution.py:178
  15.6 2.8 %collective-permute-start = (bf16[1,3,128,128]{3,2,1,0:T(8,128)(2,1)S(1)}, bf16[1,3,128,128]{3,2,1,0:T(8,128)(2,1)S(1)}, u32[]{:S(2)}, u32[]{:S(2)}) collective-permute-start(bf16[1,3,128,128]{3,2,1,0:T(8,128)(2,1)S(1)} %constant_dynamic-slice_fusion.1), channel_id=1, source_target_pairs={{1,2},{2,1},{3,4},{4,3},{5,6},{6,5},{7,8},{8,7},{9,10},{10,9},{11,... | collective-permute-start | bytes 294920 | tf_op jit(solution)/shard_map/ppermute | solution.py:177
  18.5 4.1 %collective-permute-done.5.outer = bf16[1,12,128,128]{3,2,1,0:T(8,128)(2,1)S(1)} collective-permute-done((bf16[1,12,128,128]{3,2,1,0:T(8,128)(2,1)S(1)}, bf16[1,12,128,128]{3,2,1,0:T(8,128)(2,1)S(1)}, u32[]{:S(2)}, u32[]{:S(2)}) %collective-permute-start.5) | collective-permute-done | bytes 393248 | tf_op jit(solution)/shard_map/ppermute | solution.py:181
  22.6 2.5 %collective-permute-start.7 = (bf16[1,12,128,128]{3,2,1,0:T(8,128)(2,1)S(1)}, bf16[1,12,128,128]{3,2,1,0:T(8,128)(2,1)S(1)}, u32[]{:S(2)}, u32[]{:S(2)}) collective-permute-start(bf16[1,12,128,128]{3,2,1,0:T(8,128)(2,1)S(1)} %collective-permute-done.5.outer), channel_id=1, source_target_pairs={{0,1},{1,0},{2,3},{3,2},{4,5},{5,4},{6,7},{7,6},{8,9},{9,8},{10,11... | collective-permute-start | bytes 1179656 | tf_op jit(solution)/shard_map/ppermute | solution.py:186
  25.1 0.7 %constant_dynamic-slice_fusion = bf16[1,9,128,128]{3,2,1,0:T(8,128)(2,1)} fusion(bf16[1,12,128,128]{3,2,1,0:T(8,128)(2,1)S(1)} %collective-permute-done.2.pair, s32[]{:T(128)S(6)} %select_n.30), kind=kLoop, calls=%fused_computation.4 | loop fusion | bytes 589828 | tf_op jit(solution)/shard_map/dynamic_slice | solution.py:182
  25.9 2.8 %collective-permute-start.3 = (bf16[1,9,128,128]{3,2,1,0:T(8,128)(2,1)}, bf16[1,9,128,128]{3,2,1,0:T(8,128)(2,1)S(1)}, u32[]{:S(2)}, u32[]{:S(2)}) collective-permute-start(bf16[1,9,128,128]{3,2,1,0:T(8,128)(2,1)} %constant_dynamic-slice_fusion), channel_id=1, source_target_pairs={{1,2},{2,1},{3,4},{4,3},{5,6},{6,5},{7,8},{8,7},{9,10},{10,9},{11,... | collective-permute-start | bytes 884744 | tf_op jit(solution)/shard_map/ppermute | solution.py:184
  28.7 1.3 %collective-permute-start.6 = (bf16[1,9,128,128]{3,2,1,0:T(8,128)(2,1)}, bf16[1,9,128,128]{3,2,1,0:T(8,128)(2,1)}, u32[]{:S(2)}, u32[]{:S(2)}) collective-permute-start(bf16[1,9,128,128]{3,2,1,0:T(8,128)(2,1)} %constant_dynamic-slice_fusion), channel_id=1, source_target_pairs={{1,66},{2,65},{3,68},{4,67},{5,70},{6,69},{7,72},{8,71},{9,74},{10... | collective-permute-start | bytes 884744 | tf_op jit(solution)/shard_map/ppermute | solution.py:183
  30.0 0.6 %copy-done.9 = s32[8]{0:T(128)S(1)} copy-done((s32[8]{0:T(128)S(1)}, s32[8]{0:T(128)}, u32[]{:S(2)}) %copy-start.9) | copy-done | bytes 56
  30.6 0.6 %fusion = (s32[1]{0:T(128)}, s32[1]{0:T(128)}) fusion(s32[8]{0:T(128)S(1)} %copy-done.9, s32[]{:T(128)S(6)} %select_n.26, s32[]{:T(128)S(6)} %max.3), kind=kLoop, calls=%fused_computation.6 | loop fusion | bytes 24 | tf_op jit(solution)/shard_map/dynamic_slice | solution.py:173
  32.1 0.5 copy.19
  32.7 0.8 %copy-done.7 = bf16[3,3,128,128]{3,2,1,0:T(8,128)(2,1)S(1)} copy-done((bf16[3,3,128,128]{3,2,1,0:T(8,128)(2,1)S(1)}, bf16[3,3,128,128]{3,2,1,0:T(8,128)(2,1)}, u32[]{:S(2)}) %copy-start.7) | copy-done | bytes 294936
  33.9 0.7 %copy-done.8 = bf16[3,3,128,2]{2,3,1,0:T(2,128)(2,1)S(1)} copy-done((bf16[3,3,128,2]{2,3,1,0:T(2,128)(2,1)S(1)}, bf16[3,3,128,2]{2,3,1,0:T(2,128)(2,1)}, u32[]{:S(2)}) %copy-start.8) | copy-done | bytes 4632
  34.6 0.6 %reshape.19 = bf16[3,6,128]{2,1,0:T(8,128)(2,1)} reshape(bf16[3,3,2,128]{3,2,1,0:T(2,128)(2,1)S(1)} %copy.15) | data formatting | bytes 9216 | tf_op jit(solution)/shard_map/reshape | solution.py:156
  35.2 0.7 %copy.17.state_ref = f32[2,1,12,128]{3,2,1,0:T(8,128)S(1)} copy(f32[2,1,12,128]{3,1,2,0:T(1,128)} %param.10) | data formatting | bytes 24576 | tf_op args[2]
  35.9 1.2 %stack.19.scal_ref = s32[5]{0:T(128)} concatenate(s32[1]{0:T(128)} %bitcast.1, s32[1]{0:T(128)} %get-tuple-element.5, s32[1]{0:T(128)} %bitcast.2, s32[1]{0:T(128)} %bitcast.3, s32[1]{0:T(128)} %bitcast.4), dimensions={0} | concatenate | bytes 40 | tf_op jit(solution)/shard_map/stack | solution.py:175
  37.1 0.7 %pad_bitcast_fusion.1.w3_ref = bf16[24,128]{1,0:T(8,128)(2,1)S(1)} fusion(bf16[3,6,128]{2,1,0:T(8,128)(2,1)} %reshape.19), kind=kLoop, calls=%fused_computation.3 | loop fusion | bytes 10752 | tf_op jit(solution)/shard_map/reshape | solution.py:157
  37.8 5.8 %collective-permute-done.3.pair_x = bf16[1,9,128,128]{3,2,1,0:T(8,128)(2,1)S(1)} collective-permute-done((bf16[1,9,128,128]{3,2,1,0:T(8,128)(2,1)}, bf16[1,9,128,128]{3,2,1,0:T(8,128)(2,1)S(1)}, u32[]{:S(2)}, u32[]{:S(2)}) %collective-permute-start.3) | collective-permute-done | bytes 294944 | tf_op jit(solution)/shard_map/ppermute | solution.py:184
  43.6 0.6 %copy-done.3 = s32[5]{0:T(128)S(1)} copy-done((s32[5]{0:T(128)S(1)}, s32[5]{0:T(128)}, u32[]{:S(2)}) %copy-start.3) | copy-done | bytes 44
  44.3 0.9 %copy-done.2 = bf16[1,3,128,128]{3,2,1,0:T(8,128)(2,1)S(1)} copy-done((bf16[1,3,128,128]{3,2,1,0:T(8,128)(2,1)S(1)}, bf16[1,3,128,128]{3,2,1,0:T(8,128)(2,1)}, u32[]{:S(2)}) %copy-start.2) | copy-done | bytes 98328
  45.2 9.0 %shard_map.82 = f32[2,1,12,128]{3,2,1,0:T(8,128)S(1)} custom-call(s32[5]{0:T(128)S(1)} %copy-done.3, bf16[1,12,128,128]{3,2,1,0:T(8,128)(2,1)S(1)} %copy-done, bf16[1,3,128,128]{3,2,1,0:T(8,128)(2,1)S(1)} %copy-done.2, bf16[1,12,128,128]{3,2,1,0:T(8,128)(2,1)S(1)} %collective-permute-done.1.own_c, bf16[1,12,128,128]{3,2,1,0:T(8,128)(2,1)S(1)} %collective-permute-done.2.pair, ...), custom_call_target="tpu_custom_call" | custom-call | tf_op jit(solution)/shard_map/pallas_call | solution.py:132
  54.1 0.6 %copy.18 = f32[2,1,12,128]{3,1,2,0:T(1,128)} copy(f32[2,1,12,128]{3,2,1,0:T(8,128)S(1)} %shard_map.82) | data formatting | bytes 24576 | tf_op jit(solution)/shard_map/pallas_call | solution.py:132
  (28 shorter events, 0.8 us)
Async XLA Ops:
  0.0 11.7 %collective-permute-start.2 = (bf16[1,12,128,128]{3,2,1,0:T(8,128)(2,1)}, bf16[1,12,128,128]{3,2,1,0:T(8,128)(2,1)S(1)}, u32[]{:S(2)}, u32[]{:S(2)}) collective-permute-start(bf16[1,12,128,128]{3,2,1,0:T(8,128)(2,1)} %own.1), channel_id=1, source_target_pairs={{0,32},{32,0},{64,96},{96,64},{128,160},{160,128},{192,224},{224,1... | collective-permute-start | bytes 1179656 | tf_op jit(solution)/shard_map/ppermute | solution.py:176
  11.7 10.9 %collective-permute-start.5 = (bf16[1,12,128,128]{3,2,1,0:T(8,128)(2,1)S(1)}, bf16[1,12,128,128]{3,2,1,0:T(8,128)(2,1)S(1)}, u32[]{:S(2)}, u32[]{:S(2)}) collective-permute-start(bf16[1,12,128,128]{3,2,1,0:T(8,128)(2,1)S(1)} %collective-permute-done.2.pair), channel_id=1, source_target_pairs={{0,64},{64,128},{96,32},{128,192},{160,96},{224,160},{1,65},{65,12... | collective-permute-start | bytes 1179656 | tf_op jit(solution)/shard_map/ppermute | solution.py:181
  13.0 24.8 %collective-permute-start.1 = (bf16[1,12,128,128]{3,2,1,0:T(8,128)(2,1)}, bf16[1,12,128,128]{3,2,1,0:T(8,128)(2,1)S(1)}, u32[]{:S(2)}, u32[]{:S(2)}) collective-permute-start(bf16[1,12,128,128]{3,2,1,0:T(8,128)(2,1)} %own.1), channel_id=1, source_target_pairs={{0,1},{1,0},{2,3},{3,2},{4,5},{5,4},{6,7},{7,6},{8,9},{9,8},{10,11... | collective-permute-start | bytes 1179656 | tf_op jit(solution)/shard_map/ppermute | solution.py:180
  14.6 17.3 %copy-start.6 = (bf16[3,3,162,128]{3,2,1,0:T(8,128)(2,1)S(1)}, bf16[3,3,162,128]{3,2,1,0:T(8,128)(2,1)}, u32[]{:S(2)}) copy-start(bf16[3,3,162,128]{3,2,1,0:T(8,128)(2,1)} %param.11) | copy-start | bytes 1119748
  15.6 13.1 %collective-permute-start = (bf16[1,3,128,128]{3,2,1,0:T(8,128)(2,1)S(1)}, bf16[1,3,128,128]{3,2,1,0:T(8,128)(2,1)S(1)}, u32[]{:S(2)}, u32[]{:S(2)}) collective-permute-start(bf16[1,3,128,128]{3,2,1,0:T(8,128)(2,1)S(1)} %constant_dynamic-slice_fusion.1), channel_id=1, source_target_pairs={{1,2},{2,1},{3,4},{4,3},{5,6},{6,5},{7,8},{8,7},{9,10},{10,9},{11,... | collective-permute-start | bytes 294920 | tf_op jit(solution)/shard_map/ppermute | solution.py:177
  18.4 25.2 %collective-permute-start.4 = (bf16[1,12,128,128]{3,2,1,0:T(8,128)(2,1)S(1)}, bf16[1,12,128,128]{3,2,1,0:T(8,128)(2,1)S(1)}, u32[]{:S(2)}, u32[]{:S(2)}) collective-permute-start(bf16[1,12,128,128]{3,2,1,0:T(8,128)(2,1)S(1)} %collective-permute-done.2.pair), channel_id=1, source_target_pairs={{0,1},{1,0},{2,3},{3,2},{4,5},{5,4},{6,7},{7,6},{8,9},{9,8},{10,11... | collective-permute-start | bytes 1179656 | tf_op jit(solution)/shard_map/ppermute | solution.py:185
  22.6 20.9 %collective-permute-start.7 = (bf16[1,12,128,128]{3,2,1,0:T(8,128)(2,1)S(1)}, bf16[1,12,128,128]{3,2,1,0:T(8,128)(2,1)S(1)}, u32[]{:S(2)}, u32[]{:S(2)}) collective-permute-start(bf16[1,12,128,128]{3,2,1,0:T(8,128)(2,1)S(1)} %collective-permute-done.5.outer), channel_id=1, source_target_pairs={{0,1},{1,0},{2,3},{3,2},{4,5},{5,4},{6,7},{7,6},{8,9},{9,8},{10,11... | collective-permute-start | bytes 1179656 | tf_op jit(solution)/shard_map/ppermute | solution.py:186
  25.9 17.7 %collective-permute-start.3 = (bf16[1,9,128,128]{3,2,1,0:T(8,128)(2,1)}, bf16[1,9,128,128]{3,2,1,0:T(8,128)(2,1)S(1)}, u32[]{:S(2)}, u32[]{:S(2)}) collective-permute-start(bf16[1,9,128,128]{3,2,1,0:T(8,128)(2,1)} %constant_dynamic-slice_fusion), channel_id=1, source_target_pairs={{1,2},{2,1},{3,4},{4,3},{5,6},{6,5},{7,8},{8,7},{9,10},{10,9},{11,... | collective-permute-start | bytes 884744 | tf_op jit(solution)/shard_map/ppermute | solution.py:184
  28.7 3.3 %copy-start.1 = (bf16[1,3,128,128]{3,2,1,0:T(8,128)(2,1)}, bf16[1,3,128,128]{3,2,1,0:T(8,128)(2,1)S(1)}, u32[]{:S(2)}) copy-start(bf16[1,3,128,128]{3,2,1,0:T(8,128)(2,1)S(1)} %collective-permute-done.own_x) | copy-start | bytes 294916
  28.7 14.9 %collective-permute-start.6 = (bf16[1,9,128,128]{3,2,1,0:T(8,128)(2,1)}, bf16[1,9,128,128]{3,2,1,0:T(8,128)(2,1)}, u32[]{:S(2)}, u32[]{:S(2)}) collective-permute-start(bf16[1,9,128,128]{3,2,1,0:T(8,128)(2,1)} %constant_dynamic-slice_fusion), channel_id=1, source_target_pairs={{1,66},{2,65},{3,68},{4,67},{5,70},{6,69},{7,72},{8,71},{9,74},{10... | collective-permute-start | bytes 884744 | tf_op jit(solution)/shard_map/ppermute | solution.py:183
  30.0 0.7 %copy-start.9 = (s32[8]{0:T(128)S(1)}, s32[8]{0:T(128)}, u32[]{:S(2)}) copy-start(s32[8]{0:T(128)} %param.9) | copy-start | bytes 100
  32.6 1.0 %copy-start.7 = (bf16[3,3,128,128]{3,2,1,0:T(8,128)(2,1)S(1)}, bf16[3,3,128,128]{3,2,1,0:T(8,128)(2,1)}, u32[]{:S(2)}) copy-start(bf16[3,3,128,128]{3,2,1,0:T(8,128)(2,1)} %param.13) | copy-start | bytes 884740
  33.8 9.8 %copy-start = (bf16[1,12,128,128]{3,2,1,0:T(8,128)(2,1)S(1)}, bf16[1,12,128,128]{3,2,1,0:T(8,128)(2,1)}, u32[]{:S(2)}) copy-start(bf16[1,12,128,128]{3,2,1,0:T(8,128)(2,1)} %own.1) | copy-start | bytes 1179652
  33.8 0.7 %copy-start.8 = (bf16[3,3,128,2]{2,3,1,0:T(2,128)(2,1)S(1)}, bf16[3,3,128,2]{2,3,1,0:T(2,128)(2,1)}, u32[]{:S(2)}) copy-start(bf16[3,3,128,2]{2,3,1,0:T(2,128)(2,1)} %param.15) | copy-start | bytes 13828
  43.6 0.6 %copy-start.3 = (s32[5]{0:T(128)S(1)}, s32[5]{0:T(128)}, u32[]{:S(2)}) copy-start(s32[5]{0:T(128)} %stack.19.scal_ref) | copy-start | bytes 64
  43.6 0.7 %copy-start.4 = (f32[128]{0:T(128)S(1)}, f32[128]{0:T(128)}, u32[]{:S(2)}) copy-start(f32[128]{0:T(128)} %param.12) | copy-start | bytes 1540
  43.6 0.7 %copy-start.5 = (f32[128]{0:T(128)S(1)}, f32[128]{0:T(128)}, u32[]{:S(2)}) copy-start(f32[128]{0:T(128)} %param.14) | copy-start | bytes 1540
  44.3 0.9 %copy-start.2 = (bf16[1,3,128,128]{3,2,1,0:T(8,128)(2,1)S(1)}, bf16[1,3,128,128]{3,2,1,0:T(8,128)(2,1)}, u32[]{:S(2)}) copy-start(bf16[1,3,128,128]{3,2,1,0:T(8,128)(2,1)} %copy-done.1) | copy-start | bytes 294916

commit v2 on v1

v2 whole, which is shorter than its diff:
```python
import jax
import jax.numpy as jnp
from jax import lax
from jax.experimental import pallas as pl
from jax.experimental.pallas import tpu as pltpu
from jax.sharding import PartitionSpec as P

C = 128
STRIP = 12
HALO = 9
LANES = 128


def corr_rows(src_ref, own_ref, corr_ref, nrot_ref, acc_ref, acc8_ref, base, shift):
    for k in range(26):
        turn = 16 * (k % 8)
        row = src_ref[base + (k - 7) + shift]
        if turn:
            nrot_ref[k, turn:] = row[: LANES - turn]
            nrot_ref[k, :turn] = row[LANES - turn :]
        else:
            nrot_ref[k] = row
    col = lax.broadcasted_iota(jnp.int32, (LANES, LANES), 0)
    lane = lax.broadcasted_iota(jnp.int32, (LANES, LANES), 1)
    place = (lane - col + 4) & 127
    for k in range(0, 26, 2):
        first, last = max(0, k - 8), min(17, k + 1)
        right = nrot_ref[k : k + 2].reshape(2 * LANES, C)
        for i in range(first, last + 1):
            both = lax.dot_general(
                own_ref[i], right, (((1,), (1,)), ((), ())), preferred_element_type=jnp.float32
            )
            for side in range(2):
                a = k + side - i
                part = both[:, side * LANES : (side + 1) * LANES]
                if a == 8:
                    acc8_ref[i] = part
                elif 0 <= a < 8:
                    mask = (place >> 4) == (k + side) % 8
                    pltpu.store(acc_ref.at[i], part, mask=mask)
    step_row = (lane * 57) >> 9
    step_col = lane - 9 * step_row
    reach = col + step_col - 4
    valid = (lane < 81) & (reach >= 0) & (reach < LANES)
    start = 16 * step_row + reach
    for i in range(18):
        index = (start + 16 * i) & 127
        merged = jnp.take_along_axis(acc_ref[i], index, axis=1)
        last_a = jnp.take_along_axis(acc8_ref[i], index, axis=1)
        band = jnp.where(lane < 72, merged, last_a) * (C ** (-0.5))
        corr_ref[i] = jnp.where(valid, band, 0.0).astype(jnp.bfloat16)


def shifted_sum(wide, bias):
    col = lax.broadcasted_iota(jnp.int32, (LANES, C), 0)
    left = jnp.where(col == 0, 0.0, pltpu.roll(wide[:, :C], 1, 0))
    right = jnp.where(col == LANES - 1, 0.0, pltpu.roll(wide[:, 2 * C :], LANES - 1, 0))
    return left + wide[:, C : 2 * C] + right + bias


def position(off_ref):
    sec = lax.axis_index("sec")
    strip = lax.axis_index("strip")
    core = lax.rem(strip, 2)
    parity = lax.rem(sec, 2)
    above = off_ref[sec]
    below = jnp.where(sec > 0, -off_ref[jnp.maximum(sec - 1, 0)], 0)
    return core, parity, strip * STRIP, above, below


def fetched(copies, sems):
    started = [pltpu.make_async_copy(src, dst, sems.at[n]) for n, (src, dst) in enumerate(copies)]
    for copy in started:
        copy.start()
    for copy in started:
        copy.wait()


def stacked(mid, far, near, buf, core, skip):
    whole = near.shape[1] == STRIP
    place = 21 * (1 - core) if whole else 21 - 18 * core
    return [
        (mid.at[0], buf.at[pl.ds(9 + 3 * core, STRIP)]),
        (far.at[0, pl.ds(skip, HALO)], buf.at[pl.ds(24 * core, HALO)]),
        (near.at[0], buf.at[pl.ds(place, near.shape[1])]),
    ]


def pair_kernel(
    off_ref, own, far, own_c, pair, pair_c, w_ref, corr_ref, own_buf, w1_ref,
    src_buf, nrot_ref, acc_ref, acc8_ref, sems,
):
    zeros = jnp.zeros((LANES, C), jnp.bfloat16)
    for dy in range(3):
        for dx in range(3):
            for half in range(2):
                w1_ref[dy, dx, half] = zeros
                w1_ref[dy, dx, half, :81] = w_ref[dy, dx, 81 * half : 81 * half + 81]
    core, parity, top, above, below = position(off_ref)
    copies = [
        (own.at[0], own_buf.at[pl.ds(3, 12)]),
        (far.at[0, pl.ds(0, 3)], own_buf.at[pl.ds(15 * core, 3)]),
        (own_c.at[0, pl.ds(9 * core, 3)], own_buf.at[pl.ds(15 * (1 - core), 3)]),
    ]
    fetched(copies + stacked(pair, far.at[:, pl.ds(3, HALO)], pair_c, src_buf, core, 0), sems)
    shift = jnp.where(parity == 0, above, below)
    corr_rows(src_buf, own_buf, corr_ref, nrot_ref, acc_ref, acc8_ref, 9 + 3 * core, shift)


def make_kernel(total_rows):
    def kernel(
        off_ref, own_buf, pair_corr, outer, outer_x, outer_c,
        w1_ref, w2_ref, w3_ref, b1_ref, b2_ref, state_ref, out_ref,
        src_buf, nrot_ref, acc_ref, acc8_ref, corr_ref, h1_ref, h2_ref, held_ref, sems,
    ):
        core, parity, top, above, below = position(off_ref)
        copies = [(pair_corr, corr_ref.at[1 - parity]), (state_ref, held_ref)]
        fetched(copies + stacked(outer, outer_x, outer_c, src_buf, core, 1 - core), sems)
        shift = jnp.where(parity == 0, below, above)
        corr_rows(
            src_buf, own_buf, corr_ref.at[parity], nrot_ref, acc_ref, acc8_ref, 9 + 3 * core, shift
        )
        first = jnp.concatenate(
            [
                jnp.concatenate([w1_ref[dy, dx, half] for dx in range(3)], axis=1)
                for dy in range(3)
                for half in range(2)
            ],
            axis=0,
        )
        second = jnp.concatenate(
            [jnp.concatenate([w2_ref[dy, dx] for dx in range(3)], axis=1) for dy in range(3)], axis=0
        )
        for m in range(16):
            left = jnp.concatenate(
                [corr_ref[half, m + dy] for dy in range(3) for half in range(2)], axis=1
            )
            wide = jnp.dot(left, first, preferred_element_type=jnp.float32)
            value = jnp.maximum(shifted_sum(wide, b1_ref[...]), 0.0)
            if m < 2 or m > 13:
                row = top + (m - 2)
                value = jnp.where((row >= 0) & (row < total_rows), value, 0.0)
            h1_ref[m] = value.astype(jnp.bfloat16)
        for n in range(14):
            left = jnp.concatenate([h1_ref[n], h1_ref[n + 1], h1_ref[n + 2]], axis=1)
            wide = jnp.dot(left, second, preferred_element_type=jnp.float32)
            value = jnp.maximum(shifted_sum(wide, b2_ref[...]), 0.0)
            if n < 1 or n > 12:
                row = top + (n - 1)
                value = jnp.where((row >= 0) & (row < total_rows), value, 0.0)
            h2_ref[n] = value.astype(jnp.bfloat16)
        lane = lax.broadcasted_iota(jnp.int32, (8, LANES), 1)
        sums = []
        for n in range(14):
            taps = lax.dot_general(
                w3_ref[...], h2_ref[n], (((1,), (1,)), ((), ())), preferred_element_type=jnp.float32
            )
            left = jnp.where(lane == 0, 0.0, pltpu.roll(taps[:8], 1, 1))
            right = jnp.where(lane == LANES - 1, 0.0, pltpu.roll(taps[16:], LANES - 1, 1))
            sums.append(left + taps[8:16] + right)
        for r in range(12):
            delta = sums[r][0:2] + sums[r + 1][2:4] + sums[r + 2][4:6]
            out_ref[:, r, 0, :] = held_ref[:, r, 0, :] + delta

    return kernel


HBM = pl.BlockSpec(memory_space=pl.ANY)
VMEM = pl.BlockSpec(memory_space=pltpu.VMEM)
SMEM = pl.BlockSpec(memory_space=pltpu.SMEM)
PARAMS = pltpu.CompilerParams(vmem_limit_bytes=32 * 1024 * 1024)
SOURCE = [
    pltpu.VMEM((33, LANES, C), jnp.bfloat16),
    pltpu.VMEM((26, LANES, C), jnp.bfloat16),
    pltpu.VMEM((18, LANES, LANES), jnp.float32),
    pltpu.VMEM((18, LANES, LANES), jnp.float32),
]


def pair_corr(offsets, blocks, w_first):
    rows = jax.ShapeDtypeStruct((18, LANES, C), jnp.bfloat16)
    return pl.pallas_call(
        pair_kernel,
        out_shape=(rows, rows, jax.ShapeDtypeStruct((3, 3, 2, LANES, C), jnp.bfloat16)),
        in_specs=[SMEM] + [HBM] * 5 + [VMEM],
        out_specs=(VMEM, VMEM, VMEM),
        scratch_shapes=SOURCE + [pltpu.SemaphoreType.DMA((6,))],
        compiler_params=PARAMS,
        cost_estimate=pl.CostEstimate(
            flops=2 * 18 * 9 * LANES * LANES * C, bytes_accessed=100 * LANES * C * 2, transcendentals=0
        ),
    )(offsets, *blocks, w_first)


def align(offsets, own, blocks, weights, biases, state, total_rows):
    return pl.pallas_call(
        make_kernel(total_rows),
        out_shape=jax.ShapeDtypeStruct((2, STRIP, 1, LANES), jnp.float32),
        in_specs=[SMEM, VMEM] + [HBM] * 4 + [VMEM] * 5 + [HBM],
        out_specs=VMEM,
        scratch_shapes=SOURCE
        + [
            pltpu.VMEM((2, 18, LANES, LANES), jnp.bfloat16),
            pltpu.VMEM((16, LANES, C), jnp.bfloat16),
            pltpu.VMEM((14, LANES, C), jnp.bfloat16),
            pltpu.VMEM((2, STRIP, 1, LANES), jnp.float32),
            pltpu.SemaphoreType.DMA((5,)),
        ],
        compiler_params=PARAMS,
    )(offsets, own, *blocks, *weights, *biases, state)


def arranged(w_third):
    third = jnp.pad(w_third.transpose(1, 0, 3, 2).reshape(3, 6, 128), ((0, 0), (0, 2), (0, 0)))
    return third.reshape(24, 128)


def make_body(sections, strips):
    both = ("sec", "strip")
    core_swap = [(t, t ^ 1) for t in range(strips)]
    chip_swap = [(t, ((t + 1) ^ 1) - 1) for t in range(1, strips - 1)]
    pair_swap = [(s, s ^ 1) for s in range(sections)]
    onward = [(s, s + 2 if s % 2 == 0 else s - 2) for s in range(sections)]
    onward = [(s, d) for s, d in onward if 0 <= d < sections]
    next_chip = [(s ^ 1, d) for s, d in onward]
    next_chip = [(s * strips + t, d * strips + u) for s, d in next_chip for t, u in chip_swap]

    def body(features, offsets, state, w_first, b_first, w_second, b_second, w_third):
        core = lax.rem(lax.axis_index("strip"), 2)
        pair = lax.ppermute(features, "sec", pair_swap)
        own_c = lax.ppermute(features, "strip", core_swap)
        rim = lax.dynamic_slice_in_dim(features, 9 * core, 3, 1)
        edge = lax.dynamic_slice_in_dim(features, 2 * core, HALO + 1, 1)
        third = arranged(w_third)
        pair, own_c, rim, edge, third = lax.optimization_barrier((pair, own_c, rim, edge, third))
        outer = lax.ppermute(pair, "sec", onward)
        far = jnp.concatenate([rim, lax.dynamic_slice_in_dim(pair, 3 * core, HALO, 1)], 1)
        far = lax.ppermute(far, "strip", chip_swap)
        outer_x = lax.ppermute(edge, both, next_chip)
        pair_c = lax.ppermute(pair, "strip", core_swap)
        corr, own_all, first = pair_corr(offsets, (features, far, own_c, pair, pair_c), w_first)
        outer, corr = lax.optimization_barrier((outer, corr))
        near = lax.dynamic_slice_in_dim(outer, 3 * (1 - core), HALO, 1)
        outer_c = lax.ppermute(near, "strip", core_swap)
        out = align(
            offsets,
            own_all,
            (corr, outer, outer_x, outer_c),
            (first, w_second, third),
            (b_first[None], b_second[None]),
            state.reshape(2, STRIP, 1, LANES),
            strips * STRIP,
        )
        return out.reshape(2, 1, STRIP, LANES)

    return body


def solution(mesh):
    sections, strips = mesh.shape["sec"], mesh.shape["strip"]
    in_specs = (
        P("sec", "strip", None, None),
        P(),
        P(None, "sec", "strip", None),
        P(),
        P(),
        P(),
        P(),
        P(),
    )
    out_specs = P(None, "sec", "strip", None)
    return jax.shard_map(
        make_body(sections, strips), mesh=mesh, in_specs=in_specs, out_specs=out_specs, check_vma=False
    )
```

time: 55.2 us -> 41.9 us (0.76)
  the two profiles are of different devices: /device:TPU:113 before, /device:TPU:122 now
where the time goes in v2:
time: 41.9 us; the launch traced here: 41.7 us
  waiting for transfers between devices  16.7 us (40%)
  starting transfers between devices  11.2 us (27%)
  Pallas kernels  10.3 us (25%)
  local copies, waits for them, and re-layouts  3.34 us (8%)
    ppermute x1, waiting for transfers between devices, body(): pair = lax.ppermute(features, 'sec', pair_swap)  8.68 us
    pallas_call x1, Pallas kernels, align(): pl.pallas_call(make_kernel(total_rows), out_shape=jax.ShapeDtypeStruct((2...  6.29 us
    pallas_call x1, Pallas kernels, pair_corr(): pl.pallas_call(pair_kernel, out_shape=(rows, rows, jax.ShapeDtypeStruct((...  3.96 us
    ppermute x1, waiting for transfers between devices, body(): far = lax.ppermute(far, 'strip', chip_swap)  3.5 us
    ppermute x1, starting transfers between devices, body(): pair_c = lax.ppermute(pair, 'strip', core_swap)  3.5 us
    ppermute x1, waiting for transfers between devices, body(): outer_x = lax.ppermute(edge, both, next_chip)  3.41 us
    ppermute x1, starting transfers between devices, body(): outer = lax.ppermute(pair, 'sec', onward)  2.43 us
    ppermute x1, starting transfers between devices, body(): far = lax.ppermute(far, 'strip', chip_swap)  2.05 us
  transfers between devices with their start and end apart: 7, of which 4 were waited for; matrix products, arithmetic and copies ran while one was open for 5% of the time, Pallas kernels for 10%

profile of v2, /device:TPU:122, one launch (start us, length us, event | category | flops | bytes accessed | tf_op | source)
XLA Modules:
  0.0 41.7 jit_solution(8936110735286171468)
XLA Ops:
  0.0 1.2 %collective-permute-start = (bf16[1,12,128,128]{3,2,1,0:T(8,128)(2,1)}, bf16[1,12,128,128]{3,2,1,0:T(8,128)(2,1)S(1)}, u32[]{:S(2)}, u32[]{:S(2)}) collective-permute-start(bf16[1,12,128,128]{3,2,1,0:T(8,128)(2,1)} %own.1), channel_id=1, source_target_pairs={{0,32},{32,0},{64,96},{96,64},{128,160},{160,128},{192,224},{224,1... | collective-permute-start | bytes 1179656 | tf_op jit(solution)/shard_map/ppermute | solution.py:230
  1.2 0.0 collective-permute-start.1
  1.2 0.7 %copy-done.7 = bf16[3,3,128,2]{2,3,1,0:T(2,128)(2,1)S(1)} copy-done((bf16[3,3,128,2]{2,3,1,0:T(2,128)(2,1)S(1)}, bf16[3,3,128,2]{2,3,1,0:T(2,128)(2,1)}, u32[]{:S(2)}) %copy-start.7) | copy-done | bytes 4632
  2.0 0.9 %constant_dynamic-slice_fusion.3 = bf16[1,3,128,128]{3,2,1,0:T(8,128)(2,1)S(1)} fusion(bf16[1,12,128,128]{3,2,1,0:T(8,128)(2,1)} %own.1, s32[]{:T(128)S(6)} %select_n.12), kind=kLoop, calls=%fused_computation.5 | loop fusion | bytes 196612 | tf_op jit(solution)/shard_map/dynamic_slice | solution.py:232
  2.9 1.0 %constant_dynamic-slice_fusion.2 = bf16[1,10,128,128]{3,2,1,0:T(8,128)(2,1)S(1)} fusion(bf16[1,12,128,128]{3,2,1,0:T(8,128)(2,1)} %own.1, s32[]{:T(128)S(6)} %select_n.13), kind=kLoop, calls=%fused_computation.4 | loop fusion | bytes 655364 | tf_op jit(solution)/shard_map/dynamic_slice | solution.py:233
  3.9 8.7 %collective-permute-done.pair = bf16[1,12,128,128]{3,2,1,0:T(8,128)(2,1)S(1)} collective-permute-done((bf16[1,12,128,128]{3,2,1,0:T(8,128)(2,1)}, bf16[1,12,128,128]{3,2,1,0:T(8,128)(2,1)S(1)}, u32[]{:S(2)}, u32[]{:S(2)}) %collective-permute-start) | collective-permute-done | bytes 393248 | tf_op jit(solution)/shard_map/ppermute | solution.py:230
  12.6 0.0 collective-permute-done.1.own_c
  12.6 0.0 copy-start
  12.6 0.0 copy-start.6
  12.7 2.1 %collective-permute-start.2 = (bf16[1,12,128,128]{3,2,1,0:T(8,128)(2,1)S(1)}, bf16[1,12,128,128]{3,2,1,0:T(8,128)(2,1)S(1)}, u32[]{:S(2)}, u32[]{:S(2)}) collective-permute-start(bf16[1,12,128,128]{3,2,1,0:T(8,128)(2,1)S(1)} %pad_maximum_fusion), channel_id=1, source_target_pairs={{1,2},{2,1},{3,4},{4,3},{5,6},{6,5},{7,8},{8,7},{9,10},{10,9},{11,... | collective-permute-start | bytes 1179656 | tf_op jit(solution)/shard_map/ppermute | solution.py:238
  14.7 3.5 %collective-permute-start.3 = (bf16[1,12,128,128]{3,2,1,0:T(8,128)(2,1)S(1)}, bf16[1,12,128,128]{3,2,1,0:T(8,128)(2,1)S(1)}, u32[]{:S(2)}, u32[]{:S(2)}) collective-permute-start(bf16[1,12,128,128]{3,2,1,0:T(8,128)(2,1)S(1)} %collective-permute-done.pair), channel_id=1, source_target_pairs={{0,1},{1,0},{2,3},{3,2},{4,5},{5,4},{6,7},{7,6},{8,9},{9,8},{10,11... | collective-permute-start | bytes 1179656 | tf_op jit(solution)/shard_map/ppermute | solution.py:240
  18.2 2.4 %collective-permute-start.4 = (bf16[1,12,128,128]{3,2,1,0:T(8,128)(2,1)S(1)}, bf16[1,12,128,128]{3,2,1,0:T(8,128)(2,1)S(1)}, u32[]{:S(2)}, u32[]{:S(2)}) collective-permute-start(bf16[1,12,128,128]{3,2,1,0:T(8,128)(2,1)S(1)} %collective-permute-done.pair), channel_id=1, source_target_pairs={{0,64},{64,128},{96,32},{128,192},{160,96},{224,160},{1,65},{65,12... | collective-permute-start | bytes 1179656 | tf_op jit(solution)/shard_map/ppermute | solution.py:236
  20.7 0.0 copy-start.3
  20.7 1.9 %collective-permute-start.5 = (bf16[1,10,128,128]{3,2,1,0:T(8,128)(2,1)S(1)}, bf16[1,10,128,128]{3,2,1,0:T(8,128)(2,1)S(1)}, u32[]{:S(2)}, u32[]{:S(2)}) collective-permute-start(bf16[1,10,128,128]{3,2,1,0:T(8,128)(2,1)S(1)} %constant_dynamic-slice_fusion.2), channel_id=1, source_target_pairs={{33,66},{34,65},{35,68},{36,67},{37,70},{38,69},{39,72},{40,71},{4... | collective-permute-start | bytes 983048 | tf_op jit(solution)/shard_map/ppermute | solution.py:239
  22.6 3.5 %collective-permute-done.2.far = bf16[1,12,128,128]{3,2,1,0:T(8,128)(2,1)S(1)} collective-permute-done((bf16[1,12,128,128]{3,2,1,0:T(8,128)(2,1)S(1)}, bf16[1,12,128,128]{3,2,1,0:T(8,128)(2,1)S(1)}, u32[]{:S(2)}, u32[]{:S(2)}) %collective-permute-start.2) | collective-permute-done | bytes 393248 | tf_op jit(solution)/shard_map/ppermute | solution.py:238
  26.1 0.0 collective-permute-done.3.pair_c
  26.1 4.0 %shard_map.82 = (bf16[18,128,128]{2,1,0:T(8,128)(2,1)S(1)}, bf16[18,128,128]{2,1,0:T(8,128)(2,1)S(1)}, bf16[3,3,2,128,128]{4,3,2,1,0:T(8,128)(2,1)S(1)}) custom-call(s32[8]{0:T(128)S(1)} %copy-done.3, bf16[1,12,128,128]{3,2,1,0:T(8,128)(2,1)S(1)} %copy-done, bf16[1,12,128,128]{3,2,1,0:T(8,128)(2,1)S(1)} %collective-permute-done.2.far, ...), custom_call_target="tpu_custom_call" | custom-call | flops 679477248 | bytes 3276800 | tf_op jit(solution)/shard_map/pallas_call | solution.py:182
  30.1 1.1 %collective-permute-done.4.outer = bf16[1,12,128,128]{3,2,1,0:T(8,128)(2,1)S(1)} collective-permute-done((bf16[1,12,128,128]{3,2,1,0:T(8,128)(2,1)S(1)}, bf16[1,12,128,128]{3,2,1,0:T(8,128)(2,1)S(1)}, u32[]{:S(2)}, u32[]{:S(2)}) %collective-permute-start.4) | collective-permute-done | bytes 393248 | tf_op jit(solution)/shard_map/ppermute | solution.py:236
  31.2 0.1 collective-permute-start.6
  31.3 3.4 %collective-permute-done.5.outer_x = bf16[1,10,128,128]{3,2,1,0:T(8,128)(2,1)S(1)} collective-permute-done((bf16[1,10,128,128]{3,2,1,0:T(8,128)(2,1)S(1)}, bf16[1,10,128,128]{3,2,1,0:T(8,128)(2,1)S(1)}, u32[]{:S(2)}, u32[]{:S(2)}) %collective-permute-start.5) | collective-permute-done | bytes 327712 | tf_op jit(solution)/shard_map/ppermute | solution.py:239
  34.7 0.0 collective-permute-done.6.outer_c
  34.7 0.6 %copy-done.4 = f32[128]{0:T(128)S(1)} copy-done((f32[128]{0:T(128)S(1)}, f32[128]{0:T(128)}, u32[]{:S(2)}) %copy-start.4) | copy-done | bytes 536
  35.4 0.0 copy-done.5
  35.4 6.3 %shard_map.83 = f32[2,12,1,128]{3,2,1,0:T(1,128)} custom-call(s32[8]{0:T(128)S(1)} %copy-done.3, bf16[18,128,128]{2,1,0:T(8,128)(2,1)S(1)} %get-tuple-element.18.own_buf, bf16[18,128,128]{2,1,0:T(8,128)(2,1)S(1)} %get-tuple-element.20.pair_corr, bf16[1,12,128,128]{3,2,1,0:T(8,128)(2,1)S(1)} %collective-permute-done.4.outer, ...), custom_call_target="tpu_custom_call" | custom-call | tf_op jit(solution)/shard_map/pallas_call | solution.py:196
  (16 shorter events, 0.1 us)
Async XLA Ops:
  0.0 12.6 %collective-permute-start = (bf16[1,12,128,128]{3,2,1,0:T(8,128)(2,1)}, bf16[1,12,128,128]{3,2,1,0:T(8,128)(2,1)S(1)}, u32[]{:S(2)}, u32[]{:S(2)}) collective-permute-start(bf16[1,12,128,128]{3,2,1,0:T(8,128)(2,1)} %own.1), channel_id=1, source_target_pairs={{0,32},{32,0},{64,96},{96,64},{128,160},{160,128},{192,224},{224,1... | collective-permute-start | bytes 1179656 | tf_op jit(solution)/shard_map/ppermute | solution.py:230
  1.2 11.3 %collective-permute-start.1 = (bf16[1,12,128,128]{3,2,1,0:T(8,128)(2,1)}, bf16[1,12,128,128]{3,2,1,0:T(8,128)(2,1)S(1)}, u32[]{:S(2)}, u32[]{:S(2)}) collective-permute-start(bf16[1,12,128,128]{3,2,1,0:T(8,128)(2,1)} %own.1), channel_id=1, source_target_pairs={{0,1},{1,0},{2,3},{3,2},{4,5},{5,4},{6,7},{7,6},{8,9},{9,8},{10,11... | collective-permute-start | bytes 1179656 | tf_op jit(solution)/shard_map/ppermute | solution.py:231
  1.2 0.7 %copy-start.7 = (bf16[3,3,128,2]{2,3,1,0:T(2,128)(2,1)S(1)}, bf16[3,3,128,2]{2,3,1,0:T(2,128)(2,1)}, u32[]{:S(2)}) copy-start(bf16[3,3,128,2]{2,3,1,0:T(2,128)(2,1)} %param.15) | copy-start | bytes 13828
  12.6 13.5 %copy-start = (bf16[1,12,128,128]{3,2,1,0:T(8,128)(2,1)S(1)}, bf16[1,12,128,128]{3,2,1,0:T(8,128)(2,1)}, u32[]{:S(2)}) copy-start(bf16[1,12,128,128]{3,2,1,0:T(8,128)(2,1)} %own.1) | copy-start | bytes 1179652
  12.6 13.5 %copy-start.6 = (bf16[3,3,162,128]{3,2,1,0:T(8,128)(2,1)S(1)}, bf16[3,3,162,128]{3,2,1,0:T(8,128)(2,1)}, u32[]{:S(2)}) copy-start(bf16[3,3,162,128]{3,2,1,0:T(8,128)(2,1)} %w_ref.1) | copy-start | bytes 1119748
  12.7 13.4 %collective-permute-start.2 = (bf16[1,12,128,128]{3,2,1,0:T(8,128)(2,1)S(1)}, bf16[1,12,128,128]{3,2,1,0:T(8,128)(2,1)S(1)}, u32[]{:S(2)}, u32[]{:S(2)}) collective-permute-start(bf16[1,12,128,128]{3,2,1,0:T(8,128)(2,1)S(1)} %pad_maximum_fusion), channel_id=1, source_target_pairs={{1,2},{2,1},{3,4},{4,3},{5,6},{6,5},{7,8},{8,7},{9,10},{10,9},{11,... | collective-permute-start | bytes 1179656 | tf_op jit(solution)/shard_map/ppermute | solution.py:238
  14.7 11.4 %collective-permute-start.3 = (bf16[1,12,128,128]{3,2,1,0:T(8,128)(2,1)S(1)}, bf16[1,12,128,128]{3,2,1,0:T(8,128)(2,1)S(1)}, u32[]{:S(2)}, u32[]{:S(2)}) collective-permute-start(bf16[1,12,128,128]{3,2,1,0:T(8,128)(2,1)S(1)} %collective-permute-done.pair), channel_id=1, source_target_pairs={{0,1},{1,0},{2,3},{3,2},{4,5},{5,4},{6,7},{7,6},{8,9},{9,8},{10,11... | collective-permute-start | bytes 1179656 | tf_op jit(solution)/shard_map/ppermute | solution.py:240
  18.2 12.9 %collective-permute-start.4 = (bf16[1,12,128,128]{3,2,1,0:T(8,128)(2,1)S(1)}, bf16[1,12,128,128]{3,2,1,0:T(8,128)(2,1)S(1)}, u32[]{:S(2)}, u32[]{:S(2)}) collective-permute-start(bf16[1,12,128,128]{3,2,1,0:T(8,128)(2,1)S(1)} %collective-permute-done.pair), channel_id=1, source_target_pairs={{0,64},{64,128},{96,32},{128,192},{160,96},{224,160},{1,65},{65,12... | collective-permute-start | bytes 1179656 | tf_op jit(solution)/shard_map/ppermute | solution.py:236
  20.7 5.5 %copy-start.3 = (s32[8]{0:T(128)S(1)}, s32[8]{0:T(128)}, u32[]{:S(2)}) copy-start(s32[8]{0:T(128)} %off_ref.3) | copy-start | bytes 100
  20.7 14.0 %collective-permute-start.5 = (bf16[1,10,128,128]{3,2,1,0:T(8,128)(2,1)S(1)}, bf16[1,10,128,128]{3,2,1,0:T(8,128)(2,1)S(1)}, u32[]{:S(2)}, u32[]{:S(2)}) collective-permute-start(bf16[1,10,128,128]{3,2,1,0:T(8,128)(2,1)S(1)} %constant_dynamic-slice_fusion.2), channel_id=1, source_target_pairs={{33,66},{34,65},{35,68},{36,67},{37,70},{38,69},{39,72},{40,71},{4... | collective-permute-start | bytes 983048 | tf_op jit(solution)/shard_map/ppermute | solution.py:239
  31.2 3.6 %copy-start.1 = (bf16[3,3,128,128]{3,2,1,0:T(8,128)(2,1)S(1)}, bf16[3,3,128,128]{3,2,1,0:T(8,128)(2,1)}, u32[]{:S(2)}) copy-start(bf16[3,3,128,128]{3,2,1,0:T(8,128)(2,1)} %w2_ref.1) | copy-start | bytes 884740
  31.2 3.6 %copy-start.2 = (f32[2,1,12,128]{3,1,2,0:T(1,128)S(1)}, f32[2,1,12,128]{3,1,2,0:T(1,128)}, u32[]{:S(2)}) copy-start(f32[2,1,12,128]{3,1,2,0:T(1,128)} %param.10) | copy-start | bytes 36868
  31.2 3.5 %collective-permute-start.6 = (bf16[1,9,128,128]{3,2,1,0:T(8,128)(2,1)S(1)}, bf16[1,9,128,128]{3,2,1,0:T(8,128)(2,1)S(1)}, u32[]{:S(2)}, u32[]{:S(2)}) collective-permute-start(bf16[1,9,128,128]{3,2,1,0:T(8,128)(2,1)S(1)} %constant_dynamic-slice_fusion), channel_id=1, source_target_pairs={{0,1},{1,0},{2,3},{3,2},{4,5},{5,4},{6,7},{7,6},{8,9},{9,8},{10,11... | collective-permute-start | bytes 884744 | tf_op jit(solution)/shard_map/ppermute | solution.py:244
  34.7 0.7 %copy-start.4 = (f32[128]{0:T(128)S(1)}, f32[128]{0:T(128)}, u32[]{:S(2)}) copy-start(f32[128]{0:T(128)} %param.12) | copy-start | bytes 1540
  34.7 0.7 %copy-start.5 = (f32[128]{0:T(128)S(1)}, f32[128]{0:T(128)}, u32[]{:S(2)}) copy-start(f32[128]{0:T(128)} %param.14) | copy-start | bytes 1540

commit v3 on v2

v3 whole, which is shorter than its diff:
```python
import jax
import jax.numpy as jnp
from jax import lax
from jax.experimental import pallas as pl
from jax.experimental.pallas import tpu as pltpu
from jax.sharding import PartitionSpec as P

C = 128
STRIP = 12
HALO = 9
LANES = 128


def turned(nrot_ref, mid, far, near, core, shift, far_low, far_high, near_low):
    for k in range(26):
        at = k - 7 + shift
        row = mid[0, jnp.clip(at, 0, STRIP - 1)]
        if k < 9:
            low_far = far[0, jnp.clip(at + HALO, 0, HALO - 1) + far_low]
            low_near = near[0, jnp.clip(at + HALO, 0, HALO - 1) + near_low]
            row = jnp.where(at < 0, jnp.where(core == 0, low_far, low_near), row)
        if k > 16:
            high_far = far[0, jnp.clip(at - STRIP, 0, HALO - 1) + far_high]
            high_near = near[0, jnp.clip(at - STRIP, 0, HALO - 1)]
            row = jnp.where(at >= STRIP, jnp.where(core == 0, high_near, high_far), row)
        turn = 16 * (k % 8)
        if turn:
            nrot_ref[k, turn:] = row[: LANES - turn]
            nrot_ref[k, :turn] = row[LANES - turn :]
        else:
            nrot_ref[k] = row


def corr_rows(own_ref, corr_ref, nrot_ref, acc_ref, acc8_ref):
    col = lax.broadcasted_iota(jnp.int32, (LANES, LANES), 0)
    lane = lax.broadcasted_iota(jnp.int32, (LANES, LANES), 1)
    place = (lane - col + 4) & 127
    for k in range(0, 26, 2):
        first, last = max(0, k - 8), min(17, k + 1)
        right = nrot_ref[k : k + 2].reshape(2 * LANES, C)
        for i in range(first, last + 1):
            both = lax.dot_general(
                own_ref[i], right, (((1,), (1,)), ((), ())), preferred_element_type=jnp.float32
            )
            for side in range(2):
                a = k + side - i
                part = both[:, side * LANES : (side + 1) * LANES]
                if a == 8:
                    acc8_ref[i] = part
                elif 0 <= a < 8:
                    mask = (place >> 4) == (k + side) % 8
                    pltpu.store(acc_ref.at[i], part, mask=mask)
    step_row = (lane * 57) >> 9
    step_col = lane - 9 * step_row
    reach = col + step_col - 4
    valid = (lane < 81) & (reach >= 0) & (reach < LANES)
    start = 16 * step_row + reach
    for i in range(18):
        index = (start + 16 * i) & 127
        merged = jnp.take_along_axis(acc_ref[i], index, axis=1)
        last_a = jnp.take_along_axis(acc8_ref[i], index, axis=1)
        band = jnp.where(lane < 72, merged, last_a) * (C ** (-0.5))
        corr_ref[i] = jnp.where(valid, band, 0.0).astype(jnp.bfloat16)


def shifted_sum(wide):
    col = lax.broadcasted_iota(jnp.int32, (LANES, C), 0)
    left = jnp.where(col == 0, 0.0, pltpu.roll(wide[:, :C], 1, 0))
    right = jnp.where(col == LANES - 1, 0.0, pltpu.roll(wide[:, 2 * C :], LANES - 1, 0))
    return left + wide[:, C : 2 * C] + right


def position(off_ref):
    sec = lax.axis_index("sec")
    strip = lax.axis_index("strip")
    core = lax.rem(strip, 2)
    parity = lax.rem(sec, 2)
    above = off_ref[sec]
    below = jnp.where(sec > 0, -off_ref[jnp.maximum(sec - 1, 0)], 0)
    return core, parity, strip * STRIP, above, below


def convolved(rows, kernel_blocks, m):
    left = jnp.concatenate([rows[m + dy] for dy in range(3)], axis=1)
    return jnp.dot(left, kernel_blocks, preferred_element_type=jnp.float32)


def blocks_of(w_ref):
    return jnp.concatenate(
        [jnp.concatenate([w_ref[dy, dx] for dx in range(3)], axis=1) for dy in range(3)], axis=0
    )


def pair_kernel(
    off_ref, own, far, own_c, pair, pair_c, w_ref, b1_ref, b2_ref, part_ref, own_buf, w_outer, b2_out,
    nrot_ref, acc_ref, acc8_ref, corr_ref, w_pair, halves,
):
    core, parity, top, above, below = position(off_ref)
    zeros = jnp.zeros((LANES, C), jnp.bfloat16)
    for dy in range(3):
        for dx in range(3):
            for half in range(2):
                halves[half] = zeros
                halves[half, :81] = w_ref[dy, dx, 81 * half : 81 * half + 81]
            w_pair[dy, dx] = halves[1 - parity]
            w_outer[dy, dx] = halves[parity]
    for r in range(3):
        own_buf[r] = jnp.where(core == 0, far[0, r], own_c[0, 9 + r])
        own_buf[15 + r] = jnp.where(core == 0, own_c[0, r], far[0, r])
    for r in range(STRIP):
        own_buf[3 + r] = own[0, r]
    shift = jnp.where(parity == 0, above, below)
    turned(nrot_ref, pair, far, pair_c, core, shift, 3, 3, 3)
    corr_rows(own_buf, corr_ref, nrot_ref, acc_ref, acc8_ref)
    b2_out[...] = b2_ref[...]
    kernel_blocks = blocks_of(w_pair)
    for m in range(16):
        part_ref[m] = shifted_sum(convolved(corr_ref, kernel_blocks, m)) + b1_ref[...]


def make_kernel(total_rows):
    def kernel(
        off_ref, part_ref, own_buf, outer, outer_x, outer_c, w1_ref, w2_ref, w3_ref, b2_ref,
        state_ref, out_ref, nrot_ref, acc_ref, acc8_ref, corr_ref, h1_ref, h2_ref, held_ref, sem,
    ):
        held = pltpu.make_async_copy(state_ref, held_ref, sem)
        held.start()
        core, parity, top, above, below = position(off_ref)
        shift = jnp.where(parity == 0, below, above)
        turned(nrot_ref, outer, outer_x, outer_c, core, shift, 1, 0, 0)
        corr_rows(own_buf, corr_ref, nrot_ref, acc_ref, acc8_ref)
        first = blocks_of(w1_ref)
        second = blocks_of(w2_ref)
        for m in range(16):
            value = jnp.maximum(part_ref[m] + shifted_sum(convolved(corr_ref, first, m)), 0.0)
            if m < 2 or m > 13:
                row = top + (m - 2)
                value = jnp.where((row >= 0) & (row < total_rows), value, 0.0)
            h1_ref[m] = value.astype(jnp.bfloat16)
        for n in range(14):
            value = jnp.maximum(shifted_sum(convolved(h1_ref, second, n)) + b2_ref[...], 0.0)
            if n < 1 or n > 12:
                row = top + (n - 1)
                value = jnp.where((row >= 0) & (row < total_rows), value, 0.0)
            h2_ref[n] = value.astype(jnp.bfloat16)
        lane = lax.broadcasted_iota(jnp.int32, (8, LANES), 1)
        sums = []
        for n in range(14):
            taps = lax.dot_general(
                w3_ref[...], h2_ref[n], (((1,), (1,)), ((), ())), preferred_element_type=jnp.float32
            )
            left = jnp.where(lane == 0, 0.0, pltpu.roll(taps[:8], 1, 1))
            right = jnp.where(lane == LANES - 1, 0.0, pltpu.roll(taps[16:], LANES - 1, 1))
            sums.append(left + taps[8:16] + right)
        held.wait()
        for r in range(12):
            delta = sums[r][0:2] + sums[r + 1][2:4] + sums[r + 2][4:6]
            out_ref[:, r, 0, :] = held_ref[:, r, 0, :] + delta

    return kernel


HBM = pl.BlockSpec(memory_space=pl.ANY)
VMEM = pl.BlockSpec(memory_space=pltpu.VMEM)
SMEM = pl.BlockSpec(memory_space=pltpu.SMEM)
PARAMS = pltpu.CompilerParams(vmem_limit_bytes=32 * 1024 * 1024)
CORR = [
    pltpu.VMEM((26, LANES, C), jnp.bfloat16),
    pltpu.VMEM((18, LANES, LANES), jnp.float32),
    pltpu.VMEM((18, LANES, LANES), jnp.float32),
    pltpu.VMEM((18, LANES, LANES), jnp.bfloat16),
]
TAPS = pltpu.VMEM((3, 3, LANES, C), jnp.bfloat16)


def pair_part(offsets, blocks, w_first, b_first, b_second):
    return pl.pallas_call(
        pair_kernel,
        out_shape=(
            jax.ShapeDtypeStruct((16, LANES, C), jnp.float32),
            jax.ShapeDtypeStruct((18, LANES, C), jnp.bfloat16),
            jax.ShapeDtypeStruct((3, 3, LANES, C), jnp.bfloat16),
            jax.ShapeDtypeStruct((1, C), jnp.float32),
        ),
        in_specs=[SMEM] + [VMEM] * 8,
        out_specs=(VMEM, VMEM, VMEM, VMEM),
        scratch_shapes=CORR + [TAPS, pltpu.VMEM((2, LANES, C), jnp.bfloat16)],
        compiler_params=PARAMS,
        cost_estimate=pl.CostEstimate(
            flops=2 * 18 * 9 * LANES * LANES * C, bytes_accessed=100 * LANES * C * 2, transcendentals=0
        ),
    )(offsets, *blocks, w_first, b_first, b_second)


def align(offsets, part, own, blocks, weights, b_second, state, total_rows):
    return pl.pallas_call(
        make_kernel(total_rows),
        out_shape=jax.ShapeDtypeStruct((2, STRIP, 1, LANES), jnp.float32),
        in_specs=[SMEM] + [VMEM] * 9 + [HBM],
        out_specs=VMEM,
        scratch_shapes=CORR
        + [
            pltpu.VMEM((16, LANES, C), jnp.bfloat16),
            pltpu.VMEM((14, LANES, C), jnp.bfloat16),
            pltpu.VMEM((2, STRIP, 1, LANES), jnp.float32),
            pltpu.SemaphoreType.DMA,
        ],
        compiler_params=PARAMS,
    )(offsets, part, own, *blocks, *weights, b_second, state)


def arranged(w_third):
    third = jnp.pad(w_third.transpose(1, 0, 3, 2).reshape(3, 6, 128), ((0, 0), (0, 2), (0, 0)))
    return third.reshape(24, 128)


def make_body(sections, strips):
    both = ("sec", "strip")
    core_swap = [(t, t ^ 1) for t in range(strips)]
    chip_swap = [(t, ((t + 1) ^ 1) - 1) for t in range(1, strips - 1)]
    pair_swap = [(s, s ^ 1) for s in range(sections)]
    onward = [(s, s + 2 if s % 2 == 0 else s - 2) for s in range(sections)]
    onward = [(s, d) for s, d in onward if 0 <= d < sections]
    next_chip = [(s ^ 1, d) for s, d in onward]
    next_chip = [(s * strips + t, d * strips + u) for s, d in next_chip for t, u in chip_swap]

    def body(features, offsets, state, w_first, b_first, w_second, b_second, w_third):
        core = lax.rem(lax.axis_index("strip"), 2)
        pair = lax.ppermute(features, "sec", pair_swap)
        own_c = lax.ppermute(features, "strip", core_swap)
        rim = lax.dynamic_slice_in_dim(features, 9 * core, 3, 1)
        edge = lax.dynamic_slice_in_dim(features, 2 * core, HALO + 1, 1)
        third = arranged(w_third)
        pair, own_c, rim, edge, third = lax.optimization_barrier((pair, own_c, rim, edge, third))
        outer = lax.ppermute(pair, "sec", onward)
        far = jnp.concatenate([rim, lax.dynamic_slice_in_dim(pair, 3 * core, HALO, 1)], 1)
        far = lax.ppermute(far, "strip", chip_swap)
        outer_x = lax.ppermute(edge, both, next_chip)
        pair_c = lax.ppermute(pair, "strip", core_swap)
        part, own_all, first, bias = pair_part(
            offsets, (features, far, own_c, pair, pair_c), w_first, b_first[None], b_second[None]
        )
        outer, part = lax.optimization_barrier((outer, part))
        near = lax.dynamic_slice_in_dim(outer, 3 * (1 - core), HALO, 1)
        outer_c = lax.ppermute(near, "strip", core_swap)
        out = align(
            offsets,
            part,
            own_all,
            (outer, outer_x, outer_c),
            (first, w_second, third),
            bias,
            state.reshape(2, STRIP, 1, LANES),
            strips * STRIP,
        )
        return out.reshape(2, 1, STRIP, LANES)

    return body


def solution(mesh):
    sections, strips = mesh.shape["sec"], mesh.shape["strip"]
    in_specs = (
        P("sec", "strip", None, None),
        P(),
        P(None, "sec", "strip", None),
        P(),
        P(),
        P(),
        P(),
        P(),
    )
    out_specs = P(None, "sec", "strip", None)
    return jax.shard_map(
        make_body(sections, strips), mesh=mesh, in_specs=in_specs, out_specs=out_specs, check_vma=False
    )
```

time: 41.9 us -> 40.4 us (0.964)
  Pallas kernels: 10.3 us -> 9.41 us
  waiting for transfers between devices: 16.7 us -> 16 us
    pallas_call x1, Pallas kernels: 6.29 us -> 5.47 us  [align(): pl.pallas_call(make_kernel(total_rows), out_shape=jax.ShapeDtypeStruct((2...]
    ppermute x1, waiting for transfers between devices: 1.05 us -> 0.41 us  [body(): outer = lax.ppermute(pair, 'sec', onward)]
where the time goes in v3:
time: 40.4 us; the launch traced here: 40.2 us
  waiting for transfers between devices  16 us (40%)
  starting transfers between devices  11.2 us (28%)
  Pallas kernels  9.41 us (23%)
  local copies, waits for them, and re-layouts  3.34 us (8%)
    ppermute x1, waiting for transfers between devices, body(): pair = lax.ppermute(features, 'sec', pair_swap)  8.68 us
    pallas_call x1, Pallas kernels, align(): pl.pallas_call(make_kernel(total_rows), out_shape=jax.ShapeDtypeStruct((2...  5.47 us
    pallas_call x1, Pallas kernels, pair_part(): pl.pallas_call(pair_kernel, out_shape=(jax.ShapeDtypeStruct((16, LANES, C...  3.93 us
    ppermute x1, waiting for transfers between devices, body(): far = lax.ppermute(far, 'strip', chip_swap)  3.51 us
    ppermute x1, starting transfers between devices, body(): pair_c = lax.ppermute(pair, 'strip', core_swap)  3.5 us
    ppermute x1, waiting for transfers between devices, body(): outer_x = lax.ppermute(edge, both, next_chip)  3.4 us
    ppermute x1, starting transfers between devices, body(): outer = lax.ppermute(pair, 'sec', onward)  2.43 us
    ppermute x1, starting transfers between devices, body(): far = lax.ppermute(far, 'strip', chip_swap)  2.05 us
  transfers between devices with their start and end apart: 7, of which 4 were waited for; matrix products, arithmetic and copies ran while one was open for 5% of the time, Pallas kernels for 10%

profile of v3, /device:TPU:122, one launch (start us, length us, event | category | flops | bytes accessed | tf_op | source)
XLA Modules:
  0.0 40.2 jit_solution(10571464757525767853)
XLA Ops:
  0.0 1.2 %collective-permute-start = (bf16[1,12,128,128]{3,2,1,0:T(8,128)(2,1)}, bf16[1,12,128,128]{3,2,1,0:T(8,128)(2,1)S(1)}, u32[]{:S(2)}, u32[]{:S(2)}) collective-permute-start(bf16[1,12,128,128]{3,2,1,0:T(8,128)(2,1)} %own.1), channel_id=1, source_target_pairs={{0,32},{32,0},{64,96},{96,64},{128,160},{160,128},{192,224},{224,1... | collective-permute-start | bytes 1179656 | tf_op jit(solution)/shard_map/ppermute | solution.py:229
  1.2 0.0 collective-permute-start.1
  1.2 0.7 %copy-done.7 = bf16[3,3,128,2]{2,3,1,0:T(2,128)(2,1)S(1)} copy-done((bf16[3,3,128,2]{2,3,1,0:T(2,128)(2,1)S(1)}, bf16[3,3,128,2]{2,3,1,0:T(2,128)(2,1)}, u32[]{:S(2)}) %copy-start.7) | copy-done | bytes 4632
  2.0 0.9 %constant_dynamic-slice_fusion.3 = bf16[1,3,128,128]{3,2,1,0:T(8,128)(2,1)S(1)} fusion(bf16[1,12,128,128]{3,2,1,0:T(8,128)(2,1)} %own.1, s32[]{:T(128)S(6)} %select_n.12), kind=kLoop, calls=%fused_computation.5 | loop fusion | bytes 196612 | tf_op jit(solution)/shard_map/dynamic_slice | solution.py:231
  2.9 1.0 %constant_dynamic-slice_fusion.2 = bf16[1,10,128,128]{3,2,1,0:T(8,128)(2,1)S(1)} fusion(bf16[1,12,128,128]{3,2,1,0:T(8,128)(2,1)} %own.1, s32[]{:T(128)S(6)} %select_n.13), kind=kLoop, calls=%fused_computation.4 | loop fusion | bytes 655364 | tf_op jit(solution)/shard_map/dynamic_slice | solution.py:232
  3.9 8.7 %collective-permute-done.pair = bf16[1,12,128,128]{3,2,1,0:T(8,128)(2,1)S(1)} collective-permute-done((bf16[1,12,128,128]{3,2,1,0:T(8,128)(2,1)}, bf16[1,12,128,128]{3,2,1,0:T(8,128)(2,1)S(1)}, u32[]{:S(2)}, u32[]{:S(2)}) %collective-permute-start) | collective-permute-done | bytes 393248 | tf_op jit(solution)/shard_map/ppermute | solution.py:229
  12.6 0.0 collective-permute-done.1.own_c
  12.6 0.0 copy-start
  12.6 0.0 copy-start.4
  12.7 2.1 %collective-permute-start.3 = (bf16[1,12,128,128]{3,2,1,0:T(8,128)(2,1)S(1)}, bf16[1,12,128,128]{3,2,1,0:T(8,128)(2,1)S(1)}, u32[]{:S(2)}, u32[]{:S(2)}) collective-permute-start(bf16[1,12,128,128]{3,2,1,0:T(8,128)(2,1)S(1)} %pad_maximum_fusion), channel_id=1, source_target_pairs={{1,2},{2,1},{3,4},{4,3},{5,6},{6,5},{7,8},{8,7},{9,10},{10,9},{11,... | collective-permute-start | bytes 1179656 | tf_op jit(solution)/shard_map/ppermute | solution.py:237
  14.7 3.5 %collective-permute-start.4 = (bf16[1,12,128,128]{3,2,1,0:T(8,128)(2,1)S(1)}, bf16[1,12,128,128]{3,2,1,0:T(8,128)(2,1)S(1)}, u32[]{:S(2)}, u32[]{:S(2)}) collective-permute-start(bf16[1,12,128,128]{3,2,1,0:T(8,128)(2,1)S(1)} %collective-permute-done.pair), channel_id=1, source_target_pairs={{0,1},{1,0},{2,3},{3,2},{4,5},{5,4},{6,7},{7,6},{8,9},{9,8},{10,11... | collective-permute-start | bytes 1179656 | tf_op jit(solution)/shard_map/ppermute | solution.py:239
  18.2 2.4 %collective-permute-start.2 = (bf16[1,12,128,128]{3,2,1,0:T(8,128)(2,1)S(1)}, bf16[1,12,128,128]{3,2,1,0:T(8,128)(2,1)S(1)}, u32[]{:S(2)}, u32[]{:S(2)}) collective-permute-start(bf16[1,12,128,128]{3,2,1,0:T(8,128)(2,1)S(1)} %collective-permute-done.pair), channel_id=1, source_target_pairs={{0,64},{64,128},{96,32},{128,192},{160,96},{224,160},{1,65},{65,12... | collective-permute-start | bytes 1179656 | tf_op jit(solution)/shard_map/ppermute | solution.py:235
  20.7 1.9 %collective-permute-start.5 = (bf16[1,10,128,128]{3,2,1,0:T(8,128)(2,1)S(1)}, bf16[1,10,128,128]{3,2,1,0:T(8,128)(2,1)S(1)}, u32[]{:S(2)}, u32[]{:S(2)}) collective-permute-start(bf16[1,10,128,128]{3,2,1,0:T(8,128)(2,1)S(1)} %constant_dynamic-slice_fusion.2), channel_id=1, source_target_pairs={{33,66},{34,65},{35,68},{36,67},{37,70},{38,69},{39,72},{40,71},{4... | collective-permute-start | bytes 983048 | tf_op jit(solution)/shard_map/ppermute | solution.py:238
  22.6 3.5 %collective-permute-done.3.far = bf16[1,12,128,128]{3,2,1,0:T(8,128)(2,1)S(1)} collective-permute-done((bf16[1,12,128,128]{3,2,1,0:T(8,128)(2,1)S(1)}, bf16[1,12,128,128]{3,2,1,0:T(8,128)(2,1)S(1)}, u32[]{:S(2)}, u32[]{:S(2)}) %collective-permute-start.3) | collective-permute-done | bytes 393248 | tf_op jit(solution)/shard_map/ppermute | solution.py:237
  26.1 0.0 collective-permute-done.4.pair_c
  26.1 0.6 %copy-done.3 = s32[8]{0:T(128)S(1)} copy-done((s32[8]{0:T(128)S(1)}, s32[8]{0:T(128)}, u32[]{:S(2)}) %copy-start.3) | copy-done | bytes 56
  26.8 0.0 copy-done.5
  26.8 0.0 copy-done.6
  26.8 3.9 %shard_map.82 = (f32[16,128,128]{2,1,0:T(8,128)S(1)}, bf16[18,128,128]{2,1,0:T(8,128)(2,1)S(1)}, bf16[3,3,128,128]{3,2,1,0:T(8,128)(2,1)S(1)}, f32[1,128]{1,0:T(1,128)S(1)}) custom-call(s32[8]{0:T(128)S(1)} %copy-done.3, bf16[1,12,128,128]{3,2,1,0:T(8,128)(2,1)S(1)} %copy-done, bf16[1,12,128,128]{3,2,1,0:T(8,128)(2,1)S(1)} %collective-permute-done.3.far, ...), custom_call_target="tpu_custom_call" | custom-call | flops 679477248 | bytes 3276800 | tf_op jit(solution)/shard_map/pallas_call | solution.py:177
  30.7 0.4 %collective-permute-done.2.outer = bf16[1,12,128,128]{3,2,1,0:T(8,128)(2,1)S(1)} collective-permute-done((bf16[1,12,128,128]{3,2,1,0:T(8,128)(2,1)S(1)}, bf16[1,12,128,128]{3,2,1,0:T(8,128)(2,1)S(1)}, u32[]{:S(2)}, u32[]{:S(2)}) %collective-permute-start.2) | collective-permute-done | bytes 393248 | tf_op jit(solution)/shard_map/ppermute | solution.py:235
  31.2 0.1 collective-permute-start.6
  31.3 3.4 %collective-permute-done.5.outer_x = bf16[1,10,128,128]{3,2,1,0:T(8,128)(2,1)S(1)} collective-permute-done((bf16[1,10,128,128]{3,2,1,0:T(8,128)(2,1)S(1)}, bf16[1,10,128,128]{3,2,1,0:T(8,128)(2,1)S(1)}, u32[]{:S(2)}, u32[]{:S(2)}) %collective-permute-start.5) | collective-permute-done | bytes 327712 | tf_op jit(solution)/shard_map/ppermute | solution.py:238
  34.7 0.0 collective-permute-done.6.outer_c
  34.7 5.5 %shard_map.83 = f32[2,12,1,128]{3,2,1,0:T(1,128)} custom-call(s32[8]{0:T(128)S(1)} %copy-done.3, f32[16,128,128]{2,1,0:T(8,128)S(1)} %get-tuple-element.20.part_ref, bf16[18,128,128]{2,1,0:T(8,128)(2,1)S(1)} %get-tuple-element.21.own_buf, bf16[1,12,128,128]{3,2,1,0:T(8,128)(2,1)S(1)} %collective-permute-done.2.outer, ...), custom_call_target="tpu_custom_call" | custom-call | tf_op jit(solution)/shard_map/pallas_call | solution.py:196
  (16 shorter events, 0.1 us)
Async XLA Ops:
  0.0 12.6 %collective-permute-start = (bf16[1,12,128,128]{3,2,1,0:T(8,128)(2,1)}, bf16[1,12,128,128]{3,2,1,0:T(8,128)(2,1)S(1)}, u32[]{:S(2)}, u32[]{:S(2)}) collective-permute-start(bf16[1,12,128,128]{3,2,1,0:T(8,128)(2,1)} %own.1), channel_id=1, source_target_pairs={{0,32},{32,0},{64,96},{96,64},{128,160},{160,128},{192,224},{224,1... | collective-permute-start | bytes 1179656 | tf_op jit(solution)/shard_map/ppermute | solution.py:229
  1.2 11.3 %collective-permute-start.1 = (bf16[1,12,128,128]{3,2,1,0:T(8,128)(2,1)}, bf16[1,12,128,128]{3,2,1,0:T(8,128)(2,1)S(1)}, u32[]{:S(2)}, u32[]{:S(2)}) collective-permute-start(bf16[1,12,128,128]{3,2,1,0:T(8,128)(2,1)} %own.1), channel_id=1, source_target_pairs={{0,1},{1,0},{2,3},{3,2},{4,5},{5,4},{6,7},{7,6},{8,9},{9,8},{10,11... | collective-permute-start | bytes 1179656 | tf_op jit(solution)/shard_map/ppermute | solution.py:230
  1.2 0.7 %copy-start.7 = (bf16[3,3,128,2]{2,3,1,0:T(2,128)(2,1)S(1)}, bf16[3,3,128,2]{2,3,1,0:T(2,128)(2,1)}, u32[]{:S(2)}) copy-start(bf16[3,3,128,2]{2,3,1,0:T(2,128)(2,1)} %param.15) | copy-start | bytes 13828
  12.6 13.5 %copy-start = (bf16[1,12,128,128]{3,2,1,0:T(8,128)(2,1)S(1)}, bf16[1,12,128,128]{3,2,1,0:T(8,128)(2,1)}, u32[]{:S(2)}) copy-start(bf16[1,12,128,128]{3,2,1,0:T(8,128)(2,1)} %own.1) | copy-start | bytes 1179652
  12.6 13.5 %copy-start.4 = (bf16[3,3,162,128]{3,2,1,0:T(8,128)(2,1)S(1)}, bf16[3,3,162,128]{3,2,1,0:T(8,128)(2,1)}, u32[]{:S(2)}) copy-start(bf16[3,3,162,128]{3,2,1,0:T(8,128)(2,1)} %w_ref.1) | copy-start | bytes 1119748
  12.7 13.4 %collective-permute-start.3 = (bf16[1,12,128,128]{3,2,1,0:T(8,128)(2,1)S(1)}, bf16[1,12,128,128]{3,2,1,0:T(8,128)(2,1)S(1)}, u32[]{:S(2)}, u32[]{:S(2)}) collective-permute-start(bf16[1,12,128,128]{3,2,1,0:T(8,128)(2,1)S(1)} %pad_maximum_fusion), channel_id=1, source_target_pairs={{1,2},{2,1},{3,4},{4,3},{5,6},{6,5},{7,8},{8,7},{9,10},{10,9},{11,... | collective-permute-start | bytes 1179656 | tf_op jit(solution)/shard_map/ppermute | solution.py:237
  14.7 11.4 %collective-permute-start.4 = (bf16[1,12,128,128]{3,2,1,0:T(8,128)(2,1)S(1)}, bf16[1,12,128,128]{3,2,1,0:T(8,128)(2,1)S(1)}, u32[]{:S(2)}, u32[]{:S(2)}) collective-permute-start(bf16[1,12,128,128]{3,2,1,0:T(8,128)(2,1)S(1)} %collective-permute-done.pair), channel_id=1, source_target_pairs={{0,1},{1,0},{2,3},{3,2},{4,5},{5,4},{6,7},{7,6},{8,9},{9,8},{10,11... | collective-permute-start | bytes 1179656 | tf_op jit(solution)/shard_map/ppermute | solution.py:239
  18.2 12.9 %collective-permute-start.2 = (bf16[1,12,128,128]{3,2,1,0:T(8,128)(2,1)S(1)}, bf16[1,12,128,128]{3,2,1,0:T(8,128)(2,1)S(1)}, u32[]{:S(2)}, u32[]{:S(2)}) collective-permute-start(bf16[1,12,128,128]{3,2,1,0:T(8,128)(2,1)S(1)} %collective-permute-done.pair), channel_id=1, source_target_pairs={{0,64},{64,128},{96,32},{128,192},{160,96},{224,160},{1,65},{65,12... | collective-permute-start | bytes 1179656 | tf_op jit(solution)/shard_map/ppermute | solution.py:235
  20.7 14.0 %collective-permute-start.5 = (bf16[1,10,128,128]{3,2,1,0:T(8,128)(2,1)S(1)}, bf16[1,10,128,128]{3,2,1,0:T(8,128)(2,1)S(1)}, u32[]{:S(2)}, u32[]{:S(2)}) collective-permute-start(bf16[1,10,128,128]{3,2,1,0:T(8,128)(2,1)S(1)} %constant_dynamic-slice_fusion.2), channel_id=1, source_target_pairs={{33,66},{34,65},{35,68},{36,67},{37,70},{38,69},{39,72},{40,71},{4... | collective-permute-start | bytes 983048 | tf_op jit(solution)/shard_map/ppermute | solution.py:238
  26.1 0.7 %copy-start.3 = (s32[8]{0:T(128)S(1)}, s32[8]{0:T(128)}, u32[]{:S(2)}) copy-start(s32[8]{0:T(128)} %off_ref.3) | copy-start | bytes 100
  26.1 0.7 %copy-start.5 = (f32[128]{0:T(128)S(1)}, f32[128]{0:T(128)}, u32[]{:S(2)}) copy-start(f32[128]{0:T(128)} %param.12) | copy-start | bytes 1540
  26.1 0.7 %copy-start.6 = (f32[128]{0:T(128)S(1)}, f32[128]{0:T(128)}, u32[]{:S(2)}) copy-start(f32[128]{0:T(128)} %param.14) | copy-start | bytes 1540
  31.2 3.5 %copy-start.1 = (bf16[3,3,128,128]{3,2,1,0:T(8,128)(2,1)S(1)}, bf16[3,3,128,128]{3,2,1,0:T(8,128)(2,1)}, u32[]{:S(2)}) copy-start(bf16[3,3,128,128]{3,2,1,0:T(8,128)(2,1)} %w2_ref.1) | copy-start | bytes 884740
  31.2 3.5 %copy-start.2 = (f32[2,1,12,128]{3,1,2,0:T(1,128)S(1)}, f32[2,1,12,128]{3,1,2,0:T(1,128)}, u32[]{:S(2)}) copy-start(f32[2,1,12,128]{3,1,2,0:T(1,128)} %param.10) | copy-start | bytes 36868
  31.2 3.5 %collective-permute-start.6 = (bf16[1,9,128,128]{3,2,1,0:T(8,128)(2,1)S(1)}, bf16[1,9,128,128]{3,2,1,0:T(8,128)(2,1)S(1)}, u32[]{:S(2)}, u32[]{:S(2)}) collective-permute-start(bf16[1,9,128,128]{3,2,1,0:T(8,128)(2,1)S(1)} %constant_dynamic-slice_fusion), channel_id=1, source_target_pairs={{0,1},{1,0},{2,3},{3,2},{4,5},{5,4},{6,7},{7,6},{8,9},{9,8},{10,11... | collective-permute-start | bytes 884744 | tf_op jit(solution)/shard_map/ppermute | solution.py:245

commit v4 on v3

--- a/solution.py
+++ b/solution.py
@@ -53,20 +53,24 @@
     step_row = (lane * 57) >> 9
     step_col = lane - 9 * step_row
     reach = col + step_col - 4
-    valid = (lane < 81) & (reach >= 0) & (reach < LANES)
+    valid = (reach >= 0) & (reach < LANES)
     start = 16 * step_row + reach
     for i in range(18):
         index = (start + 16 * i) & 127
         merged = jnp.take_along_axis(acc_ref[i], index, axis=1)
         last_a = jnp.take_along_axis(acc8_ref[i], index, axis=1)
         band = jnp.where(lane < 72, merged, last_a) * (C ** (-0.5))
-        corr_ref[i] = jnp.where(valid, band, 0.0).astype(jnp.bfloat16)
+        head = jnp.where(valid[:8], band[:8], 0.0)
+        tail = jnp.where(valid[-8:], band[-8:], 0.0)
+        corr_ref[i] = jnp.concatenate([head, band[8:-8], tail], axis=0).astype(jnp.bfloat16)
 
 
 def shifted_sum(wide):
-    col = lax.broadcasted_iota(jnp.int32, (LANES, C), 0)
-    left = jnp.where(col == 0, 0.0, pltpu.roll(wide[:, :C], 1, 0))
-    right = jnp.where(col == LANES - 1, 0.0, pltpu.roll(wide[:, 2 * C :], LANES - 1, 0))
+    row = lax.broadcasted_iota(jnp.int32, (8, C), 0)
+    left = pltpu.roll(wide[:, :C], 1, 0)
+    left = jnp.concatenate([jnp.where(row == 0, 0.0, left[:8]), left[8:]], axis=0)
+    right = pltpu.roll(wide[:, 2 * C :], LANES - 1, 0)
+    right = jnp.concatenate([right[:-8], jnp.where(row == 7, 0.0, right[-8:])], axis=0)
     return left + wide[:, C : 2 * C] + right
 
 
@@ -81,14 +85,16 @@
 
 
 def convolved(rows, kernel_blocks, m):
-    left = jnp.concatenate([rows[m + dy] for dy in range(3)], axis=1)
-    return jnp.dot(left, kernel_blocks, preferred_element_type=jnp.float32)
+    left = jnp.concatenate([rows[m + dy] for dy in range(4)], axis=1)
+    both = jnp.dot(left, kernel_blocks, preferred_element_type=jnp.float32)
+    return shifted_sum(both[:, : 3 * C]), shifted_sum(both[:, 3 * C :])
 
 
 def blocks_of(w_ref):
-    return jnp.concatenate(
-        [jnp.concatenate([w_ref[dy, dx] for dx in range(3)], axis=1) for dy in range(3)], axis=0
-    )
+    zeros = jnp.zeros((C, 3 * C), jnp.bfloat16)
+    taps = [jnp.concatenate([w_ref[dy, dx] for dx in range(3)], axis=1) for dy in range(3)]
+    low = jnp.concatenate(taps + [zeros], axis=0)
+    return jnp.concatenate([low, jnp.concatenate([zeros] + taps, axis=0)], axis=1)
 
 
 def pair_kernel(
@@ -114,8 +120,9 @@
     corr_rows(own_buf, corr_ref, nrot_ref, acc_ref, acc8_ref)
     b2_out[...] = b2_ref[...]
     kernel_blocks = blocks_of(w_pair)
-    for m in range(16):
-        part_ref[m] = shifted_sum(convolved(corr_ref, kernel_blocks, m)) + b1_ref[...]
+    for m in range(0, 16, 2):
+        for side, value in enumerate(convolved(corr_ref, kernel_blocks, m)):
+            part_ref[m + side] = value + b1_ref[...]
 
 
 def make_kernel(total_rows):
@@ -131,27 +138,34 @@
         corr_rows(own_buf, corr_ref, nrot_ref, acc_ref, acc8_ref)
         first = blocks_of(w1_ref)
         second = blocks_of(w2_ref)
-        for m in range(16):
-            value = jnp.maximum(part_ref[m] + shifted_sum(convolved(corr_ref, first, m)), 0.0)
-            if m < 2 or m > 13:
-                row = top + (m - 2)
-                value = jnp.where((row >= 0) & (row < total_rows), value, 0.0)
-            h1_ref[m] = value.astype(jnp.bfloat16)
-        for n in range(14):
-            value = jnp.maximum(shifted_sum(convolved(h1_ref, second, n)) + b2_ref[...], 0.0)
-            if n < 1 or n > 12:
-                row = top + (n - 1)
-                value = jnp.where((row >= 0) & (row < total_rows), value, 0.0)
-            h2_ref[n] = value.astype(jnp.bfloat16)
+        for m in range(0, 16, 2):
+            for r, value in enumerate(convolved(corr_ref, first, m), m):
+                value = jnp.maximum(part_ref[r] + value, 0.0)
+                if r < 2 or r > 13:
+                    row = top + (r - 2)
+                    value = jnp.where((row >= 0) & (row < total_rows), value, 0.0)
+                h1_ref[r] = value.astype(jnp.bfloat16)
+        for n in range(0, 14, 2):
+            for r, value in enumerate(convolved(h1_ref, second, n), n):
+                value = jnp.maximum(value + b2_ref[...], 0.0)
+                if r < 1 or r > 12:
+                    row = top + (r - 1)
+                    value = jnp.where((row >= 0) & (row < total_rows), value, 0.0)
+                h2_ref[r] = value.astype(jnp.bfloat16)
         lane = lax.broadcasted_iota(jnp.int32, (8, LANES), 1)
         sums = []
-        for n in range(14):
+        for n in range(0, 14, 2):
             taps = lax.dot_general(
-                w3_ref[...], h2_ref[n], (((1,), (1,)), ((), ())), preferred_element_type=jnp.float32
+                w3_ref[...],
+                h2_ref[n : n + 2].reshape(2 * LANES, C),
+                (((1,), (1,)), ((), ())),
+                preferred_element_type=jnp.float32,
             )
-            left = jnp.where(lane == 0, 0.0, pltpu.roll(taps[:8], 1, 1))
-            right = jnp.where(lane == LANES - 1, 0.0, pltpu.roll(taps[16:], LANES - 1, 1))
-            sums.append(left + taps[8:16] + right)
+            for side in range(2):
+                tap = taps[:, side * LANES : (side + 1) * LANES]
+                left = jnp.where(lane == 0, 0.0, pltpu.roll(tap[:8], 1, 1))
+                right = jnp.where(lane == LANES - 1, 0.0, pltpu.roll(tap[16:], LANES - 1, 1))
+                sums.append(left + tap[8:16] + right)
         held.wait()
         for r in range(12):
             delta = sums[r][0:2] + sums[r + 1][2:4] + sums[r + 2][4:6]

time: 40.4 us -> 39.9 us (0.988)
  Pallas kernels: 9.41 us -> 8.63 us
    pallas_call x1, Pallas kernels: 5.47 us -> 4.94 us  [align(): pl.pallas_call(make_kernel(total_rows), out_shape=jax.ShapeDtypeStruct((2...]
  transfers between devices with their start and end apart: 7 -> 7, of which waited for: 4 -> 4; matrix products, arithmetic and copies ran while one was open for 5% -> 5% of each run, Pallas kernels for 10% -> 9%
where the time goes in v4:
time: 39.9 us; the launch traced here: 39.6 us
  waiting for transfers between devices  16.3 us (41%)
  starting transfers between devices  11.2 us (28%)
  Pallas kernels  8.63 us (22%)
  local copies, waits for them, and re-layouts  3.34 us (8%)
    ppermute x1, waiting for transfers between devices, body(): pair = lax.ppermute(features, 'sec', pair_swap)  8.68 us
    pallas_call x1, Pallas kernels, align(): pl.pallas_call(make_kernel(total_rows), out_shape=jax.ShapeDtypeStruct((2...  4.94 us
    pallas_call x1, Pallas kernels, pair_part(): pl.pallas_call(pair_kernel, out_shape=(jax.ShapeDtypeStruct((16, LANES, C...  3.69 us
    ppermute x1, waiting for transfers between devices, body(): far = lax.ppermute(far, 'strip', chip_swap)  3.51 us
    ppermute x1, starting transfers between devices, body(): pair_c = lax.ppermute(pair, 'strip', core_swap)  3.5 us
    ppermute x1, waiting for transfers between devices, body(): outer_x = lax.ppermute(edge, both, next_chip)  3.4 us
    ppermute x1, starting transfers between devices, body(): outer = lax.ppermute(pair, 'sec', onward)  2.43 us
    ppermute x1, starting transfers between devices, body(): far = lax.ppermute(far, 'strip', chip_swap)  2.05 us
  transfers between devices with their start and end apart: 7, of which 4 were waited for; matrix products, arithmetic and copies ran while one was open for 5% of the time, Pallas kernels for 9%

profile of v4, /device:TPU:122, one launch (start us, length us, event | category | flops | bytes accessed | tf_op | source)
XLA Modules:
  0.0 39.6 jit_solution(13512793227845935218)
XLA Ops:
  0.0 1.2 %collective-permute-start = (bf16[1,12,128,128]{3,2,1,0:T(8,128)(2,1)}, bf16[1,12,128,128]{3,2,1,0:T(8,128)(2,1)S(1)}, u32[]{:S(2)}, u32[]{:S(2)}) collective-permute-start(bf16[1,12,128,128]{3,2,1,0:T(8,128)(2,1)} %own.1), channel_id=1, source_target_pairs={{0,32},{32,0},{64,96},{96,64},{128,160},{160,128},{192,224},{224,1... | collective-permute-start | bytes 1179656 | tf_op jit(solution)/shard_map/ppermute | solution.py:243
  1.2 0.0 collective-permute-start.1
  1.2 0.7 %copy-done.7 = bf16[3,3,128,2]{2,3,1,0:T(2,128)(2,1)S(1)} copy-done((bf16[3,3,128,2]{2,3,1,0:T(2,128)(2,1)S(1)}, bf16[3,3,128,2]{2,3,1,0:T(2,128)(2,1)}, u32[]{:S(2)}) %copy-start.7) | copy-done | bytes 4632
  2.0 0.9 %constant_dynamic-slice_fusion.3 = bf16[1,3,128,128]{3,2,1,0:T(8,128)(2,1)S(1)} fusion(bf16[1,12,128,128]{3,2,1,0:T(8,128)(2,1)} %own.1, s32[]{:T(128)S(6)} %select_n.12), kind=kLoop, calls=%fused_computation.5 | loop fusion | bytes 196612 | tf_op jit(solution)/shard_map/dynamic_slice | solution.py:245
  2.9 1.0 %constant_dynamic-slice_fusion.2 = bf16[1,10,128,128]{3,2,1,0:T(8,128)(2,1)S(1)} fusion(bf16[1,12,128,128]{3,2,1,0:T(8,128)(2,1)} %own.1, s32[]{:T(128)S(6)} %select_n.13), kind=kLoop, calls=%fused_computation.4 | loop fusion | bytes 655364 | tf_op jit(solution)/shard_map/dynamic_slice | solution.py:246
  3.9 8.7 %collective-permute-done.pair = bf16[1,12,128,128]{3,2,1,0:T(8,128)(2,1)S(1)} collective-permute-done((bf16[1,12,128,128]{3,2,1,0:T(8,128)(2,1)}, bf16[1,12,128,128]{3,2,1,0:T(8,128)(2,1)S(1)}, u32[]{:S(2)}, u32[]{:S(2)}) %collective-permute-start) | collective-permute-done | bytes 393248 | tf_op jit(solution)/shard_map/ppermute | solution.py:243
  12.6 0.0 collective-permute-done.1.own_c
  12.6 0.0 copy-start
  12.6 0.0 copy-start.4
  12.7 2.1 %collective-permute-start.3 = (bf16[1,12,128,128]{3,2,1,0:T(8,128)(2,1)S(1)}, bf16[1,12,128,128]{3,2,1,0:T(8,128)(2,1)S(1)}, u32[]{:S(2)}, u32[]{:S(2)}) collective-permute-start(bf16[1,12,128,128]{3,2,1,0:T(8,128)(2,1)S(1)} %pad_maximum_fusion), channel_id=1, source_target_pairs={{1,2},{2,1},{3,4},{4,3},{5,6},{6,5},{7,8},{8,7},{9,10},{10,9},{11,... | collective-permute-start | bytes 1179656 | tf_op jit(solution)/shard_map/ppermute | solution.py:251
  14.7 3.5 %collective-permute-start.4 = (bf16[1,12,128,128]{3,2,1,0:T(8,128)(2,1)S(1)}, bf16[1,12,128,128]{3,2,1,0:T(8,128)(2,1)S(1)}, u32[]{:S(2)}, u32[]{:S(2)}) collective-permute-start(bf16[1,12,128,128]{3,2,1,0:T(8,128)(2,1)S(1)} %collective-permute-done.pair), channel_id=1, source_target_pairs={{0,1},{1,0},{2,3},{3,2},{4,5},{5,4},{6,7},{7,6},{8,9},{9,8},{10,11... | collective-permute-start | bytes 1179656 | tf_op jit(solution)/shard_map/ppermute | solution.py:253
  18.2 2.4 %collective-permute-start.2 = (bf16[1,12,128,128]{3,2,1,0:T(8,128)(2,1)S(1)}, bf16[1,12,128,128]{3,2,1,0:T(8,128)(2,1)S(1)}, u32[]{:S(2)}, u32[]{:S(2)}) collective-permute-start(bf16[1,12,128,128]{3,2,1,0:T(8,128)(2,1)S(1)} %collective-permute-done.pair), channel_id=1, source_target_pairs={{0,64},{64,128},{96,32},{128,192},{160,96},{224,160},{1,65},{65,12... | collective-permute-start | bytes 1179656 | tf_op jit(solution)/shard_map/ppermute | solution.py:249
  20.7 1.9 %collective-permute-start.5 = (bf16[1,10,128,128]{3,2,1,0:T(8,128)(2,1)S(1)}, bf16[1,10,128,128]{3,2,1,0:T(8,128)(2,1)S(1)}, u32[]{:S(2)}, u32[]{:S(2)}) collective-permute-start(bf16[1,10,128,128]{3,2,1,0:T(8,128)(2,1)S(1)} %constant_dynamic-slice_fusion.2), channel_id=1, source_target_pairs={{33,66},{34,65},{35,68},{36,67},{37,70},{38,69},{39,72},{40,71},{4... | collective-permute-start | bytes 983048 | tf_op jit(solution)/shard_map/ppermute | solution.py:252
  22.6 3.5 %collective-permute-done.3.far = bf16[1,12,128,128]{3,2,1,0:T(8,128)(2,1)S(1)} collective-permute-done((bf16[1,12,128,128]{3,2,1,0:T(8,128)(2,1)S(1)}, bf16[1,12,128,128]{3,2,1,0:T(8,128)(2,1)S(1)}, u32[]{:S(2)}, u32[]{:S(2)}) %collective-permute-start.3) | collective-permute-done | bytes 393248 | tf_op jit(solution)/shard_map/ppermute | solution.py:251
  26.1 0.0 collective-permute-done.4.pair_c
  26.1 0.6 %copy-done.3 = s32[8]{0:T(128)S(1)} copy-done((s32[8]{0:T(128)S(1)}, s32[8]{0:T(128)}, u32[]{:S(2)}) %copy-start.3) | copy-done | bytes 56
  26.8 0.0 copy-done.5
  26.8 0.0 copy-done.6
  26.8 3.7 %shard_map.82 = (f32[16,128,128]{2,1,0:T(8,128)S(1)}, bf16[18,128,128]{2,1,0:T(8,128)(2,1)S(1)}, bf16[3,3,128,128]{3,2,1,0:T(8,128)(2,1)S(1)}, f32[1,128]{1,0:T(1,128)S(1)}) custom-call(s32[8]{0:T(128)S(1)} %copy-done.3, bf16[1,12,128,128]{3,2,1,0:T(8,128)(2,1)S(1)} %copy-done, bf16[1,12,128,128]{3,2,1,0:T(8,128)(2,1)S(1)} %collective-permute-done.3.far, ...), custom_call_target="tpu_custom_call" | custom-call | flops 679477248 | bytes 3276800 | tf_op jit(solution)/shard_map/pallas_call | solution.py:191
  30.5 0.7 %collective-permute-done.2.outer = bf16[1,12,128,128]{3,2,1,0:T(8,128)(2,1)S(1)} collective-permute-done((bf16[1,12,128,128]{3,2,1,0:T(8,128)(2,1)S(1)}, bf16[1,12,128,128]{3,2,1,0:T(8,128)(2,1)S(1)}, u32[]{:S(2)}, u32[]{:S(2)}) %collective-permute-start.2) | collective-permute-done | bytes 393248 | tf_op jit(solution)/shard_map/ppermute | solution.py:249
  31.2 0.1 collective-permute-start.6
  31.3 3.4 %collective-permute-done.5.outer_x = bf16[1,10,128,128]{3,2,1,0:T(8,128)(2,1)S(1)} collective-permute-done((bf16[1,10,128,128]{3,2,1,0:T(8,128)(2,1)S(1)}, bf16[1,10,128,128]{3,2,1,0:T(8,128)(2,1)S(1)}, u32[]{:S(2)}, u32[]{:S(2)}) %collective-permute-start.5) | collective-permute-done | bytes 327712 | tf_op jit(solution)/shard_map/ppermute | solution.py:252
  34.7 0.0 collective-permute-done.6.outer_c
  34.7 4.9 %shard_map.83 = f32[2,12,1,128]{3,2,1,0:T(1,128)} custom-call(s32[8]{0:T(128)S(1)} %copy-done.3, f32[16,128,128]{2,1,0:T(8,128)S(1)} %get-tuple-element.20.part_ref, bf16[18,128,128]{2,1,0:T(8,128)(2,1)S(1)} %get-tuple-element.21.own_buf, bf16[1,12,128,128]{3,2,1,0:T(8,128)(2,1)S(1)} %collective-permute-done.2.outer, ...), custom_call_target="tpu_custom_call" | custom-call | tf_op jit(solution)/shard_map/pallas_call | solution.py:210
  (16 shorter events, 0.1 us)
Async XLA Ops:
  0.0 12.6 %collective-permute-start = (bf16[1,12,128,128]{3,2,1,0:T(8,128)(2,1)}, bf16[1,12,128,128]{3,2,1,0:T(8,128)(2,1)S(1)}, u32[]{:S(2)}, u32[]{:S(2)}) collective-permute-start(bf16[1,12,128,128]{3,2,1,0:T(8,128)(2,1)} %own.1), channel_id=1, source_target_pairs={{0,32},{32,0},{64,96},{96,64},{128,160},{160,128},{192,224},{224,1... | collective-permute-start | bytes 1179656 | tf_op jit(solution)/shard_map/ppermute | solution.py:243
  1.2 11.3 %collective-permute-start.1 = (bf16[1,12,128,128]{3,2,1,0:T(8,128)(2,1)}, bf16[1,12,128,128]{3,2,1,0:T(8,128)(2,1)S(1)}, u32[]{:S(2)}, u32[]{:S(2)}) collective-permute-start(bf16[1,12,128,128]{3,2,1,0:T(8,128)(2,1)} %own.1), channel_id=1, source_target_pairs={{0,1},{1,0},{2,3},{3,2},{4,5},{5,4},{6,7},{7,6},{8,9},{9,8},{10,11... | collective-permute-start | bytes 1179656 | tf_op jit(solution)/shard_map/ppermute | solution.py:244
  1.2 0.7 %copy-start.7 = (bf16[3,3,128,2]{2,3,1,0:T(2,128)(2,1)S(1)}, bf16[3,3,128,2]{2,3,1,0:T(2,128)(2,1)}, u32[]{:S(2)}) copy-start(bf16[3,3,128,2]{2,3,1,0:T(2,128)(2,1)} %param.15) | copy-start | bytes 13828
  12.6 13.5 %copy-start = (bf16[1,12,128,128]{3,2,1,0:T(8,128)(2,1)S(1)}, bf16[1,12,128,128]{3,2,1,0:T(8,128)(2,1)}, u32[]{:S(2)}) copy-start(bf16[1,12,128,128]{3,2,1,0:T(8,128)(2,1)} %own.1) | copy-start | bytes 1179652
  12.6 13.5 %copy-start.4 = (bf16[3,3,162,128]{3,2,1,0:T(8,128)(2,1)S(1)}, bf16[3,3,162,128]{3,2,1,0:T(8,128)(2,1)}, u32[]{:S(2)}) copy-start(bf16[3,3,162,128]{3,2,1,0:T(8,128)(2,1)} %w_ref.1) | copy-start | bytes 1119748
  12.7 13.4 %collective-permute-start.3 = (bf16[1,12,128,128]{3,2,1,0:T(8,128)(2,1)S(1)}, bf16[1,12,128,128]{3,2,1,0:T(8,128)(2,1)S(1)}, u32[]{:S(2)}, u32[]{:S(2)}) collective-permute-start(bf16[1,12,128,128]{3,2,1,0:T(8,128)(2,1)S(1)} %pad_maximum_fusion), channel_id=1, source_target_pairs={{1,2},{2,1},{3,4},{4,3},{5,6},{6,5},{7,8},{8,7},{9,10},{10,9},{11,... | collective-permute-start | bytes 1179656 | tf_op jit(solution)/shard_map/ppermute | solution.py:251
  14.7 11.4 %collective-permute-start.4 = (bf16[1,12,128,128]{3,2,1,0:T(8,128)(2,1)S(1)}, bf16[1,12,128,128]{3,2,1,0:T(8,128)(2,1)S(1)}, u32[]{:S(2)}, u32[]{:S(2)}) collective-permute-start(bf16[1,12,128,128]{3,2,1,0:T(8,128)(2,1)S(1)} %collective-permute-done.pair), channel_id=1, source_target_pairs={{0,1},{1,0},{2,3},{3,2},{4,5},{5,4},{6,7},{7,6},{8,9},{9,8},{10,11... | collective-permute-start | bytes 1179656 | tf_op jit(solution)/shard_map/ppermute | solution.py:253
  18.2 12.9 %collective-permute-start.2 = (bf16[1,12,128,128]{3,2,1,0:T(8,128)(2,1)S(1)}, bf16[1,12,128,128]{3,2,1,0:T(8,128)(2,1)S(1)}, u32[]{:S(2)}, u32[]{:S(2)}) collective-permute-start(bf16[1,12,128,128]{3,2,1,0:T(8,128)(2,1)S(1)} %collective-permute-done.pair), channel_id=1, source_target_pairs={{0,64},{64,128},{96,32},{128,192},{160,96},{224,160},{1,65},{65,12... | collective-permute-start | bytes 1179656 | tf_op jit(solution)/shard_map/ppermute | solution.py:249
  20.7 14.0 %collective-permute-start.5 = (bf16[1,10,128,128]{3,2,1,0:T(8,128)(2,1)S(1)}, bf16[1,10,128,128]{3,2,1,0:T(8,128)(2,1)S(1)}, u32[]{:S(2)}, u32[]{:S(2)}) collective-permute-start(bf16[1,10,128,128]{3,2,1,0:T(8,128)(2,1)S(1)} %constant_dynamic-slice_fusion.2), channel_id=1, source_target_pairs={{33,66},{34,65},{35,68},{36,67},{37,70},{38,69},{39,72},{40,71},{4... | collective-permute-start | bytes 983048 | tf_op jit(solution)/shard_map/ppermute | solution.py:252
  26.1 0.7 %copy-start.3 = (s32[8]{0:T(128)S(1)}, s32[8]{0:T(128)}, u32[]{:S(2)}) copy-start(s32[8]{0:T(128)} %off_ref.3) | copy-start | bytes 100
  26.1 0.7 %copy-start.5 = (f32[128]{0:T(128)S(1)}, f32[128]{0:T(128)}, u32[]{:S(2)}) copy-start(f32[128]{0:T(128)} %param.12) | copy-start | bytes 1540
  26.1 0.7 %copy-start.6 = (f32[128]{0:T(128)S(1)}, f32[128]{0:T(128)}, u32[]{:S(2)}) copy-start(f32[128]{0:T(128)} %param.14) | copy-start | bytes 1540
  31.2 3.5 %copy-start.1 = (bf16[3,3,128,128]{3,2,1,0:T(8,128)(2,1)S(1)}, bf16[3,3,128,128]{3,2,1,0:T(8,128)(2,1)}, u32[]{:S(2)}) copy-start(bf16[3,3,128,128]{3,2,1,0:T(8,128)(2,1)} %w2_ref.1) | copy-start | bytes 884740
  31.2 3.5 %copy-start.2 = (f32[2,1,12,128]{3,1,2,0:T(1,128)S(1)}, f32[2,1,12,128]{3,1,2,0:T(1,128)}, u32[]{:S(2)}) copy-start(f32[2,1,12,128]{3,1,2,0:T(1,128)} %param.10) | copy-start | bytes 36868
  31.2 3.5 %collective-permute-start.6 = (bf16[1,9,128,128]{3,2,1,0:T(8,128)(2,1)S(1)}, bf16[1,9,128,128]{3,2,1,0:T(8,128)(2,1)S(1)}, u32[]{:S(2)}, u32[]{:S(2)}) collective-permute-start(bf16[1,9,128,128]{3,2,1,0:T(8,128)(2,1)S(1)} %constant_dynamic-slice_fusion), channel_id=1, source_target_pairs={{0,1},{1,0},{2,3},{3,2},{4,5},{5,4},{6,7},{7,6},{8,9},{9,8},{10,11... | collective-permute-start | bytes 884744 | tf_op jit(solution)/shard_map/ppermute | solution.py:259

commit v5 on v4

--- a/solution.py
+++ b/solution.py
@@ -116,7 +116,7 @@
     for r in range(STRIP):
         own_buf[3 + r] = own[0, r]
     shift = jnp.where(parity == 0, above, below)
-    turned(nrot_ref, pair, far, pair_c, core, shift, 3, 3, 3)
+    turned(nrot_ref, pair, far, pair_c, core, shift, 3, 3, 0)
     corr_rows(own_buf, corr_ref, nrot_ref, acc_ref, acc8_ref)
     b2_out[...] = b2_ref[...]
     kernel_blocks = blocks_of(w_pair)
@@ -134,7 +134,7 @@
         held.start()
         core, parity, top, above, below = position(off_ref)
         shift = jnp.where(parity == 0, below, above)
-        turned(nrot_ref, outer, outer_x, outer_c, core, shift, 1, 0, 0)
+        turned(nrot_ref, outer, outer_x, outer_c, core, shift, 0, 0, 0)
         corr_rows(own_buf, corr_ref, nrot_ref, acc_ref, acc8_ref)
         first = blocks_of(w1_ref)
         second = blocks_of(w2_ref)
@@ -243,14 +243,16 @@
         pair = lax.ppermute(features, "sec", pair_swap)
         own_c = lax.ppermute(features, "strip", core_swap)
         rim = lax.dynamic_slice_in_dim(features, 9 * core, 3, 1)
-        edge = lax.dynamic_slice_in_dim(features, 2 * core, HALO + 1, 1)
+        edge = lax.dynamic_slice_in_dim(features, 3 * core, HALO, 1)
         third = arranged(w_third)
         pair, own_c, rim, edge, third = lax.optimization_barrier((pair, own_c, rim, edge, third))
         outer = lax.ppermute(pair, "sec", onward)
         far = jnp.concatenate([rim, lax.dynamic_slice_in_dim(pair, 3 * core, HALO, 1)], 1)
         far = lax.ppermute(far, "strip", chip_swap)
         outer_x = lax.ppermute(edge, both, next_chip)
-        pair_c = lax.ppermute(pair, "strip", core_swap)
+        pair_c = lax.ppermute(
+            lax.dynamic_slice_in_dim(pair, 3 * (1 - core), HALO, 1), "strip", core_swap
+        )
         part, own_all, first, bias = pair_part(
             offsets, (features, far, own_c, pair, pair_c), w_first, b_first[None], b_second[None]
         )

time: 39.9 us -> 38.9 us (0.975)
  waiting for transfers between devices: 16.3 us -> 15.5 us
    ppermute x1, waiting for transfers between devices: 0.66 us -> 0.01 us  [body(): outer = lax.ppermute(pair, 'sec', onward)]
  transfers between devices with their start and end apart: 7 -> 7, of which waited for: 4 -> 3; matrix products, arithmetic and copies ran while one was open for 5% -> 5% of each run, Pallas kernels for 9% -> 10%
where the time goes in v5:
time: 38.9 us; the launch traced here: 38.7 us
  waiting for transfers between devices  15.5 us (40%)
  starting transfers between devices  11 us (28%)
  Pallas kernels  8.65 us (22%)
  local copies, waits for them, and re-layouts  3.37 us (9%)
    ppermute x1, waiting for transfers between devices, body(): pair = lax.ppermute(features, 'sec', pair_swap)  8.7 us
    pallas_call x1, Pallas kernels, align(): pl.pallas_call(make_kernel(total_rows), out_shape=jax.ShapeDtypeStruct((2...  4.95 us
    ppermute x1, waiting for transfers between devices, body(): far = lax.ppermute(far, 'strip', chip_swap)  3.78 us
    pallas_call x1, Pallas kernels, pair_part(): pl.pallas_call(pair_kernel, out_shape=(jax.ShapeDtypeStruct((16, LANES, C...  3.7 us
    ppermute x1, starting transfers between devices, body(): lax.ppermute(lax.dynamic_slice_in_dim(pair, 3 * (1 - core), HALO, 1), 'st...  3.22 us
    ppermute x1, waiting for transfers between devices, body(): outer_x = lax.ppermute(edge, both, next_chip)  3.02 us
    ppermute x1, starting transfers between devices, body(): outer = lax.ppermute(pair, 'sec', onward)  2.44 us
    ppermute x1, starting transfers between devices, body(): far = lax.ppermute(far, 'strip', chip_swap)  2.05 us
  transfers between devices with their start and end apart: 7, of which 3 were waited for; matrix products, arithmetic and copies ran while one was open for 5% of the time, Pallas kernels for 10%

profile of v5, /device:TPU:122, one launch (start us, length us, event | category | flops | bytes accessed | tf_op | source)
XLA Modules:
  0.0 38.7 jit_solution(16451214359636564229)
XLA Ops:
  0.0 1.2 %collective-permute-start = (bf16[1,12,128,128]{3,2,1,0:T(8,128)(2,1)}, bf16[1,12,128,128]{3,2,1,0:T(8,128)(2,1)S(1)}, u32[]{:S(2)}, u32[]{:S(2)}) collective-permute-start(bf16[1,12,128,128]{3,2,1,0:T(8,128)(2,1)} %own.1), channel_id=1, source_target_pairs={{0,32},{32,0},{64,96},{96,64},{128,160},{160,128},{192,224},{224,1... | collective-permute-start | bytes 1179656 | tf_op jit(solution)/shard_map/ppermute | solution.py:243
  1.2 0.0 collective-permute-start.1
  1.2 0.7 %copy-done.7 = bf16[3,3,128,2]{2,3,1,0:T(2,128)(2,1)S(1)} copy-done((bf16[3,3,128,2]{2,3,1,0:T(2,128)(2,1)S(1)}, bf16[3,3,128,2]{2,3,1,0:T(2,128)(2,1)}, u32[]{:S(2)}) %copy-start.7) | copy-done | bytes 4632
  2.0 0.9 %constant_dynamic-slice_fusion.4 = bf16[1,3,128,128]{3,2,1,0:T(8,128)(2,1)S(1)} fusion(bf16[1,12,128,128]{3,2,1,0:T(8,128)(2,1)} %own.1, s32[]{:T(128)S(6)} %select_n.11), kind=kLoop, calls=%fused_computation.6 | loop fusion | bytes 196612 | tf_op jit(solution)/shard_map/dynamic_slice | solution.py:245
  2.9 1.0 %constant_dynamic-slice_fusion.3 = bf16[1,9,128,128]{3,2,1,0:T(8,128)(2,1)S(1)} fusion(bf16[1,12,128,128]{3,2,1,0:T(8,128)(2,1)} %own.1, s32[]{:T(128)S(6)} %select_n.12), kind=kLoop, calls=%fused_computation.5 | loop fusion | bytes 589828 | tf_op jit(solution)/shard_map/dynamic_slice | solution.py:246
  3.9 8.7 %collective-permute-done.pair = bf16[1,12,128,128]{3,2,1,0:T(8,128)(2,1)S(1)} collective-permute-done((bf16[1,12,128,128]{3,2,1,0:T(8,128)(2,1)}, bf16[1,12,128,128]{3,2,1,0:T(8,128)(2,1)S(1)}, u32[]{:S(2)}, u32[]{:S(2)}) %collective-permute-start) | collective-permute-done | bytes 393248 | tf_op jit(solution)/shard_map/ppermute | solution.py:243
  12.6 0.0 copy-start
  12.6 0.0 copy-start.4
  12.7 2.1 %collective-permute-start.3 = (bf16[1,12,128,128]{3,2,1,0:T(8,128)(2,1)S(1)}, bf16[1,12,128,128]{3,2,1,0:T(8,128)(2,1)S(1)}, u32[]{:S(2)}, u32[]{:S(2)}) collective-permute-start(bf16[1,12,128,128]{3,2,1,0:T(8,128)(2,1)S(1)} %pad_maximum_fusion), channel_id=1, source_target_pairs={{1,2},{2,1},{3,4},{4,3},{5,6},{6,5},{7,8},{8,7},{9,10},{10,9},{11,... | collective-permute-start | bytes 1179656 | tf_op jit(solution)/shard_map/ppermute | solution.py:251
  14.7 2.4 %collective-permute-start.2 = (bf16[1,12,128,128]{3,2,1,0:T(8,128)(2,1)S(1)}, bf16[1,12,128,128]{3,2,1,0:T(8,128)(2,1)S(1)}, u32[]{:S(2)}, u32[]{:S(2)}) collective-permute-start(bf16[1,12,128,128]{3,2,1,0:T(8,128)(2,1)S(1)} %collective-permute-done.pair), channel_id=1, source_target_pairs={{0,64},{64,128},{96,32},{128,192},{160,96},{224,160},{1,65},{65,12... | collective-permute-start | bytes 1179656 | tf_op jit(solution)/shard_map/ppermute | solution.py:249
  17.2 3.2 %collective-permute-start.4 = (bf16[1,9,128,128]{3,2,1,0:T(8,128)(2,1)S(1)}, bf16[1,9,128,128]{3,2,1,0:T(8,128)(2,1)S(1)}, u32[]{:S(2)}, u32[]{:S(2)}) collective-permute-start(bf16[1,9,128,128]{3,2,1,0:T(8,128)(2,1)S(1)} %get-tuple-element.27), channel_id=1, source_target_pairs={{0,1},{1,0},{2,3},{3,2},{4,5},{5,4},{6,7},{7,6},{8,9},{9,8},{10,11... | collective-permute-start | bytes 884744 | tf_op jit(solution)/shard_map/ppermute | solution.py:253
  20.4 1.9 %collective-permute-start.5 = (bf16[1,9,128,128]{3,2,1,0:T(8,128)(2,1)S(1)}, bf16[1,9,128,128]{3,2,1,0:T(8,128)(2,1)S(1)}, u32[]{:S(2)}, u32[]{:S(2)}) collective-permute-start(bf16[1,9,128,128]{3,2,1,0:T(8,128)(2,1)S(1)} %constant_dynamic-slice_fusion.3), channel_id=1, source_target_pairs={{33,66},{34,65},{35,68},{36,67},{37,70},{38,69},{39,72},{40,71},{4... | collective-permute-start | bytes 884744 | tf_op jit(solution)/shard_map/ppermute | solution.py:252
  22.3 0.0 collective-permute-done.4.pair_c
  22.3 3.8 %collective-permute-done.3.far = bf16[1,12,128,128]{3,2,1,0:T(8,128)(2,1)S(1)} collective-permute-done((bf16[1,12,128,128]{3,2,1,0:T(8,128)(2,1)S(1)}, bf16[1,12,128,128]{3,2,1,0:T(8,128)(2,1)S(1)}, u32[]{:S(2)}, u32[]{:S(2)}) %collective-permute-start.3) | collective-permute-done | bytes 393248 | tf_op jit(solution)/shard_map/ppermute | solution.py:251
  26.2 0.6 %copy-done.3 = s32[8]{0:T(128)S(1)} copy-done((s32[8]{0:T(128)S(1)}, s32[8]{0:T(128)}, u32[]{:S(2)}) %copy-start.3) | copy-done | bytes 56
  26.8 0.0 copy-done.5
  26.8 0.0 copy-done.6
  26.8 3.7 %shard_map.82 = (f32[16,128,128]{2,1,0:T(8,128)S(1)}, bf16[18,128,128]{2,1,0:T(8,128)(2,1)S(1)}, bf16[3,3,128,128]{3,2,1,0:T(8,128)(2,1)S(1)}, f32[1,128]{1,0:T(1,128)S(1)}) custom-call(s32[8]{0:T(128)S(1)} %copy-done.3, bf16[1,12,128,128]{3,2,1,0:T(8,128)(2,1)S(1)} %copy-done, bf16[1,12,128,128]{3,2,1,0:T(8,128)(2,1)S(1)} %collective-permute-done.3.far, ...), custom_call_target="tpu_custom_call" | custom-call | flops 679477248 | bytes 3276800 | tf_op jit(solution)/shard_map/pallas_call | solution.py:191
  30.5 0.0 collective-permute-done.2.outer
  30.5 0.0 copy-start.1
  30.5 0.0 copy-start.2
  30.6 0.1 collective-permute-start.6
  30.7 3.0 %collective-permute-done.5.outer_x = bf16[1,9,128,128]{3,2,1,0:T(8,128)(2,1)S(1)} collective-permute-done((bf16[1,9,128,128]{3,2,1,0:T(8,128)(2,1)S(1)}, bf16[1,9,128,128]{3,2,1,0:T(8,128)(2,1)S(1)}, u32[]{:S(2)}, u32[]{:S(2)}) %collective-permute-start.5) | collective-permute-done | bytes 294944 | tf_op jit(solution)/shard_map/ppermute | solution.py:252
  33.7 4.9 %shard_map.83 = f32[2,12,1,128]{3,2,1,0:T(1,128)} custom-call(s32[8]{0:T(128)S(1)} %copy-done.3, f32[16,128,128]{2,1,0:T(8,128)S(1)} %get-tuple-element.20.part_ref, bf16[18,128,128]{2,1,0:T(8,128)(2,1)S(1)} %get-tuple-element.21.own_buf, bf16[1,12,128,128]{3,2,1,0:T(8,128)(2,1)S(1)} %collective-permute-done.2.outer, ...), custom_call_target="tpu_custom_call" | custom-call | tf_op jit(solution)/shard_map/pallas_call | solution.py:210
  (16 shorter events, 0.2 us)
Async XLA Ops:
  0.0 12.6 %collective-permute-start = (bf16[1,12,128,128]{3,2,1,0:T(8,128)(2,1)}, bf16[1,12,128,128]{3,2,1,0:T(8,128)(2,1)S(1)}, u32[]{:S(2)}, u32[]{:S(2)}) collective-permute-start(bf16[1,12,128,128]{3,2,1,0:T(8,128)(2,1)} %own.1), channel_id=1, source_target_pairs={{0,32},{32,0},{64,96},{96,64},{128,160},{160,128},{192,224},{224,1... | collective-permute-start | bytes 1179656 | tf_op jit(solution)/shard_map/ppermute | solution.py:243
  1.2 11.3 %collective-permute-start.1 = (bf16[1,12,128,128]{3,2,1,0:T(8,128)(2,1)}, bf16[1,12,128,128]{3,2,1,0:T(8,128)(2,1)S(1)}, u32[]{:S(2)}, u32[]{:S(2)}) collective-permute-start(bf16[1,12,128,128]{3,2,1,0:T(8,128)(2,1)} %own.1), channel_id=1, source_target_pairs={{0,1},{1,0},{2,3},{3,2},{4,5},{5,4},{6,7},{7,6},{8,9},{9,8},{10,11... | collective-permute-start | bytes 1179656 | tf_op jit(solution)/shard_map/ppermute | solution.py:244
  1.2 0.7 %copy-start.7 = (bf16[3,3,128,2]{2,3,1,0:T(2,128)(2,1)S(1)}, bf16[3,3,128,2]{2,3,1,0:T(2,128)(2,1)}, u32[]{:S(2)}) copy-start(bf16[3,3,128,2]{2,3,1,0:T(2,128)(2,1)} %param.15) | copy-start | bytes 13828
  12.6 13.5 %copy-start = (bf16[1,12,128,128]{3,2,1,0:T(8,128)(2,1)S(1)}, bf16[1,12,128,128]{3,2,1,0:T(8,128)(2,1)}, u32[]{:S(2)}) copy-start(bf16[1,12,128,128]{3,2,1,0:T(8,128)(2,1)} %own.1) | copy-start | bytes 1179652
  12.6 13.5 %copy-start.4 = (bf16[3,3,162,128]{3,2,1,0:T(8,128)(2,1)S(1)}, bf16[3,3,162,128]{3,2,1,0:T(8,128)(2,1)}, u32[]{:S(2)}) copy-start(bf16[3,3,162,128]{3,2,1,0:T(8,128)(2,1)} %w_ref.1) | copy-start | bytes 1119748
  12.7 13.4 %collective-permute-start.3 = (bf16[1,12,128,128]{3,2,1,0:T(8,128)(2,1)S(1)}, bf16[1,12,128,128]{3,2,1,0:T(8,128)(2,1)S(1)}, u32[]{:S(2)}, u32[]{:S(2)}) collective-permute-start(bf16[1,12,128,128]{3,2,1,0:T(8,128)(2,1)S(1)} %pad_maximum_fusion), channel_id=1, source_target_pairs={{1,2},{2,1},{3,4},{4,3},{5,6},{6,5},{7,8},{8,7},{9,10},{10,9},{11,... | collective-permute-start | bytes 1179656 | tf_op jit(solution)/shard_map/ppermute | solution.py:251
  14.7 15.8 %collective-permute-start.2 = (bf16[1,12,128,128]{3,2,1,0:T(8,128)(2,1)S(1)}, bf16[1,12,128,128]{3,2,1,0:T(8,128)(2,1)S(1)}, u32[]{:S(2)}, u32[]{:S(2)}) collective-permute-start(bf16[1,12,128,128]{3,2,1,0:T(8,128)(2,1)S(1)} %collective-permute-done.pair), channel_id=1, source_target_pairs={{0,64},{64,128},{96,32},{128,192},{160,96},{224,160},{1,65},{65,12... | collective-permute-start | bytes 1179656 | tf_op jit(solution)/shard_map/ppermute | solution.py:249
  17.2 5.1 %collective-permute-start.4 = (bf16[1,9,128,128]{3,2,1,0:T(8,128)(2,1)S(1)}, bf16[1,9,128,128]{3,2,1,0:T(8,128)(2,1)S(1)}, u32[]{:S(2)}, u32[]{:S(2)}) collective-permute-start(bf16[1,9,128,128]{3,2,1,0:T(8,128)(2,1)S(1)} %get-tuple-element.27), channel_id=1, source_target_pairs={{0,1},{1,0},{2,3},{3,2},{4,5},{5,4},{6,7},{7,6},{8,9},{9,8},{10,11... | collective-permute-start | bytes 884744 | tf_op jit(solution)/shard_map/ppermute | solution.py:253
  20.4 13.3 %collective-permute-start.5 = (bf16[1,9,128,128]{3,2,1,0:T(8,128)(2,1)S(1)}, bf16[1,9,128,128]{3,2,1,0:T(8,128)(2,1)S(1)}, u32[]{:S(2)}, u32[]{:S(2)}) collective-permute-start(bf16[1,9,128,128]{3,2,1,0:T(8,128)(2,1)S(1)} %constant_dynamic-slice_fusion.3), channel_id=1, source_target_pairs={{33,66},{34,65},{35,68},{36,67},{37,70},{38,69},{39,72},{40,71},{4... | collective-permute-start | bytes 884744 | tf_op jit(solution)/shard_map/ppermute | solution.py:252
  26.1 0.7 %copy-start.3 = (s32[8]{0:T(128)S(1)}, s32[8]{0:T(128)}, u32[]{:S(2)}) copy-start(s32[8]{0:T(128)} %off_ref.3) | copy-start | bytes 100
  26.1 0.7 %copy-start.5 = (f32[128]{0:T(128)S(1)}, f32[128]{0:T(128)}, u32[]{:S(2)}) copy-start(f32[128]{0:T(128)} %param.12) | copy-start | bytes 1540
  26.1 0.7 %copy-start.6 = (f32[128]{0:T(128)S(1)}, f32[128]{0:T(128)}, u32[]{:S(2)}) copy-start(f32[128]{0:T(128)} %param.14) | copy-start | bytes 1540
  30.5 3.2 %copy-start.1 = (bf16[3,3,128,128]{3,2,1,0:T(8,128)(2,1)S(1)}, bf16[3,3,128,128]{3,2,1,0:T(8,128)(2,1)}, u32[]{:S(2)}) copy-start(bf16[3,3,128,128]{3,2,1,0:T(8,128)(2,1)} %w2_ref.1) | copy-start | bytes 884740
  30.5 3.2 %copy-start.2 = (f32[2,1,12,128]{3,1,2,0:T(1,128)S(1)}, f32[2,1,12,128]{3,1,2,0:T(1,128)}, u32[]{:S(2)}) copy-start(f32[2,1,12,128]{3,1,2,0:T(1,128)} %param.10) | copy-start | bytes 36868
  30.6 3.1 %collective-permute-start.6 = (bf16[1,9,128,128]{3,2,1,0:T(8,128)(2,1)S(1)}, bf16[1,9,128,128]{3,2,1,0:T(8,128)(2,1)S(1)}, u32[]{:S(2)}, u32[]{:S(2)}) collective-permute-start(bf16[1,9,128,128]{3,2,1,0:T(8,128)(2,1)S(1)} %constant_dynamic-slice_fusion), channel_id=1, source_target_pairs={{0,1},{1,0},{2,3},{3,2},{4,5},{5,4},{6,7},{7,6},{8,9},{9,8},{10,11... | collective-permute-start | bytes 884744 | tf_op jit(solution)/shard_map/ppermute | solution.py:261

commit v6 on v5

--- a/solution.py
+++ b/solution.py
@@ -98,7 +98,7 @@
 
 
 def pair_kernel(
-    off_ref, own, far, own_c, pair, pair_c, w_ref, b1_ref, b2_ref, part_ref, own_buf, w_outer, b2_out,
+    off_ref, own, far, own_c, pair, pair_c, w_ref, bias_ref, part_ref, own_buf, w_outer, bias_out,
     nrot_ref, acc_ref, acc8_ref, corr_ref, w_pair, halves,
 ):
     core, parity, top, above, below = position(off_ref)
@@ -118,11 +118,11 @@
     shift = jnp.where(parity == 0, above, below)
     turned(nrot_ref, pair, far, pair_c, core, shift, 3, 3, 0)
     corr_rows(own_buf, corr_ref, nrot_ref, acc_ref, acc8_ref)
-    b2_out[...] = b2_ref[...]
+    bias_out[...] = bias_ref[1:2]
     kernel_blocks = blocks_of(w_pair)
     for m in range(0, 16, 2):
         for side, value in enumerate(convolved(corr_ref, kernel_blocks, m)):
-            part_ref[m + side] = value + b1_ref[...]
+            part_ref[m + side] = value + bias_ref[0:1]
 
 
 def make_kernel(total_rows):
@@ -187,7 +187,7 @@
 TAPS = pltpu.VMEM((3, 3, LANES, C), jnp.bfloat16)
 
 
-def pair_part(offsets, blocks, w_first, b_first, b_second):
+def pair_part(offsets, blocks, w_first, biases):
     return pl.pallas_call(
         pair_kernel,
         out_shape=(
@@ -196,14 +196,14 @@
             jax.ShapeDtypeStruct((3, 3, LANES, C), jnp.bfloat16),
             jax.ShapeDtypeStruct((1, C), jnp.float32),
         ),
-        in_specs=[SMEM] + [VMEM] * 8,
+        in_specs=[SMEM] + [VMEM] * 7,
         out_specs=(VMEM, VMEM, VMEM, VMEM),
         scratch_shapes=CORR + [TAPS, pltpu.VMEM((2, LANES, C), jnp.bfloat16)],
         compiler_params=PARAMS,
         cost_estimate=pl.CostEstimate(
             flops=2 * 18 * 9 * LANES * LANES * C, bytes_accessed=100 * LANES * C * 2, transcendentals=0
         ),
-    )(offsets, *blocks, w_first, b_first, b_second)
+    )(offsets, *blocks, w_first, biases)
 
 
 def align(offsets, part, own, blocks, weights, b_second, state, total_rows):
@@ -245,7 +245,11 @@
         rim = lax.dynamic_slice_in_dim(features, 9 * core, 3, 1)
         edge = lax.dynamic_slice_in_dim(features, 3 * core, HALO, 1)
         third = arranged(w_third)
-        pair, own_c, rim, edge, third = lax.optimization_barrier((pair, own_c, rim, edge, third))
+        offsets = jnp.clip(offsets, -2, 2)
+        biases = jnp.stack([b_first, b_second])
+        pair, own_c, rim, edge, third, offsets, biases = lax.optimization_barrier(
+            (pair, own_c, rim, edge, third, offsets, biases)
+        )
         outer = lax.ppermute(pair, "sec", onward)
         far = jnp.concatenate([rim, lax.dynamic_slice_in_dim(pair, 3 * core, HALO, 1)], 1)
         far = lax.ppermute(far, "strip", chip_swap)
@@ -254,7 +258,7 @@
             lax.dynamic_slice_in_dim(pair, 3 * (1 - core), HALO, 1), "strip", core_swap
         )
         part, own_all, first, bias = pair_part(
-            offsets, (features, far, own_c, pair, pair_c), w_first, b_first[None], b_second[None]
+            offsets, (features, far, own_c, pair, pair_c), w_first, biases
         )
         outer, part = lax.optimization_barrier((outer, part))
         near = lax.dynamic_slice_in_dim(outer, 3 * (1 - core), HALO, 1)

time: 38.9 us -> 38.9 us (level)
  local copies, waits for them, and re-layouts: 3.37 us -> 2.71 us
  waiting for transfers between devices: 15.5 us -> 16.1 us
    unnamed x16, local copies, waits for them, and re-layouts: 1.38 us -> 0.69 us
    ppermute x1, waiting for transfers between devices: 3.02 us -> 3.7 us  [body(): outer_x = lax.ppermute(edge, both, next_chip)]
where the time goes in v6:
time: 38.9 us; the launch traced here: 38.7 us
  waiting for transfers between devices  16.1 us (41%)
  starting transfers between devices  11 us (28%)
  Pallas kernels  8.65 us (22%)
  local copies, waits for them, and re-layouts  2.71 us (7%)
    ppermute x1, waiting for transfers between devices, body(): pair = lax.ppermute(features, 'sec', pair_swap)  8.64 us
    pallas_call x1, Pallas kernels, align(): pl.pallas_call(make_kernel(total_rows), out_shape=jax.ShapeDtypeStruct((2...  4.94 us
    ppermute x1, waiting for transfers between devices, body(): far = lax.ppermute(far, 'strip', chip_swap)  3.78 us
    pallas_call x1, Pallas kernels, pair_part(): pl.pallas_call(pair_kernel, out_shape=(jax.ShapeDtypeStruct((16, LANES, C...  3.7 us
    ppermute x1, waiting for transfers between devices, body(): outer_x = lax.ppermute(edge, both, next_chip)  3.7 us
    ppermute x1, starting transfers between devices, body(): lax.ppermute(lax.dynamic_slice_in_dim(pair, 3 * (1 - core), HALO, 1), 'st...  3.22 us
    ppermute x1, starting transfers between devices, body(): outer = lax.ppermute(pair, 'sec', onward)  2.44 us
    ppermute x1, starting transfers between devices, body(): far = lax.ppermute(far, 'strip', chip_swap)  2.05 us
  transfers between devices with their start and end apart: 7, of which 3 were waited for; matrix products, arithmetic and copies ran while one was open for 5% of the time, Pallas kernels for 10%

profile of v6, /device:TPU:122, one launch (start us, length us, event | category | flops | bytes accessed | tf_op | source)
XLA Modules:
  0.0 38.7 jit_solution(15007271810232636251)
XLA Ops:
  0.0 1.2 %collective-permute-start = (bf16[1,12,128,128]{3,2,1,0:T(8,128)(2,1)}, bf16[1,12,128,128]{3,2,1,0:T(8,128)(2,1)S(1)}, u32[]{:S(2)}, u32[]{:S(2)}) collective-permute-start(bf16[1,12,128,128]{3,2,1,0:T(8,128)(2,1)} %own.1), channel_id=1, source_target_pairs={{0,32},{32,0},{64,96},{96,64},{128,160},{160,128},{192,224},{224,1... | collective-permute-start | bytes 1179656 | tf_op jit(solution)/shard_map/ppermute | solution.py:243
  1.2 0.0 collective-permute-start.1
  1.2 0.9 %constant_dynamic-slice_fusion.4 = bf16[1,3,128,128]{3,2,1,0:T(8,128)(2,1)S(1)} fusion(bf16[1,12,128,128]{3,2,1,0:T(8,128)(2,1)} %own.1, s32[]{:T(128)S(6)} %select_n.11), kind=kLoop, calls=%fused_computation.6 | loop fusion | bytes 196612 | tf_op jit(solution)/shard_map/dynamic_slice | solution.py:245
  2.2 0.0 copy-start.5
  2.2 0.0 copy-start.6
  2.2 0.6 %copy-done.5 = f32[128]{0:T(128)S(1)} copy-done((f32[128]{0:T(128)S(1)}, f32[128]{0:T(128)}, u32[]{:S(2)}) %copy-start.5) | copy-done | bytes 536
  2.9 0.0 copy-done.6
  2.9 0.0 copy-start.7
  2.9 1.0 %constant_dynamic-slice_fusion.3 = bf16[1,9,128,128]{3,2,1,0:T(8,128)(2,1)S(1)} fusion(bf16[1,12,128,128]{3,2,1,0:T(8,128)(2,1)} %own.1, s32[]{:T(128)S(6)} %select_n.12), kind=kLoop, calls=%fused_computation.5 | loop fusion | bytes 589828 | tf_op jit(solution)/shard_map/dynamic_slice | solution.py:246
  3.9 8.6 %collective-permute-done.pair = bf16[1,12,128,128]{3,2,1,0:T(8,128)(2,1)S(1)} collective-permute-done((bf16[1,12,128,128]{3,2,1,0:T(8,128)(2,1)}, bf16[1,12,128,128]{3,2,1,0:T(8,128)(2,1)S(1)}, u32[]{:S(2)}, u32[]{:S(2)}) %collective-permute-start) | collective-permute-done | bytes 393248 | tf_op jit(solution)/shard_map/ppermute | solution.py:243
  12.6 0.0 collective-permute-done.1.own_c
  12.6 0.0 copy-start
  12.6 0.0 copy-start.3
  12.7 2.1 %collective-permute-start.3 = (bf16[1,12,128,128]{3,2,1,0:T(8,128)(2,1)S(1)}, bf16[1,12,128,128]{3,2,1,0:T(8,128)(2,1)S(1)}, u32[]{:S(2)}, u32[]{:S(2)}) collective-permute-start(bf16[1,12,128,128]{3,2,1,0:T(8,128)(2,1)S(1)} %pad_maximum_fusion), channel_id=1, source_target_pairs={{1,2},{2,1},{3,4},{4,3},{5,6},{6,5},{7,8},{8,7},{9,10},{10,9},{11,... | collective-permute-start | bytes 1179656 | tf_op jit(solution)/shard_map/ppermute | solution.py:255
  14.7 2.4 %collective-permute-start.2 = (bf16[1,12,128,128]{3,2,1,0:T(8,128)(2,1)S(1)}, bf16[1,12,128,128]{3,2,1,0:T(8,128)(2,1)S(1)}, u32[]{:S(2)}, u32[]{:S(2)}) collective-permute-start(bf16[1,12,128,128]{3,2,1,0:T(8,128)(2,1)S(1)} %collective-permute-done.pair), channel_id=1, source_target_pairs={{0,64},{64,128},{96,32},{128,192},{160,96},{224,160},{1,65},{65,12... | collective-permute-start | bytes 1179656 | tf_op jit(solution)/shard_map/ppermute | solution.py:253
  17.2 3.2 %collective-permute-start.4 = (bf16[1,9,128,128]{3,2,1,0:T(8,128)(2,1)S(1)}, bf16[1,9,128,128]{3,2,1,0:T(8,128)(2,1)S(1)}, u32[]{:S(2)}, u32[]{:S(2)}) collective-permute-start(bf16[1,9,128,128]{3,2,1,0:T(8,128)(2,1)S(1)} %get-tuple-element.31), channel_id=1, source_target_pairs={{0,1},{1,0},{2,3},{3,2},{4,5},{5,4},{6,7},{7,6},{8,9},{9,8},{10,11... | collective-permute-start | bytes 884744 | tf_op jit(solution)/shard_map/ppermute | solution.py:257
  20.4 1.9 %collective-permute-start.5 = (bf16[1,9,128,128]{3,2,1,0:T(8,128)(2,1)S(1)}, bf16[1,9,128,128]{3,2,1,0:T(8,128)(2,1)S(1)}, u32[]{:S(2)}, u32[]{:S(2)}) collective-permute-start(bf16[1,9,128,128]{3,2,1,0:T(8,128)(2,1)S(1)} %constant_dynamic-slice_fusion.3), channel_id=1, source_target_pairs={{33,66},{34,65},{35,68},{36,67},{37,70},{38,69},{39,72},{40,71},{4... | collective-permute-start | bytes 884744 | tf_op jit(solution)/shard_map/ppermute | solution.py:256
  22.3 3.8 %collective-permute-done.3.far = bf16[1,12,128,128]{3,2,1,0:T(8,128)(2,1)S(1)} collective-permute-done((bf16[1,12,128,128]{3,2,1,0:T(8,128)(2,1)S(1)}, bf16[1,12,128,128]{3,2,1,0:T(8,128)(2,1)S(1)}, u32[]{:S(2)}, u32[]{:S(2)}) %collective-permute-start.3) | collective-permute-done | bytes 393248 | tf_op jit(solution)/shard_map/ppermute | solution.py:255
  26.1 3.7 %shard_map.82 = (f32[16,128,128]{2,1,0:T(8,128)S(1)}, bf16[18,128,128]{2,1,0:T(8,128)(2,1)S(1)}, bf16[3,3,128,128]{3,2,1,0:T(8,128)(2,1)S(1)}, f32[1,128]{1,0:T(1,128)S(1)}) custom-call(s32[8]{0:T(128)S(1)} %broadcast_clamp_fusion.off_ref, bf16[1,12,128,128]{3,2,1,0:T(8,128)(2,1)S(1)} %copy-done, bf16[1,12,128,128]{3,2,1,0:T(8,128)(2,1)S(1)} %collective-permute-done.3.far, ...), custom_call_target="tpu_custom_call" | custom-call | flops 679477248 | bytes 3276800 | tf_op jit(solution)/shard_map/pallas_call | solution.py:191
  29.9 0.0 copy-start.1
  29.9 0.0 copy-start.2
  29.9 0.1 collective-permute-start.6
  30.0 3.7 %collective-permute-done.5.outer_x = bf16[1,9,128,128]{3,2,1,0:T(8,128)(2,1)S(1)} collective-permute-done((bf16[1,9,128,128]{3,2,1,0:T(8,128)(2,1)S(1)}, bf16[1,9,128,128]{3,2,1,0:T(8,128)(2,1)S(1)}, u32[]{:S(2)}, u32[]{:S(2)}) %collective-permute-start.5) | collective-permute-done | bytes 294944 | tf_op jit(solution)/shard_map/ppermute | solution.py:256
  33.7 4.9 %shard_map.83 = f32[2,12,1,128]{3,2,1,0:T(1,128)} custom-call(s32[8]{0:T(128)S(1)} %broadcast_clamp_fusion.off_ref, f32[16,128,128]{2,1,0:T(8,128)S(1)} %get-tuple-element.24.part_ref, bf16[18,128,128]{2,1,0:T(8,128)(2,1)S(1)} %get-tuple-element.25.own_buf, bf16[1,12,128,128]{3,2,1,0:T(8,128)(2,1)S(1)} %collective-permute-done.2.outer, ...), custom_call_target="tpu_custom_call" | custom-call | tf_op jit(solution)/shard_map/pallas_call | solution.py:210
  (18 shorter events, 0.2 us)
Async XLA Ops:
  0.0 12.6 %collective-permute-start = (bf16[1,12,128,128]{3,2,1,0:T(8,128)(2,1)}, bf16[1,12,128,128]{3,2,1,0:T(8,128)(2,1)S(1)}, u32[]{:S(2)}, u32[]{:S(2)}) collective-permute-start(bf16[1,12,128,128]{3,2,1,0:T(8,128)(2,1)} %own.1), channel_id=1, source_target_pairs={{0,32},{32,0},{64,96},{96,64},{128,160},{160,128},{192,224},{224,1... | collective-permute-start | bytes 1179656 | tf_op jit(solution)/shard_map/ppermute | solution.py:243
  1.2 11.3 %collective-permute-start.1 = (bf16[1,12,128,128]{3,2,1,0:T(8,128)(2,1)}, bf16[1,12,128,128]{3,2,1,0:T(8,128)(2,1)S(1)}, u32[]{:S(2)}, u32[]{:S(2)}) collective-permute-start(bf16[1,12,128,128]{3,2,1,0:T(8,128)(2,1)} %own.1), channel_id=1, source_target_pairs={{0,1},{1,0},{2,3},{3,2},{4,5},{5,4},{6,7},{7,6},{8,9},{9,8},{10,11... | collective-permute-start | bytes 1179656 | tf_op jit(solution)/shard_map/ppermute | solution.py:244
  1.2 0.9 %copy-start.4 = (bf16[3,3,128,2]{2,3,1,0:T(2,128)(2,1)S(1)}, bf16[3,3,128,2]{2,3,1,0:T(2,128)(2,1)}, u32[]{:S(2)}) copy-start(bf16[3,3,128,2]{2,3,1,0:T(2,128)(2,1)} %param.15) | copy-start | bytes 13828
  2.2 0.7 %copy-start.5 = (f32[128]{0:T(128)S(1)}, f32[128]{0:T(128)}, u32[]{:S(2)}) copy-start(f32[128]{0:T(128)} %param.14) | copy-start | bytes 1540
  2.2 0.7 %copy-start.6 = (f32[128]{0:T(128)S(1)}, f32[128]{0:T(128)}, u32[]{:S(2)}) copy-start(f32[128]{0:T(128)} %param.12) | copy-start | bytes 1540
  2.9 1.0 %copy-start.7 = (s32[8]{0:T(128)S(1)}, s32[8]{0:T(128)}, u32[]{:S(2)}) copy-start(s32[8]{0:T(128)} %param.9) | copy-start | bytes 100
  12.6 13.5 %copy-start = (bf16[1,12,128,128]{3,2,1,0:T(8,128)(2,1)S(1)}, bf16[1,12,128,128]{3,2,1,0:T(8,128)(2,1)}, u32[]{:S(2)}) copy-start(bf16[1,12,128,128]{3,2,1,0:T(8,128)(2,1)} %own.1) | copy-start | bytes 1179652
  12.6 13.5 %copy-start.3 = (bf16[3,3,162,128]{3,2,1,0:T(8,128)(2,1)S(1)}, bf16[3,3,162,128]{3,2,1,0:T(8,128)(2,1)}, u32[]{:S(2)}) copy-start(bf16[3,3,162,128]{3,2,1,0:T(8,128)(2,1)} %w_ref.1) | copy-start | bytes 1119748
  12.7 13.4 %collective-permute-start.3 = (bf16[1,12,128,128]{3,2,1,0:T(8,128)(2,1)S(1)}, bf16[1,12,128,128]{3,2,1,0:T(8,128)(2,1)S(1)}, u32[]{:S(2)}, u32[]{:S(2)}) collective-permute-start(bf16[1,12,128,128]{3,2,1,0:T(8,128)(2,1)S(1)} %pad_maximum_fusion), channel_id=1, source_target_pairs={{1,2},{2,1},{3,4},{4,3},{5,6},{6,5},{7,8},{8,7},{9,10},{10,9},{11,... | collective-permute-start | bytes 1179656 | tf_op jit(solution)/shard_map/ppermute | solution.py:255
  14.7 15.1 %collective-permute-start.2 = (bf16[1,12,128,128]{3,2,1,0:T(8,128)(2,1)S(1)}, bf16[1,12,128,128]{3,2,1,0:T(8,128)(2,1)S(1)}, u32[]{:S(2)}, u32[]{:S(2)}) collective-permute-start(bf16[1,12,128,128]{3,2,1,0:T(8,128)(2,1)S(1)} %collective-permute-done.pair), channel_id=1, source_target_pairs={{0,64},{64,128},{96,32},{128,192},{160,96},{224,160},{1,65},{65,12... | collective-permute-start | bytes 1179656 | tf_op jit(solution)/shard_map/ppermute | solution.py:253
  17.2 5.1 %collective-permute-start.4 = (bf16[1,9,128,128]{3,2,1,0:T(8,128)(2,1)S(1)}, bf16[1,9,128,128]{3,2,1,0:T(8,128)(2,1)S(1)}, u32[]{:S(2)}, u32[]{:S(2)}) collective-permute-start(bf16[1,9,128,128]{3,2,1,0:T(8,128)(2,1)S(1)} %get-tuple-element.31), channel_id=1, source_target_pairs={{0,1},{1,0},{2,3},{3,2},{4,5},{5,4},{6,7},{7,6},{8,9},{9,8},{10,11... | collective-permute-start | bytes 884744 | tf_op jit(solution)/shard_map/ppermute | solution.py:257
  20.4 13.3 %collective-permute-start.5 = (bf16[1,9,128,128]{3,2,1,0:T(8,128)(2,1)S(1)}, bf16[1,9,128,128]{3,2,1,0:T(8,128)(2,1)S(1)}, u32[]{:S(2)}, u32[]{:S(2)}) collective-permute-start(bf16[1,9,128,128]{3,2,1,0:T(8,128)(2,1)S(1)} %constant_dynamic-slice_fusion.3), channel_id=1, source_target_pairs={{33,66},{34,65},{35,68},{36,67},{37,70},{38,69},{39,72},{40,71},{4... | collective-permute-start | bytes 884744 | tf_op jit(solution)/shard_map/ppermute | solution.py:256
  29.9 3.9 %copy-start.1 = (bf16[3,3,128,128]{3,2,1,0:T(8,128)(2,1)S(1)}, bf16[3,3,128,128]{3,2,1,0:T(8,128)(2,1)}, u32[]{:S(2)}) copy-start(bf16[3,3,128,128]{3,2,1,0:T(8,128)(2,1)} %w2_ref.1) | copy-start | bytes 884740
  29.9 3.9 %copy-start.2 = (f32[2,1,12,128]{3,1,2,0:T(1,128)S(1)}, f32[2,1,12,128]{3,1,2,0:T(1,128)}, u32[]{:S(2)}) copy-start(f32[2,1,12,128]{3,1,2,0:T(1,128)} %param.10) | copy-start | bytes 36868
  29.9 3.8 %collective-permute-start.6 = (bf16[1,9,128,128]{3,2,1,0:T(8,128)(2,1)S(1)}, bf16[1,9,128,128]{3,2,1,0:T(8,128)(2,1)S(1)}, u32[]{:S(2)}, u32[]{:S(2)}) collective-permute-start(bf16[1,9,128,128]{3,2,1,0:T(8,128)(2,1)S(1)} %constant_dynamic-slice_fusion), channel_id=1, source_target_pairs={{0,1},{1,0},{2,3},{3,2},{4,5},{5,4},{6,7},{7,6},{8,9},{9,8},{10,11... | collective-permute-start | bytes 884744 | tf_op jit(solution)/shard_map/ppermute | solution.py:265

commit v7 on v6

--- a/solution.py
+++ b/solution.py
@@ -111,7 +111,7 @@
             w_pair[dy, dx] = halves[1 - parity]
             w_outer[dy, dx] = halves[parity]
     for r in range(3):
-        own_buf[r] = jnp.where(core == 0, far[0, r], own_c[0, 9 + r])
+        own_buf[r] = jnp.where(core == 0, far[0, r], own_c[0, r])
         own_buf[15 + r] = jnp.where(core == 0, own_c[0, r], far[0, r])
     for r in range(STRIP):
         own_buf[3 + r] = own[0, r]
@@ -241,7 +241,9 @@
     def body(features, offsets, state, w_first, b_first, w_second, b_second, w_third):
         core = lax.rem(lax.axis_index("strip"), 2)
         pair = lax.ppermute(features, "sec", pair_swap)
-        own_c = lax.ppermute(features, "strip", core_swap)
+        own_c = lax.ppermute(
+            lax.dynamic_slice_in_dim(features, 9 * (1 - core), 3, 1), "strip", core_swap
+        )
         rim = lax.dynamic_slice_in_dim(features, 9 * core, 3, 1)
         edge = lax.dynamic_slice_in_dim(features, 3 * core, HALO, 1)
         third = arranged(w_third)

time: 38.9 us -> 38.9 us (level)
  waiting for transfers between devices: 16.1 us -> 15.7 us
    unnamed x16, local copies, waits for them, and re-layouts: 0.69 us -> 1.97 us
    dynamic_slice x1, local copies, waits for them, and re-layouts: 0.99 us -> 0.03 us  [body(): edge = lax.dynamic_slice_in_dim(features, 3 * core, HALO, 1)]
    ppermute x1, waiting for transfers between devices: 8.64 us -> 8.17 us  [body(): pair = lax.ppermute(features, 'sec', pair_swap)]
  transfers between devices with their start and end apart: 7 -> 7, of which waited for: 3 -> 3; matrix products, arithmetic and copies ran while one was open for 5% -> 3% of each run, Pallas kernels for 10% -> 10%
where the time goes in v7:
time: 38.9 us; the launch traced here: 38.6 us
  waiting for transfers between devices  15.7 us (40%)
  starting transfers between devices  11 us (28%)
  Pallas kernels  8.58 us (22%)
  local copies, waits for them, and re-layouts  3.08 us (8%)
    ppermute x1, waiting for transfers between devices, body(): pair = lax.ppermute(features, 'sec', pair_swap)  8.17 us
    pallas_call x1, Pallas kernels, align(): pl.pallas_call(make_kernel(total_rows), out_shape=jax.ShapeDtypeStruct((2...  4.9 us
    ppermute x1, waiting for transfers between devices, body(): far = lax.ppermute(far, 'strip', chip_swap)  3.78 us
    ppermute x1, waiting for transfers between devices, body(): outer_x = lax.ppermute(edge, both, next_chip)  3.73 us
    pallas_call x1, Pallas kernels, pair_part(): pl.pallas_call(pair_kernel, out_shape=(jax.ShapeDtypeStruct((16, LANES, C...  3.68 us
    ppermute x1, starting transfers between devices, body(): lax.ppermute(lax.dynamic_slice_in_dim(pair, 3 * (1 - core), HALO, 1), 'st...  3.22 us
    ppermute x1, starting transfers between devices, body(): outer = lax.ppermute(pair, 'sec', onward)  2.44 us
    ppermute x1, starting transfers between devices, body(): far = lax.ppermute(far, 'strip', chip_swap)  2.05 us
  transfers between devices with their start and end apart: 7, of which 3 were waited for; matrix products, arithmetic and copies ran while one was open for 3% of the time, Pallas kernels for 10%

profile of v7, /device:TPU:122, one launch (start us, length us, event | category | flops | bytes accessed | tf_op | source)
XLA Modules:
  0.0 38.6 jit_solution(234712677496695249)
XLA Ops:
  0.0 1.2 %collective-permute-start = (bf16[1,12,128,128]{3,2,1,0:T(8,128)(2,1)}, bf16[1,12,128,128]{3,2,1,0:T(8,128)(2,1)S(1)}, u32[]{:S(2)}, u32[]{:S(2)}) collective-permute-start(bf16[1,12,128,128]{3,2,1,0:T(8,128)(2,1)} %own.1), channel_id=1, source_target_pairs={{0,32},{32,0},{64,96},{96,64},{128,160},{160,128},{192,224},{224,1... | collective-permute-start | bytes 1179656 | tf_op jit(solution)/shard_map/ppermute | solution.py:243
  1.2 1.0 %constant_dynamic-slice_fusion.4 = (bf16[1,3,128,128]{3,2,1,0:T(8,128)(2,1)S(1)}, bf16[1,3,128,128]{3,2,1,0:T(8,128)(2,1)S(1)}) fusion(bf16[1,12,128,128]{3,2,1,0:T(8,128)(2,1)} %own.1, s32[]{:T(128)S(6)} %select_n.15, s32[]{:T(128)S(6)} %select_n.14), kind=kLoop, calls=%fused_computation.6 | loop fusion | bytes 393224 | tf_op jit(solution)/shard_map/dynamic_slice | solution.py:247
  2.2 0.1 collective-permute-start.1
  2.3 0.0 copy-start.4
  2.4 0.6 %copy-done.4 = bf16[3,3,128,2]{2,3,1,0:T(2,128)(2,1)S(1)} copy-done((bf16[3,3,128,2]{2,3,1,0:T(2,128)(2,1)S(1)}, bf16[3,3,128,2]{2,3,1,0:T(2,128)(2,1)}, u32[]{:S(2)}) %copy-start.4) | copy-done | bytes 4632
  3.1 0.6 %copy-done.7 = s32[8]{0:T(128)S(1)} copy-done((s32[8]{0:T(128)S(1)}, s32[8]{0:T(128)}, u32[]{:S(2)}) %copy-start.7) | copy-done | bytes 56
  3.7 0.6 %copy-done.5 = f32[128]{0:T(128)S(1)} copy-done((f32[128]{0:T(128)S(1)}, f32[128]{0:T(128)}, u32[]{:S(2)}) %copy-start.5) | copy-done | bytes 536
  4.4 0.0 copy-done.6
  4.4 0.0 collective-permute-done.1.own_c
  4.4 8.2 %collective-permute-done.pair = bf16[1,12,128,128]{3,2,1,0:T(8,128)(2,1)S(1)} collective-permute-done((bf16[1,12,128,128]{3,2,1,0:T(8,128)(2,1)}, bf16[1,12,128,128]{3,2,1,0:T(8,128)(2,1)S(1)}, u32[]{:S(2)}, u32[]{:S(2)}) %collective-permute-start) | collective-permute-done | bytes 393248 | tf_op jit(solution)/shard_map/ppermute | solution.py:243
  12.6 0.0 copy-start.3
  12.7 2.1 %collective-permute-start.3 = (bf16[1,12,128,128]{3,2,1,0:T(8,128)(2,1)S(1)}, bf16[1,12,128,128]{3,2,1,0:T(8,128)(2,1)S(1)}, u32[]{:S(2)}, u32[]{:S(2)}) collective-permute-start(bf16[1,12,128,128]{3,2,1,0:T(8,128)(2,1)S(1)} %pad_maximum_fusion), channel_id=1, source_target_pairs={{1,2},{2,1},{3,4},{4,3},{5,6},{6,5},{7,8},{8,7},{9,10},{10,9},{11,... | collective-permute-start | bytes 1179656 | tf_op jit(solution)/shard_map/ppermute | solution.py:257
  14.7 2.4 %collective-permute-start.2 = (bf16[1,12,128,128]{3,2,1,0:T(8,128)(2,1)S(1)}, bf16[1,12,128,128]{3,2,1,0:T(8,128)(2,1)S(1)}, u32[]{:S(2)}, u32[]{:S(2)}) collective-permute-start(bf16[1,12,128,128]{3,2,1,0:T(8,128)(2,1)S(1)} %collective-permute-done.pair), channel_id=1, source_target_pairs={{0,64},{64,128},{96,32},{128,192},{160,96},{224,160},{1,65},{65,12... | collective-permute-start | bytes 1179656 | tf_op jit(solution)/shard_map/ppermute | solution.py:255
  17.2 3.2 %collective-permute-start.4 = (bf16[1,9,128,128]{3,2,1,0:T(8,128)(2,1)S(1)}, bf16[1,9,128,128]{3,2,1,0:T(8,128)(2,1)S(1)}, u32[]{:S(2)}, u32[]{:S(2)}) collective-permute-start(bf16[1,9,128,128]{3,2,1,0:T(8,128)(2,1)S(1)} %get-tuple-element.31), channel_id=1, source_target_pairs={{0,1},{1,0},{2,3},{3,2},{4,5},{5,4},{6,7},{7,6},{8,9},{9,8},{10,11... | collective-permute-start | bytes 884744 | tf_op jit(solution)/shard_map/ppermute | solution.py:259
  20.4 1.9 %collective-permute-start.5 = (bf16[1,9,128,128]{3,2,1,0:T(8,128)(2,1)S(1)}, bf16[1,9,128,128]{3,2,1,0:T(8,128)(2,1)S(1)}, u32[]{:S(2)}, u32[]{:S(2)}) collective-permute-start(bf16[1,9,128,128]{3,2,1,0:T(8,128)(2,1)S(1)} %constant_dynamic-slice_fusion.3), channel_id=1, source_target_pairs={{33,66},{34,65},{35,68},{36,67},{37,70},{38,69},{39,72},{40,71},{4... | collective-permute-start | bytes 884744 | tf_op jit(solution)/shard_map/ppermute | solution.py:258
  22.3 0.0 collective-permute-done.4.pair_c
  22.3 3.8 %collective-permute-done.3.far = bf16[1,12,128,128]{3,2,1,0:T(8,128)(2,1)S(1)} collective-permute-done((bf16[1,12,128,128]{3,2,1,0:T(8,128)(2,1)S(1)}, bf16[1,12,128,128]{3,2,1,0:T(8,128)(2,1)S(1)}, u32[]{:S(2)}, u32[]{:S(2)}) %collective-permute-start.3) | collective-permute-done | bytes 393248 | tf_op jit(solution)/shard_map/ppermute | solution.py:257
  26.1 3.7 %shard_map.82 = (f32[16,128,128]{2,1,0:T(8,128)S(1)}, bf16[18,128,128]{2,1,0:T(8,128)(2,1)S(1)}, bf16[3,3,128,128]{3,2,1,0:T(8,128)(2,1)S(1)}, f32[1,128]{1,0:T(1,128)S(1)}) custom-call(s32[8]{0:T(128)S(1)} %broadcast_clamp_fusion.off_ref, bf16[1,12,128,128]{3,2,1,0:T(8,128)(2,1)S(1)} %copy-done, bf16[1,12,128,128]{3,2,1,0:T(8,128)(2,1)S(1)} %collective-permute-done.3.far, ...), custom_call_target="tpu_custom_call" | custom-call | flops 679477248 | bytes 3276800 | tf_op jit(solution)/shard_map/pallas_call | solution.py:191
  29.8 0.0 collective-permute-done.2.outer
  29.8 0.0 copy-start.1
  29.8 0.0 copy-start.2
  29.9 0.1 collective-permute-start.6
  30.0 3.7 %collective-permute-done.5.outer_x = bf16[1,9,128,128]{3,2,1,0:T(8,128)(2,1)S(1)} collective-permute-done((bf16[1,9,128,128]{3,2,1,0:T(8,128)(2,1)S(1)}, bf16[1,9,128,128]{3,2,1,0:T(8,128)(2,1)S(1)}, u32[]{:S(2)}, u32[]{:S(2)}) %collective-permute-start.5) | collective-permute-done | bytes 294944 | tf_op jit(solution)/shard_map/ppermute | solution.py:258
  33.7 4.9 %shard_map.83 = f32[2,12,1,128]{3,2,1,0:T(1,128)} custom-call(s32[8]{0:T(128)S(1)} %broadcast_clamp_fusion.off_ref, f32[16,128,128]{2,1,0:T(8,128)S(1)} %get-tuple-element.24.part_ref, bf16[18,128,128]{2,1,0:T(8,128)(2,1)S(1)} %get-tuple-element.25.own_buf, bf16[1,12,128,128]{3,2,1,0:T(8,128)(2,1)S(1)} %collective-permute-done.2.outer, ...), custom_call_target="tpu_custom_call" | custom-call | tf_op jit(solution)/shard_map/pallas_call | solution.py:210
  (18 shorter events, 0.2 us)
Async XLA Ops:
  0.0 2.3 %copy-start = (bf16[1,12,128,128]{3,2,1,0:T(8,128)(2,1)S(1)}, bf16[1,12,128,128]{3,2,1,0:T(8,128)(2,1)}, u32[]{:S(2)}) copy-start(bf16[1,12,128,128]{3,2,1,0:T(8,128)(2,1)} %own.1) | copy-start | bytes 1179652
  0.0 12.6 %collective-permute-start = (bf16[1,12,128,128]{3,2,1,0:T(8,128)(2,1)}, bf16[1,12,128,128]{3,2,1,0:T(8,128)(2,1)S(1)}, u32[]{:S(2)}, u32[]{:S(2)}) collective-permute-start(bf16[1,12,128,128]{3,2,1,0:T(8,128)(2,1)} %own.1), channel_id=1, source_target_pairs={{0,32},{32,0},{64,96},{96,64},{128,160},{160,128},{192,224},{224,1... | collective-permute-start | bytes 1179656 | tf_op jit(solution)/shard_map/ppermute | solution.py:243
  2.2 2.2 %collective-permute-start.1 = (bf16[1,3,128,128]{3,2,1,0:T(8,128)(2,1)S(1)}, bf16[1,3,128,128]{3,2,1,0:T(8,128)(2,1)S(1)}, u32[]{:S(2)}, u32[]{:S(2)}) collective-permute-start(bf16[1,3,128,128]{3,2,1,0:T(8,128)(2,1)S(1)} %get-tuple-element.34), channel_id=1, source_target_pairs={{0,1},{1,0},{2,3},{3,2},{4,5},{5,4},{6,7},{7,6},{8,9},{9,8},{10,11... | collective-permute-start | bytes 294920 | tf_op jit(solution)/shard_map/ppermute | solution.py:244
  2.3 0.7 %copy-start.4 = (bf16[3,3,128,2]{2,3,1,0:T(2,128)(2,1)S(1)}, bf16[3,3,128,2]{2,3,1,0:T(2,128)(2,1)}, u32[]{:S(2)}) copy-start(bf16[3,3,128,2]{2,3,1,0:T(2,128)(2,1)} %param.15) | copy-start | bytes 13828
  3.1 0.7 %copy-start.7 = (s32[8]{0:T(128)S(1)}, s32[8]{0:T(128)}, u32[]{:S(2)}) copy-start(s32[8]{0:T(128)} %param.9) | copy-start | bytes 100
  3.7 0.7 %copy-start.5 = (f32[128]{0:T(128)S(1)}, f32[128]{0:T(128)}, u32[]{:S(2)}) copy-start(f32[128]{0:T(128)} %param.14) | copy-start | bytes 1540
  3.7 0.7 %copy-start.6 = (f32[128]{0:T(128)S(1)}, f32[128]{0:T(128)}, u32[]{:S(2)}) copy-start(f32[128]{0:T(128)} %param.12) | copy-start | bytes 1540
  12.6 13.5 %copy-start.3 = (bf16[3,3,162,128]{3,2,1,0:T(8,128)(2,1)S(1)}, bf16[3,3,162,128]{3,2,1,0:T(8,128)(2,1)}, u32[]{:S(2)}) copy-start(bf16[3,3,162,128]{3,2,1,0:T(8,128)(2,1)} %w_ref.1) | copy-start | bytes 1119748
  12.7 13.4 %collective-permute-start.3 = (bf16[1,12,128,128]{3,2,1,0:T(8,128)(2,1)S(1)}, bf16[1,12,128,128]{3,2,1,0:T(8,128)(2,1)S(1)}, u32[]{:S(2)}, u32[]{:S(2)}) collective-permute-start(bf16[1,12,128,128]{3,2,1,0:T(8,128)(2,1)S(1)} %pad_maximum_fusion), channel_id=1, source_target_pairs={{1,2},{2,1},{3,4},{4,3},{5,6},{6,5},{7,8},{8,7},{9,10},{10,9},{11,... | collective-permute-start | bytes 1179656 | tf_op jit(solution)/shard_map/ppermute | solution.py:257
  14.7 15.1 %collective-permute-start.2 = (bf16[1,12,128,128]{3,2,1,0:T(8,128)(2,1)S(1)}, bf16[1,12,128,128]{3,2,1,0:T(8,128)(2,1)S(1)}, u32[]{:S(2)}, u32[]{:S(2)}) collective-permute-start(bf16[1,12,128,128]{3,2,1,0:T(8,128)(2,1)S(1)} %collective-permute-done.pair), channel_id=1, source_target_pairs={{0,64},{64,128},{96,32},{128,192},{160,96},{224,160},{1,65},{65,12... | collective-permute-start | bytes 1179656 | tf_op jit(solution)/shard_map/ppermute | solution.py:255
  17.2 5.1 %collective-permute-start.4 = (bf16[1,9,128,128]{3,2,1,0:T(8,128)(2,1)S(1)}, bf16[1,9,128,128]{3,2,1,0:T(8,128)(2,1)S(1)}, u32[]{:S(2)}, u32[]{:S(2)}) collective-permute-start(bf16[1,9,128,128]{3,2,1,0:T(8,128)(2,1)S(1)} %get-tuple-element.31), channel_id=1, source_target_pairs={{0,1},{1,0},{2,3},{3,2},{4,5},{5,4},{6,7},{7,6},{8,9},{9,8},{10,11... | collective-permute-start | bytes 884744 | tf_op jit(solution)/shard_map/ppermute | solution.py:259
  20.4 13.3 %collective-permute-start.5 = (bf16[1,9,128,128]{3,2,1,0:T(8,128)(2,1)S(1)}, bf16[1,9,128,128]{3,2,1,0:T(8,128)(2,1)S(1)}, u32[]{:S(2)}, u32[]{:S(2)}) collective-permute-start(bf16[1,9,128,128]{3,2,1,0:T(8,128)(2,1)S(1)} %constant_dynamic-slice_fusion.3), channel_id=1, source_target_pairs={{33,66},{34,65},{35,68},{36,67},{37,70},{38,69},{39,72},{40,71},{4... | collective-permute-start | bytes 884744 | tf_op jit(solution)/shard_map/ppermute | solution.py:258
  29.8 3.9 %copy-start.1 = (bf16[3,3,128,128]{3,2,1,0:T(8,128)(2,1)S(1)}, bf16[3,3,128,128]{3,2,1,0:T(8,128)(2,1)}, u32[]{:S(2)}) copy-start(bf16[3,3,128,128]{3,2,1,0:T(8,128)(2,1)} %w2_ref.1) | copy-start | bytes 884740
  29.8 3.9 %copy-start.2 = (f32[2,1,12,128]{3,1,2,0:T(1,128)S(1)}, f32[2,1,12,128]{3,1,2,0:T(1,128)}, u32[]{:S(2)}) copy-start(f32[2,1,12,128]{3,1,2,0:T(1,128)} %param.10) | copy-start | bytes 36868
  29.9 3.8 %collective-permute-start.6 = (bf16[1,9,128,128]{3,2,1,0:T(8,128)(2,1)S(1)}, bf16[1,9,128,128]{3,2,1,0:T(8,128)(2,1)S(1)}, u32[]{:S(2)}, u32[]{:S(2)}) collective-permute-start(bf16[1,9,128,128]{3,2,1,0:T(8,128)(2,1)S(1)} %constant_dynamic-slice_fusion), channel_id=1, source_target_pairs={{0,1},{1,0},{2,3},{3,2},{4,5},{5,4},{6,7},{7,6},{8,9},{9,8},{10,11... | collective-permute-start | bytes 884744 | tf_op jit(solution)/shard_map/ppermute | solution.py:267
